TPU v7x, 32 devices: a whole 2x2x4 slice. The times are simulated.
32 devices in a mesh: row: 8 (over y, x, core), col: 4 (over z).
Axes of the slice: x: 2, y: 2, z: 4, core: 2. Of those that a mesh axis runs over, the one named last changes fastest.
Arguments:
- p_cov: bfloat16 [4096, 4096], P('row', 'col'), may hold values from -6 to 6, as said below
- f_blocks: bfloat16 [32, 7, 128, 128], P('row'), may hold values from -0.1875 to 0.1875
- stencil_cols: int32 [32, 7], replicated, may hold values from 0 to 31, as said below
- localization_weights: bfloat16 [4096, 4096], P('row', 'col'), may hold values from 0.25 to 1, as said below
- block_mask: int32 [32, 32], P('row', 'col'), may hold values from 0 to 1, as said below
- disturbance_variances: float32 [4096], P('row'), may hold values from 0.5 to 2
Outputs:
- predicted_spread_matrix: float32 [4096, 4096], P('row', 'col')
Inputs may be any that keep to these rules, and one draw needn't show every extreme that they name: `stencil_cols`: block row i lists i, i - 1, i + 1, one block 2 to 3 above and one below, and i - 4 and i + 4, each clamped to 0 .. 31. Symmetric: p_cov equals its transpose. `localization_weights`: Symmetric: taper equals its transpose. Symmetric: block_mask equals its transpose.
All inputs are finite; a program needn't handle non-finite values.
Results may differ from a plain program's by a relative error of at most 0.0029.
Values may be sent and summed in bfloat16 or wider, within the bound.
No kernel may reach another device: no remote copies, remote signals or barrier semaphores. Data moves between devices by JAX's collectives and lax.ppermute only.
A program may use at most 64 MiB of HBM per device.

v0:
```python
import jax
import jax.numpy as jnp
from jax import lax
from jax.sharding import PartitionSpec as P

STENCIL = 7
BAND = 4


def extended_2(array, sides, width):
    for axis, dim in sides:
        devices, length = (lax.axis_size(axis), array.shape[dim])
        up = [(i, (i + 1) % devices) for i in range(devices - 1)]
        down = [(j, i) for i, j in up]
        last = lax.slice_in_dim(array, length - width, length, axis=dim)
        first = lax.slice_in_dim(array, 0, width, axis=dim)
        before = lax.ppermute(last, axis, up)
        after = lax.ppermute(first, axis, down)
        array = jnp.concatenate([before, array, after], axis=dim)
    return array


def broadcast(block, axis, holder):
    block = jnp.where(lax.axis_index(axis) == holder, block, jnp.zeros_like(block))
    return lax.psum(block, axis)


def on_device(
    p_cov, f_blocks, stencil_cols, localization_weights, block_mask, disturbance_variances
):
    row_count = lax.axis_size("row")
    col_count = lax.axis_size("col")
    fan_ratio = row_count // col_count
    row_idx = lax.axis_index("row")
    col_idx = lax.axis_index("col")
    block_rows = f_blocks.shape[0]
    block_size = f_blocks.shape[2]
    tile_horizontal_extent = p_cov.shape[1]
    slab = tile_horizontal_extent // block_size
    tile_vertical_extent = block_rows * block_size
    extended = extended_2(p_cov, (("row", 0),), BAND * block_size)
    ext_blocks = extended.reshape(block_rows + 2 * BAND, block_size, tile_horizontal_extent)
    own_cols = lax.dynamic_slice_in_dim(stencil_cols, row_idx * block_rows, block_rows, 0)
    local_rows = own_cols - (row_idx * block_rows - BAND)
    accum = jnp.zeros((block_rows, block_size, tile_horizontal_extent), jnp.float32)
    for entry in range(STENCIL):
        picked = jnp.take(ext_blocks, local_rows[:, entry], axis=0)
        accum = accum + jnp.einsum(
            "iab,ibn->ian", f_blocks[:, entry], picked, preferred_element_type=jnp.float32
        )
    inter = accum.reshape(tile_vertical_extent, tile_horizontal_extent).astype(jnp.bfloat16)
    fetched = []
    for block_offset in range(fan_ratio):
        root = col_idx * fan_ratio + block_offset
        fetched.append(broadcast(f_blocks, "row", root))
    f_need = jnp.concatenate(fetched, axis=0)
    inter_ext = extended_2(inter, (("col", 1),), BAND * block_size)
    ext_cols = inter_ext.reshape(tile_vertical_extent, slab + 2 * BAND, block_size)
    need_cols = lax.dynamic_slice_in_dim(stencil_cols, col_idx * slab, slab, 0)
    source = need_cols - (col_idx * slab - BAND)
    spread = jnp.zeros((tile_vertical_extent, slab, block_size), jnp.float32)
    for entry in range(STENCIL):
        picked = jnp.take(ext_cols, source[:, entry], axis=1)
        spread = spread + jnp.einsum(
            "rjb,jab->rja", picked, f_need[:, entry], preferred_element_type=jnp.float32
        )
    filtered_tile_entries = (
        spread.reshape(block_rows, block_size, slab, block_size)
        * block_mask.astype(jnp.float32)[:, None, :, None]
    )
    predicted_spread_matrix = localization_weights.astype(
        jnp.float32
    ) * filtered_tile_entries.reshape(tile_vertical_extent, tile_horizontal_extent)
    glob_rows = row_idx * tile_vertical_extent + jnp.arange(tile_vertical_extent, dtype=jnp.int32)
    glob_cols = col_idx * tile_horizontal_extent + jnp.arange(
        tile_horizontal_extent, dtype=jnp.int32
    )
    is_main_tile = glob_rows[:, None] == glob_cols[None, :]
    return predicted_spread_matrix + jnp.where(is_main_tile, disturbance_variances[:, None], 0.0)


def solution(mesh):
    placed = (
        P("row", "col"),
        P("row", None, None, None),
        P(),
        P("row", "col"),
        P("row", "col"),
        P("row"),
    )
    return jax.shard_map(
        on_device, mesh=mesh, in_specs=placed, out_specs=P("row", "col"), check_vma=False
    )
```

profile of v0, /device:TPU:0, one launch (start us, length us, event | category | flops | bytes accessed | tf_op | source)
XLA Modules:
  0.0 126.0 jit_solution(6801844438422916949)
XLA Ops:
  6.5 2.5 %collective-permute-start = (bf16[512,1024]{1,0:T(8,128)(2,1)}, bf16[512,1024]{1,0:T(8,128)(2,1)S(1)}, u32[]{:S(2)}, u32[]{:S(2)}) collective-permute-start(bf16[512,1024]{1,0:T(8,128)(2,1)} %param.10), channel_id=1, source_target_pairs={{0,4},{4,8},{8,12},{12,16},{16,20},{20,24},{24,28},{1,5},{5,9},{9,... | collective-permute-start | bytes 3145736 | tf_op jit(solution)/shard_map/ppermute | solution.py:17
  10.3 3.0 %broadcast_select_fusion = (bf16[4,7,128,128]{3,2,0,1:T(8,128)(2,1)}, bf16[4,7,128,128]{3,2,0,1:T(8,128)(2,1)}, bf16[4,7,128,128]{3,2,0,1:T(8,128)(2,1)}) fusion(pred[]{:T(512)S(6)} %eq.20, bf16[4,7,128,128]{3,2,1,0:T(8,128)(2,1)} %param.11, pred[]{:T(512)S(6)} %eq.19), kind=kLoop, calls=%fused_computation.68 | loop fusion | flops 917504 | bytes 3670018 | tf_op jit(solution)/shard_map/jit(_where)/select_n | solution.py:24
  15.9 2.1 %pad_maximum_fusion = bf16[1536,1024]{1,0:T(8,128)(2,1)S(1)} fusion(bf16[512,1024]{1,0:T(8,128)(2,1)} %collective-permute-done.1, bf16[512,1024]{1,0:T(8,128)(2,1)} %param.10, bf16[512,1024]{1,0:T(8,128)(2,1)} %copy-done.14), kind=kLoop, calls=%fused_computation.14 | loop fusion | flops 9437184 | bytes 6291456 | tf_op jit(solution)/shard_map/concatenate | solution.py:19
  18.0 1.6 %gather_fusion.4 = bf16[4,128,1024]{2,1,0:T(8,128)(2,1)} fusion(bf16[12,128,1024]{2,1,0:T(8,128)(2,1)S(1)} %bitcast.121, s32[1024]{0:T(1024)S(1)} %get-tuple-element.68), kind=kCustom, calls=%fused_computation.5.clone | custom fusion | bytes 2097168 | tf_op jit(solution)/shard_map/jit(_take)/gather | solution.py:47
  19.7 1.6 %gather_fusion.3 = bf16[4,128,1024]{2,1,0:T(8,128)(2,1)} fusion(bf16[12,128,1024]{2,1,0:T(8,128)(2,1)S(1)} %bitcast.122, s32[1024]{0:T(1024)S(1)} %get-tuple-element.69), kind=kCustom, calls=%fused_computation.4.clone | custom fusion | bytes 2097168 | tf_op jit(solution)/shard_map/jit(_take)/gather | solution.py:47
  21.3 1.6 %gather_fusion.2 = bf16[4,128,1024]{2,1,0:T(8,128)(2,1)} fusion(bf16[12,128,1024]{2,1,0:T(8,128)(2,1)S(1)} %bitcast.123, s32[1024]{0:T(1024)S(1)} %get-tuple-element.70), kind=kCustom, calls=%fused_computation.3.clone | custom fusion | bytes 2097168 | tf_op jit(solution)/shard_map/jit(_take)/gather | solution.py:47
  22.9 1.6 %gather_fusion.1 = bf16[4,128,1024]{2,1,0:T(8,128)(2,1)} fusion(bf16[12,128,1024]{2,1,0:T(8,128)(2,1)S(1)} %bitcast.124, s32[1024]{0:T(1024)S(1)} %get-tuple-element.71), kind=kCustom, calls=%fused_computation.2.clone | custom fusion | bytes 2097168 | tf_op jit(solution)/shard_map/jit(_take)/gather | solution.py:47
  24.5 1.6 %gather_fusion.5 = bf16[4,128,1024]{2,1,0:T(8,128)(2,1)} fusion(bf16[12,128,1024]{2,1,0:T(8,128)(2,1)S(1)} %bitcast.125, s32[1024]{0:T(1024)S(1)} %get-tuple-element.67), kind=kCustom, calls=%fused_computation.6.clone | custom fusion | bytes 2097168 | tf_op jit(solution)/shard_map/jit(_take)/gather | solution.py:47
  27.6 1.6 %gather_fusion.6 = bf16[4,128,1024]{2,1,0:T(8,128)(2,1)} fusion(bf16[12,128,1024]{2,1,0:T(8,128)(2,1)S(1)} %bitcast.127, s32[1024]{0:T(1024)S(1)} %get-tuple-element.66), kind=kCustom, calls=%fused_computation.7.clone | custom fusion | bytes 2097168 | tf_op jit(solution)/shard_map/jit(_take)/gather | solution.py:47
  29.2 1.9 %fusion.25 = f32[4,1024,128]{1,2,0:T(8,128)S(1)} fusion(bf16[4,128,1024]{2,1,0:T(8,128)(2,1)} %gather_fusion.4, pred[4]{0:T(512)(128)(4,1)S(1)} %get-tuple-element.56, bf16[4,7,128,128]{3,2,0,1:T(8,128)(2,1)} %get-tuple-element.41), kind=kOutput, calls=%fused_computation.44 | convolution fusion | flops 134742016 | bytes 3276804 | tf_op jit(solution)/shard_map/iab,ibn->ian/dot_general | solution.py:48
  37.4 3.5 %collective-permute-start.2 = (bf16[512,512]{0,1:T(8,128)(2,1)S(1)}, bf16[512,512]{0,1:T(8,128)(2,1)S(1)}, u32[]{:S(2)}, u32[]{:S(2)}) collective-permute-start(bf16[512,512]{0,1:T(8,128)(2,1)S(1)} %get-tuple-element.37), channel_id=1, source_target_pairs={{0,1},{1,2},{2,3},{4,5},{5,6},{6,7},{8,9},{9,10},{10,11},{12,13},{... | collective-permute-start | bytes 1572872 | tf_op jit(solution)/shard_map/ppermute | solution.py:17
  42.3 41.3 %all-reduce.3.cloned.1.call-done = (bf16[4,7,128,128]{3,2,0,1:T(8,128)(2,1)}, bf16[4,7,128,128]{3,2,0,1:T(8,128)(2,1)}) async-done(((bf16[4,7,128,128]{3,2,0,1:T(8,128)(2,1)}, bf16[4,7,128,128]{3,2,0,1:T(8,128)(2,1)}), (bf16[4,7,128,128]{3,2,0,1:T(8,128)(2,1)}, bf16[4,7,128,128]{3,2,0,1:T(8,128)(2,1)})) %all-reduce.3.cloned.1.call-update) | async-done | bytes 1835024 | tf_op jit(solution)/shard_map/psum | solution.py:25
  83.6 2.5 %constant_dynamic-update-slice_fusion.1 = bf16[8,7,128,128]{3,2,0,1:T(8,128)(2,1)} fusion(bf16[4,7,128,128]{3,2,0,1:T(8,128)(2,1)} %get-tuple-element.6), kind=kLoop, calls=%fused_computation.113 | loop fusion | bytes 1835008
  88.7 3.0 %copy.39 = bf16[512,16,128]{2,0,1:T(8,128)(2,1)S(1)} copy(bf16[512,16,128]{0,2,1:T(8,128)(2,1)} %bitcast.129) | data formatting | bytes 4194304 | tf_op jit(solution)/shard_map/reshape | solution.py:58
  91.7 1.7 %gather_fusion.8 = bf16[8,512,128]{2,1,0:T(8,128)(2,1)} fusion(bf16[512,16,128]{2,0,1:T(8,128)(2,1)S(1)} %copy.39, s32[1024]{0:T(1024)S(1)} %get-tuple-element.77), kind=kCustom, calls=%fused_computation.8.clone | custom fusion | bytes 2097184 | tf_op jit(solution)/shard_map/jit(_take)/gather | solution.py:63
  93.4 1.7 %gather_fusion.7 = bf16[8,512,128]{2,1,0:T(8,128)(2,1)} fusion(bf16[512,16,128]{2,0,1:T(8,128)(2,1)S(1)} %copy.39, s32[1024]{0:T(1024)S(1)} %pad_clamp_fusion.6), kind=kCustom, calls=%fused_computation.1.clone | custom fusion | bytes 2097184 | tf_op jit(solution)/shard_map/jit(_take)/gather | solution.py:63
  95.0 1.6 %gather_fusion.9 = bf16[8,512,128]{2,1,0:T(8,128)(2,1)} fusion(bf16[512,16,128]{2,0,1:T(8,128)(2,1)S(1)} %copy.39, s32[1024]{0:T(1024)S(1)} %get-tuple-element.76), kind=kCustom, calls=%fused_computation.9.clone | custom fusion | bytes 2097184 | tf_op jit(solution)/shard_map/jit(_take)/gather | solution.py:63
  96.7 1.7 %gather_fusion.10 = bf16[8,512,128]{2,1,0:T(8,128)(2,1)} fusion(bf16[512,16,128]{2,0,1:T(8,128)(2,1)S(1)} %copy.39, s32[1024]{0:T(1024)S(1)} %get-tuple-element.75), kind=kCustom, calls=%fused_computation.10.clone | custom fusion | bytes 2097184 | tf_op jit(solution)/shard_map/jit(_take)/gather | solution.py:63
  98.4 1.6 %gather_fusion.11 = bf16[8,512,128]{2,1,0:T(8,128)(2,1)} fusion(bf16[512,16,128]{2,0,1:T(8,128)(2,1)S(1)} %copy.39, s32[1024]{0:T(1024)S(1)} %get-tuple-element.74), kind=kCustom, calls=%fused_computation.11.clone | custom fusion | bytes 2097184 | tf_op jit(solution)/shard_map/jit(_take)/gather | solution.py:63
  100.0 1.6 %gather_fusion.12 = bf16[8,512,128]{2,1,0:T(8,128)(2,1)} fusion(bf16[512,16,128]{2,0,1:T(8,128)(2,1)S(1)} %copy.39, s32[1024]{0:T(1024)S(1)} %get-tuple-element.73), kind=kCustom, calls=%fused_computation.12.clone | custom fusion | bytes 2097184 | tf_op jit(solution)/shard_map/jit(_take)/gather | solution.py:63
  102.4 1.9 %fusion.11 = f32[8,128,512]{2,1,0:T(8,128)S(1)} fusion(bf16[8,512,128]{2,1,0:T(8,128)(2,1)} %gather_fusion.8, pred[8]{0:T(512)(128)(4,1)S(1)} %get-tuple-element.50, bf16[8,7,128,128]{3,2,0,1:T(8,128)(2,1)} %constant_dynamic-update-slice_fusion), kind=kOutput, calls=%fused_computation.30 | convolution fusion | flops 134742016 | bytes 3407880 | tf_op jit(solution)/shard_map/rjb,jab->rja/dot_general | solution.py:64
  112.1 1.8 %add_add_fusion = f32[8,128,512]{2,1,0:T(8,128)S(1)} fusion(f32[8,128,512]{2,1,0:T(8,128)S(1)} %fusion.3, f32[8,128,512]{2,1,0:T(8,128)S(1)} %fusion.5, f32[8,128,512]{2,1,0:T(8,128)S(1)} %fusion.7, f32[8,128,512]{2,1,0:T(8,128)S(1)} %fusion.9, f32[8,128,512]{2,1,0:T(8,128)S(1)} %fusion.13, f32[8,128,512]{2,1,0:T(8,128)S(1)} %fusion.11, ...), kind=kOutput, calls=%fused_computation.20 | convolution fusion | flops 137887744 | bytes 15990792 | tf_op jit(solution)/shard_map/rjb,jab->rja/dot_general | solution.py:64
  113.8 1.8 %copy.46 = f32[512,1024]{1,0:T(8,128)} copy(f32[512,1024]{0,1:T(8,128)S(1)} %bitcast.128) | data formatting | bytes 4194304 | tf_op jit(solution)/shard_map/reshape | solution.py:68
  117.2 1.9 %fusion.1 = f32[512,1024]{1,0:T(8,128)} fusion(f32[512,1024]{1,0:T(8,128)S(1)} %copy-done, f32[64,8,8,128]{3,2,1,0:T(8,128)S(1)} %bitcast.130, bf16[512,1024]{1,0:T(8,128)(2,1)S(1)} %copy-done.13, f32[512]{0:T(512)S(1)} %copy-done.17, s32[1024]{0:T(1024)S(1)} %iota_add_fusion, s32[512]{0:T(512)S(1)} %iota_add_fusion.1), kind=kLoop, calls=%fused_computation.17 | loop fusion | flops 3145728 | bytes 7348224 | tf_op jit(solution)/shard_map/add | solution.py:79
  (79 shorter events, 25.4 us)
Async XLA Ops:
  6.5 77.1 %all-reduce.3.cloned.1.call-start = ((), (), s32[]{:S(2)}) async-start(), calls=%async_computation | async-start | bytes 3670016 | tf_op jit(solution)/shard_map/psum | solution.py:25
  6.5 7.1 %collective-permute-start = (bf16[512,1024]{1,0:T(8,128)(2,1)}, bf16[512,1024]{1,0:T(8,128)(2,1)S(1)}, u32[]{:S(2)}, u32[]{:S(2)}) collective-permute-start(bf16[512,1024]{1,0:T(8,128)(2,1)} %param.10), channel_id=1, source_target_pairs={{0,4},{4,8},{8,12},{12,16},{16,20},{20,24},{24,28},{1,5},{5,9},{9,... | collective-permute-start | bytes 3145736 | tf_op jit(solution)/shard_map/ppermute | solution.py:17
  9.0 6.9 %collective-permute-start.1 = (bf16[512,1024]{1,0:T(8,128)(2,1)}, bf16[512,1024]{1,0:T(8,128)(2,1)}, u32[]{:S(2)}, u32[]{:S(2)}) collective-permute-start(bf16[512,1024]{1,0:T(8,128)(2,1)} %param.10), channel_id=1, source_target_pairs={{4,0},{8,4},{12,8},{16,12},{20,16},{24,20},{28,24},{5,1},{9,5},{13... | collective-permute-start | bytes 3145736 | tf_op jit(solution)/shard_map/ppermute | solution.py:18
  10.3 3.0 %copy-start.16 = (s32[32,7]{0,1:T(8,128)S(1)}, s32[32,7]{0,1:T(8,128)}, u32[]{:S(2)}) copy-start(s32[32,7]{0,1:T(8,128)} %param.12) | copy-start | bytes 2692
  13.6 1.0 copy-start.14
  29.2 1.9 %copy-start.9 = (bf16[4,128,1024]{2,1,0:T(8,128)(2,1)S(1)}, bf16[4,128,1024]{2,1,0:T(8,128)(2,1)}, u32[]{:S(2)}) copy-start(bf16[4,128,1024]{2,1,0:T(8,128)(2,1)} %gather_fusion.3) | copy-start | bytes 3145732
  29.2 2.0 %copy-start.12 = (bf16[4,7,128,128]{3,2,0,1:T(8,128)(2,1)S(1)}, bf16[4,7,128,128]{3,2,0,1:T(8,128)(2,1)}, u32[]{:S(2)}) copy-start(bf16[4,7,128,128]{3,2,0,1:T(8,128)(2,1)} %get-tuple-element.41) | copy-start | bytes 2752516
  31.1 1.2 copy-start.5
  31.7 1.3 %copy-start.6 = (bf16[4,128,1024]{2,1,0:T(8,128)(2,1)S(1)}, bf16[4,128,1024]{2,1,0:T(8,128)(2,1)}, u32[]{:S(2)}) copy-start(bf16[4,128,1024]{2,1,0:T(8,128)(2,1)} %gather_fusion.1) | copy-start | bytes 3145732
  32.9 1.3 copy-start.3
  33.5 1.3 %copy-start.2 = (bf16[4,128,1024]{2,1,0:T(8,128)(2,1)S(1)}, bf16[4,128,1024]{2,1,0:T(8,128)(2,1)}, u32[]{:S(2)}) copy-start(bf16[4,128,1024]{2,1,0:T(8,128)(2,1)} %gather_fusion) | copy-start | bytes 3145732
  34.7 1.3 %copy-start.1 = (bf16[4,128,1024]{2,1,0:T(8,128)(2,1)S(1)}, bf16[4,128,1024]{2,1,0:T(8,128)(2,1)}, u32[]{:S(2)}) copy-start(bf16[4,128,1024]{2,1,0:T(8,128)(2,1)} %gather_fusion.6) | copy-start | bytes 3145732
  36.8 5.5 %copy-start.18 = (s32[4,8]{1,0:T(4,128)S(1)}, s32[4,8]{1,0:T(4,128)}, u32[]{:S(2)}) copy-start(s32[4,8]{1,0:T(4,128)} %param.14) | copy-start | bytes 388
  37.4 49.8 %collective-permute-start.2 = (bf16[512,512]{0,1:T(8,128)(2,1)S(1)}, bf16[512,512]{0,1:T(8,128)(2,1)S(1)}, u32[]{:S(2)}, u32[]{:S(2)}) collective-permute-start(bf16[512,512]{0,1:T(8,128)(2,1)S(1)} %get-tuple-element.37), channel_id=1, source_target_pairs={{0,1},{1,2},{2,3},{4,5},{5,6},{6,7},{8,9},{9,10},{10,11},{12,13},{... | collective-permute-start | bytes 1572872 | tf_op jit(solution)/shard_map/ppermute | solution.py:17
  41.0 46.2 %collective-permute-start.3 = (bf16[512,512]{0,1:T(8,128)(2,1)S(1)}, bf16[512,512]{0,1:T(8,128)(2,1)S(1)}, u32[]{:S(2)}, u32[]{:S(2)}) collective-permute-start(bf16[512,512]{0,1:T(8,128)(2,1)S(1)} %get-tuple-element.38), channel_id=1, source_target_pairs={{1,0},{2,1},{3,2},{5,4},{6,5},{7,6},{9,8},{10,9},{11,10},{13,12},{... | collective-permute-start | bytes 1572872 | tf_op jit(solution)/shard_map/ppermute | solution.py:18
  83.6 2.5 %copy-start.15 = (bf16[4,7,128,128]{3,2,0,1:T(8,128)(2,1)S(1)}, bf16[4,7,128,128]{3,2,0,1:T(8,128)(2,1)}, u32[]{:S(2)}) copy-start(bf16[4,7,128,128]{3,2,0,1:T(8,128)(2,1)} %get-tuple-element.8) | copy-start | bytes 2752516
  102.4 1.9 %copy-start.10 = (bf16[8,512,128]{2,1,0:T(8,128)(2,1)S(1)}, bf16[8,512,128]{2,1,0:T(8,128)(2,1)}, u32[]{:S(2)}) copy-start(bf16[8,512,128]{2,1,0:T(8,128)(2,1)} %gather_fusion.7) | copy-start | bytes 3145732
  104.3 1.6 %copy-start.11 = (bf16[8,512,128]{2,1,0:T(8,128)(2,1)S(1)}, bf16[8,512,128]{2,1,0:T(8,128)(2,1)}, u32[]{:S(2)}) copy-start(bf16[8,512,128]{2,1,0:T(8,128)(2,1)} %gather_fusion.9) | copy-start | bytes 3145732
  105.9 1.6 %copy-start.7 = (bf16[8,512,128]{2,1,0:T(8,128)(2,1)S(1)}, bf16[8,512,128]{2,1,0:T(8,128)(2,1)}, u32[]{:S(2)}) copy-start(bf16[8,512,128]{2,1,0:T(8,128)(2,1)} %gather_fusion.10) | copy-start | bytes 3145732
  107.5 1.6 %copy-start.8 = (bf16[8,512,128]{2,1,0:T(8,128)(2,1)S(1)}, bf16[8,512,128]{2,1,0:T(8,128)(2,1)}, u32[]{:S(2)}) copy-start(bf16[8,512,128]{2,1,0:T(8,128)(2,1)} %gather_fusion.11) | copy-start | bytes 3145732
  109.0 1.6 %copy-start.4 = (bf16[8,512,128]{2,1,0:T(8,128)(2,1)S(1)}, bf16[8,512,128]{2,1,0:T(8,128)(2,1)}, u32[]{:S(2)}) copy-start(bf16[8,512,128]{2,1,0:T(8,128)(2,1)} %gather_fusion.12) | copy-start | bytes 3145732
  113.8 2.0 %copy-start.13 = (bf16[512,1024]{1,0:T(8,128)(2,1)S(1)}, bf16[512,1024]{1,0:T(8,128)(2,1)}, u32[]{:S(2)}) copy-start(bf16[512,1024]{1,0:T(8,128)(2,1)} %param.13) | copy-start | bytes 3145732
  115.7 1.6 %copy-start = (f32[512,1024]{1,0:T(8,128)S(1)}, f32[512,1024]{1,0:T(8,128)}, u32[]{:S(2)}) copy-start(f32[512,1024]{1,0:T(8,128)} %copy.46) | copy-start | bytes 6291460
  115.7 1.6 %copy-start.17 = (f32[512]{0:T(512)S(1)}, f32[512]{0:T(512)}, u32[]{:S(2)}) copy-start(f32[512]{0:T(512)} %param.15) | copy-start | bytes 6148
Sparse Core Ops, SparseCore 0:
  13.4 70.1 all-reduce.2
where the time goes:
time: 127 us; the launch traced here: 126 us
  waiting for transfers between devices  42.6 us (34%)
  local copies, waits for them, and re-layouts  35.7 us (28%)
  matrix products  16.6 us (13%)
  between operations  13.9 us (11%)
  other arithmetic  8.67 us (7%)
  starting transfers between devices  8.55 us (7%)
    psum x1, waiting for transfers between devices, broadcast(): return lax.psum(block, axis)  41.3 us
    dot_general x7, matrix products, on_device(): jnp.einsum('rjb,jab->rja', picked, f_need[:, entry], preferred_element_ty...  11.3 us
    gather x7, local copies, waits for them, and re-layouts, on_device(): picked = jnp.take(ext_blocks, local_rows[:, entry], axis=0)  11.2 us
    gather x7, local copies, waits for them, and re-layouts, on_device(): picked = jnp.take(ext_cols, source[:, entry], axis=1)  10.7 us
    unnamed x39, local copies, waits for them, and re-layouts  7.09 us
    ppermute x2, starting transfers between devices, extended_2(): before = lax.ppermute(last, axis, up)  5.97 us
    dot_general x7, matrix products, on_device(): jnp.einsum('iab,ibn->ian', f_blocks[:, entry], picked, preferred_element_...  5.27 us
    concatenate x2, other arithmetic, extended_2(): array = jnp.concatenate([before, array, after], axis=dim)  3.54 us
  transfers between devices with their start and end apart: 5, of which 2 were waited for; matrix products, arithmetic and copies ran while one was open for 21% of the time, Pallas kernels for 0%

commit v1 on v0

v1 whole, which is shorter than its diff:
```python
import functools

import jax
import jax.numpy as jnp
from jax import lax
from jax.experimental import pallas as pl
from jax.experimental.pallas import tpu as pltpu
from jax.sharding import PartitionSpec as P

STENCIL = 7
BAND = 4
ANY = pl.ANY


def up_down(devices):
    up = [(i, i + 1) for i in range(devices - 1)]
    return up, [(j, i) for i, j in up]


def source_plane(c, a, cols):
    if cols & (cols - 1):
        return a
    return c ^ (((a ^ c) - 1) % cols)


def group_pairs(rows, cols):
    fan = rows // cols
    pairs = []
    for t in range(rows):
        a, k = divmod(t, fan)
        for c in range(cols):
            if a != c:
                pairs.append(((c * fan + k) * cols + source_plane(c, a, cols), t * cols + c))
    return pairs


def stage1_kernel(cols_ref, f_ref, before_hbm, own_hbm, after_hbm, out_ref, ext, sem):
    rows = f_ref.shape[0]
    bs = f_ref.shape[2]
    n = out_ref.shape[1]
    first = lax.axis_index("row") * rows
    halo = before_hbm.shape[0]
    tall = own_hbm.shape[0]
    copies = [
        pltpu.make_async_copy(own_hbm, ext.at[pl.ds(halo, tall)], sem.at[0]),
        pltpu.make_async_copy(before_hbm, ext.at[pl.ds(0, halo)], sem.at[1]),
        pltpu.make_async_copy(after_hbm, ext.at[pl.ds(halo + tall, halo)], sem.at[2]),
    ]
    for copy in copies:
        copy.start()
    for copy in copies:
        copy.wait()
    tile = min(256, n)
    for i in range(rows):
        lhs = jnp.concatenate([f_ref[i, e] for e in range(STENCIL)], axis=1)
        starts = [
            pl.multiple_of((cols_ref[first + i, e] - first + BAND) * bs, bs)
            for e in range(STENCIL)
        ]
        for t in range(n // tile):
            rhs = jnp.concatenate(
                [ext[pl.ds(s, bs), t * tile : (t + 1) * tile] for s in starts], axis=0
            )
            out_ref[i * bs : (i + 1) * bs, t * tile : (t + 1) * tile] = jnp.dot(
                lhs, rhs, preferred_element_type=jnp.float32
            ).astype(out_ref.dtype)


def stage2_kernel(
    fan, cols_ref, mask_ref, q_ref, w_ref, left_hbm, own_hbm, right_hbm, mine_hbm, others_hbm,
    out_ref, ext, f_all, sem,
):
    j = pl.program_id(0)
    slab = pl.num_programs(0)
    bs = out_ref.shape[1]
    rows = out_ref.shape[0] // bs
    group = f_all.shape[0] // fan
    row_idx, col_idx = lax.axis_index("row"), lax.axis_index("col")
    halo, wide = left_hbm.shape[1], own_hbm.shape[1]

    @pl.when(j == 0)
    def _():
        k = lax.rem(row_idx, fan)
        copies = [
            pltpu.make_async_copy(own_hbm, ext.at[:, pl.ds(halo, wide)], sem.at[0]),
            pltpu.make_async_copy(left_hbm, ext.at[:, pl.ds(0, halo)], sem.at[1]),
            pltpu.make_async_copy(right_hbm, ext.at[:, pl.ds(halo + wide, halo)], sem.at[2]),
            pltpu.make_async_copy(mine_hbm, f_all.at[pl.ds(k * group, group)], sem.at[3]),
        ]
        for step in range(1, fan):
            at = lax.rem(k + step, fan) * group
            copies.append(
                pltpu.make_async_copy(
                    others_hbm.at[step - 1], f_all.at[pl.ds(at, group)], sem.at[3 + step]
                )
            )
        for copy in copies:
            copy.start()
        for copy in copies:
            copy.wait()

    col = col_idx * slab + j
    first = col_idx * slab - BAND
    lhs = jnp.concatenate(
        [
            ext[:, pl.ds(pl.multiple_of((cols_ref[col, e] - first) * bs, bs), bs)]
            for e in range(STENCIL)
        ],
        axis=1,
    )
    rhs = jnp.concatenate([f_all[j, e] for e in range(STENCIL)], axis=1)
    spread = lax.dot_general(
        lhs, rhs, (((1,), (1,)), ((), ())), preferred_element_type=jnp.float32
    )
    eye = lax.broadcasted_iota(jnp.int32, (bs, bs), 0) == lax.broadcasted_iota(
        jnp.int32, (bs, bs), 1
    )
    for i in range(rows):
        at = slice(i * bs, (i + 1) * bs)
        keep = mask_ref[i, j].astype(jnp.float32)
        on_main = (row_idx * rows + i == col).astype(jnp.float32)
        noise = jnp.where(eye, q_ref[i : i + 1, :] * on_main, 0.0)
        out_ref[at, :] = w_ref[at, :].astype(jnp.float32) * (spread[at] * keep) + noise


def on_device(
    p_cov, f_blocks, stencil_cols, localization_weights, block_mask, disturbance_variances
):
    rows, cols = lax.axis_size("row"), lax.axis_size("col")
    fan = rows // cols
    block_rows, bs = f_blocks.shape[0], f_blocks.shape[2]
    tall, wide = p_cov.shape
    slab = wide // bs
    halo = BAND * bs

    up, down = up_down(rows)
    before = lax.ppermute(p_cov[tall - halo :], "row", up)
    after = lax.ppermute(p_cov[:halo], "row", down)
    mine = jnp.where(
        lax.axis_index("row") // fan == lax.axis_index("col"),
        f_blocks,
        lax.ppermute(f_blocks, ("row", "col"), group_pairs(rows, cols)),
    )
    others = []
    for step in range(1, fan):
        turn = [(r // fan * fan + (r + step) % fan, r) for r in range(rows)]
        others.append(lax.ppermute(mine, "row", turn))
    others = jnp.stack(others)

    smem = pl.BlockSpec(memory_space=pltpu.SMEM)
    hbm = pl.BlockSpec(memory_space=ANY)
    vmem = pl.BlockSpec(memory_space=pltpu.VMEM)
    inter = pl.pallas_call(
        stage1_kernel,
        out_shape=jax.ShapeDtypeStruct((tall, wide), jnp.bfloat16),
        in_specs=[smem, vmem, hbm, hbm, hbm],
        out_specs=vmem,
        scratch_shapes=[
            pltpu.VMEM((tall + 2 * halo, wide), jnp.bfloat16),
            pltpu.SemaphoreType.DMA((3,)),
        ],
        compiler_params=pltpu.CompilerParams(vmem_limit_bytes=16 * 2**20),
        name="stage1",
    )(stencil_cols, f_blocks, before, p_cov, after)

    up, down = up_down(cols)
    left = lax.ppermute(inter[:, wide - halo :], "col", up)
    right = lax.ppermute(inter[:, :halo], "col", down)

    return pl.pallas_call(
        functools.partial(stage2_kernel, fan),
        out_shape=jax.ShapeDtypeStruct((tall, wide), jnp.float32),
        grid=(slab,),
        in_specs=[
            smem,
            smem,
            pl.BlockSpec((block_rows, bs), lambda j: (0, 0)),
            pl.BlockSpec((tall, bs), lambda j: (0, j)),
            hbm,
            hbm,
            hbm,
            hbm,
            hbm,
        ],
        out_specs=pl.BlockSpec((tall, bs), lambda j: (0, j)),
        scratch_shapes=[
            pltpu.VMEM((tall, wide + 2 * halo), jnp.bfloat16),
            pltpu.VMEM((slab, STENCIL, bs, bs), jnp.bfloat16),
            pltpu.SemaphoreType.DMA((3 + fan,)),
        ],
        compiler_params=pltpu.CompilerParams(vmem_limit_bytes=16 * 2**20),
        name="stage2",
    )(
        stencil_cols,
        block_mask,
        disturbance_variances.reshape(block_rows, bs),
        localization_weights,
        left,
        inter,
        right,
        mine,
        others,
    )


def solution(mesh):
    placed = (
        P("row", "col"),
        P("row", None, None, None),
        P(),
        P("row", "col"),
        P("row", "col"),
        P("row"),
    )
    return jax.shard_map(
        on_device, mesh=mesh, in_specs=placed, out_specs=P("row", "col"), check_vma=False
    )
```

time: 127 us -> 95.8 us (0.75)
  the two profiles are of different devices: /device:TPU:0 before, /device:TPU:19 now
where the time goes in v1:
time: 95.8 us; the launch traced here: 95.5 us
  waiting for transfers between devices  65.2 us (68%)
  starting transfers between devices  17.2 us (18%)
  Pallas kernels  11.6 us (12%)
  other arithmetic  1.28 us (1%)
    ppermute x1, waiting for transfers between devices, on_device(): after = lax.ppermute(p_cov[:halo], 'row', down)  36.6 us
    ppermute x1, waiting for transfers between devices, on_device(): lax.ppermute(f_blocks, ('row', 'col'), group_pairs(rows, cols))  16.2 us
    pallas_call x1, Pallas kernels, on_device(): pl.pallas_call(functools.partial(stage2_kernel, fan), out_shape=jax.Shape...  7.83 us
    ppermute x1, waiting for transfers between devices, on_device(): right = lax.ppermute(inter[:, :halo], 'col', down)  6.72 us
    ppermute x1, starting transfers between devices, on_device(): before = lax.ppermute(p_cov[tall - halo:], 'row', up)  6.71 us
    ppermute x1, waiting for transfers between devices, on_device(): left = lax.ppermute(inter[:, wide - halo:], 'col', up)  4.1 us
    pallas_call x1, Pallas kernels, on_device(): pl.pallas_call(stage1_kernel, out_shape=jax.ShapeDtypeStruct((tall, wide)...  3.73 us
    ppermute x1, starting transfers between devices, on_device(): left = lax.ppermute(inter[:, wide - halo:], 'col', up)  3.39 us
  transfers between devices with their start and end apart: 6, of which 5 were waited for; matrix products, arithmetic and copies ran while one was open for 2% of the time, Pallas kernels for 4%

profile of v1, /device:TPU:19, one launch (start us, length us, event | category | flops | bytes accessed | tf_op | source)
XLA Modules:
  0.0 95.5 jit_solution(18201003640794454647)
XLA Ops:
  0.0 1.4 %collective-permute-start.4 = (bf16[4,7,128,128]{3,2,1,0:T(8,128)(2,1)}, bf16[4,7,128,128]{3,2,1,0:T(8,128)(2,1)}, u32[]{:S(2)}, u32[]{:S(2)}) collective-permute-start(bf16[4,7,128,128]{3,2,1,0:T(8,128)(2,1)} %f_ref.1), channel_id=1, source_target_pairs={{9,1},{19,2},{25,3},{13,5},{23,6},{29,7},{0,8},{16,10},{26,11},{4,... | collective-permute-start | bytes 2752520 | tf_op jit(solution)/shard_map/ppermute | solution.py:142
  1.4 6.7 %collective-permute-start = (bf16[512,1024]{1,0:T(8,128)(2,1)}, bf16[512,1024]{1,0:T(8,128)(2,1)}, u32[]{:S(2)}, u32[]{:S(2)}) collective-permute-start(bf16[512,1024]{1,0:T(8,128)(2,1)} %own_hbm.1), channel_id=1, source_target_pairs={{0,4},{4,8},{8,12},{12,16},{16,20},{20,24},{24,28},{1,5},{5,9},{9,... | collective-permute-start | bytes 3145736 | tf_op jit(solution)/shard_map/ppermute | solution.py:137
  8.2 1.9 %collective-permute-start.1 = (bf16[512,1024]{1,0:T(8,128)(2,1)}, bf16[512,1024]{1,0:T(8,128)(2,1)}, u32[]{:S(2)}, u32[]{:S(2)}) collective-permute-start(bf16[512,1024]{1,0:T(8,128)(2,1)} %own_hbm.1), channel_id=1, source_target_pairs={{4,0},{8,4},{12,8},{16,12},{20,16},{24,20},{28,24},{5,1},{9,5},{13... | collective-permute-start | bytes 3145736 | tf_op jit(solution)/shard_map/ppermute | solution.py:138
  10.1 16.2 %collective-permute-done.4 = bf16[4,7,128,128]{3,2,1,0:T(8,128)(2,1)} collective-permute-done((bf16[4,7,128,128]{3,2,1,0:T(8,128)(2,1)}, bf16[4,7,128,128]{3,2,1,0:T(8,128)(2,1)}, u32[]{:S(2)}, u32[]{:S(2)}) %collective-permute-start.4) | collective-permute-done | bytes 917536 | tf_op jit(solution)/shard_map/ppermute | solution.py:142
  26.3 1.3 %broadcast_select_fusion.mine_hbm = bf16[4,7,128,128]{3,2,1,0:T(8,128)(2,1)S(1)} fusion(bf16[4,7,128,128]{3,2,1,0:T(8,128)(2,1)} %f_ref.1, bf16[4,7,128,128]{3,2,1,0:T(8,128)(2,1)} %collective-permute-done.4, pred[]{:T(512)S(6)} %eq.3), kind=kLoop, calls=%fused_computation | loop fusion | flops 458752 | bytes 2752513 | tf_op jit(solution)/shard_map/jit(_where)/select_n | solution.py:139
  27.6 1.7 %collective-permute-start.5 = (bf16[4,7,128,128]{3,2,1,0:T(8,128)(2,1)S(1)}, bf16[4,7,128,128]{3,2,1,0:T(8,128)(2,1)}, u32[]{:S(2)}, u32[]{:S(2)}) collective-permute-start(bf16[4,7,128,128]{3,2,1,0:T(8,128)(2,1)S(1)} %broadcast_select_fusion.mine_hbm), channel_id=1, source_target_pairs={{4,0},{0,4},{12,8},{8,12},{20,16},{16,20},{28,24},{24,28},{5,1},{1... | collective-permute-start | bytes 2752520 | tf_op jit(solution)/shard_map/ppermute | solution.py:147
  29.3 0.0 copy-done.5
  29.3 0.1 copy.8.cols_ref
  29.4 1.6 %collective-permute-done.before_hbm = bf16[512,1024]{1,0:T(8,128)(2,1)} collective-permute-done((bf16[512,1024]{1,0:T(8,128)(2,1)}, bf16[512,1024]{1,0:T(8,128)(2,1)}, u32[]{:S(2)}, u32[]{:S(2)}) %collective-permute-start) | collective-permute-done | bytes 1048608 | tf_op jit(solution)/shard_map/ppermute | solution.py:137
  30.9 36.6 %collective-permute-done.1.after_hbm = bf16[512,1024]{1,0:T(8,128)(2,1)} collective-permute-done((bf16[512,1024]{1,0:T(8,128)(2,1)}, bf16[512,1024]{1,0:T(8,128)(2,1)}, u32[]{:S(2)}, u32[]{:S(2)}) %collective-permute-start.1) | collective-permute-done | bytes 1048608 | tf_op jit(solution)/shard_map/ppermute | solution.py:138
  67.5 0.0 copy-done
  67.5 0.0 copy-done.1
  67.5 3.7 %stage1.1.own_hbm = bf16[512,1024]{1,0:T(8,128)(2,1)S(1)} custom-call(s32[32,7]{1,0:T(8,128)S(1)} %copy.8.cols_ref, bf16[4,7,128,128]{3,2,1,0:T(8,128)(2,1)S(1)} %copy-done, bf16[512,1024]{1,0:T(8,128)(2,1)} %collective-permute-done.before_hbm, bf16[512,1024]{1,0:T(8,128)(2,1)S(1)} %copy-done.1, bf16[512,1024]{1,0:T(8,128)(2,1)} %collective-permute-done.1.after_hbm), custom_call_target="tpu_custom_call" | custom-call | tf_op jit(solution)/shard_map/stage1/pallas_call | solution.py:153
  71.3 0.0 copy-start.2
  71.3 0.0 copy-start.3
  71.3 0.0 copy-start.4
  71.3 0.1 fusion
  71.4 2.1 %collective-permute-start.3 = (bf16[512,512]{1,0:T(8,128)(2,1)S(1)}, bf16[512,512]{1,0:T(8,128)(2,1)S(1)}, u32[]{:S(2)}, u32[]{:S(2)}) collective-permute-start(bf16[512,512]{1,0:T(8,128)(2,1)S(1)} %get-tuple-element.5), channel_id=1, source_target_pairs={{1,0},{2,1},{3,2},{5,4},{6,5},{7,6},{9,8},{10,9},{11,10},{13,12},{... | collective-permute-start | bytes 1572872 | tf_op jit(solution)/shard_map/ppermute | solution.py:168
  73.4 3.4 %collective-permute-start.2 = (bf16[512,512]{1,0:T(8,128)(2,1)S(1)}, bf16[512,512]{1,0:T(8,128)(2,1)S(1)}, u32[]{:S(2)}, u32[]{:S(2)}) collective-permute-start(bf16[512,512]{1,0:T(8,128)(2,1)S(1)} %get-tuple-element.6), channel_id=1, source_target_pairs={{0,1},{1,2},{2,3},{4,5},{5,6},{6,7},{8,9},{9,10},{10,11},{12,13},{... | collective-permute-start | bytes 1572872 | tf_op jit(solution)/shard_map/ppermute | solution.py:167
  76.8 6.7 %collective-permute-done.3.right_hbm = bf16[512,512]{1,0:T(8,128)(2,1)S(1)} collective-permute-done((bf16[512,512]{1,0:T(8,128)(2,1)S(1)}, bf16[512,512]{1,0:T(8,128)(2,1)S(1)}, u32[]{:S(2)}, u32[]{:S(2)}) %collective-permute-start.3) | collective-permute-done | bytes 524320 | tf_op jit(solution)/shard_map/ppermute | solution.py:168
  83.6 4.1 %collective-permute-done.2.left_hbm = bf16[512,512]{1,0:T(8,128)(2,1)S(1)} collective-permute-done((bf16[512,512]{1,0:T(8,128)(2,1)S(1)}, bf16[512,512]{1,0:T(8,128)(2,1)S(1)}, u32[]{:S(2)}, u32[]{:S(2)}) %collective-permute-start.2) | collective-permute-done | bytes 524320 | tf_op jit(solution)/shard_map/ppermute | solution.py:167
  87.7 0.0 collective-permute-done.5
  87.7 0.0 copy-done.4
  87.7 7.8 %stage2.1 = f32[512,1024]{1,0:T(8,128)} custom-call(s32[32,7]{1,0:T(8,128)S(1)} %copy.8.cols_ref, s32[4,8]{1,0:T(4,128)S(1)} %copy-done.3, f32[4,128]{1,0:T(4,128)S(1)} %bitcast.2, bf16[512,1024]{1,0:T(8,128)(2,1)S(1)} %copy-done.2, bf16[512,512]{1,0:T(8,128)(2,1)S(1)} %collective-permute-done.2.left_hbm, bf16[512,1024]{1,0:T(8,128)(2,1)S(1)} %stage1.1.own_hbm, ...), custom_call_target="tpu_custom_call" | custom-call | tf_op jit(solution)/shard_map/stage2/pallas_call | solution.py:170
  (5 shorter events, 0.0 us)
Async XLA Ops:
  0.0 67.5 %copy-start = (bf16[4,7,128,128]{3,2,1,0:T(8,128)(2,1)S(1)}, bf16[4,7,128,128]{3,2,1,0:T(8,128)(2,1)}, u32[]{:S(2)}) copy-start(bf16[4,7,128,128]{3,2,1,0:T(8,128)(2,1)} %f_ref.1) | copy-start | bytes 2752516
  0.0 67.5 %copy-start.1 = (bf16[512,1024]{1,0:T(8,128)(2,1)S(1)}, bf16[512,1024]{1,0:T(8,128)(2,1)}, u32[]{:S(2)}) copy-start(bf16[512,1024]{1,0:T(8,128)(2,1)} %own_hbm.1) | copy-start | bytes 3145732
  0.0 29.3 %copy-start.5 = (s32[32,7]{0,1:T(8,128)S(1)}, s32[32,7]{0,1:T(8,128)}, u32[]{:S(2)}) copy-start(s32[32,7]{0,1:T(8,128)} %param.8) | copy-start | bytes 2692
  0.0 26.3 %collective-permute-start.4 = (bf16[4,7,128,128]{3,2,1,0:T(8,128)(2,1)}, bf16[4,7,128,128]{3,2,1,0:T(8,128)(2,1)}, u32[]{:S(2)}, u32[]{:S(2)}) collective-permute-start(bf16[4,7,128,128]{3,2,1,0:T(8,128)(2,1)} %f_ref.1), channel_id=1, source_target_pairs={{9,1},{19,2},{25,3},{13,5},{23,6},{29,7},{0,8},{16,10},{26,11},{4,... | collective-permute-start | bytes 2752520 | tf_op jit(solution)/shard_map/ppermute | solution.py:142
  1.4 29.5 %collective-permute-start = (bf16[512,1024]{1,0:T(8,128)(2,1)}, bf16[512,1024]{1,0:T(8,128)(2,1)}, u32[]{:S(2)}, u32[]{:S(2)}) collective-permute-start(bf16[512,1024]{1,0:T(8,128)(2,1)} %own_hbm.1), channel_id=1, source_target_pairs={{0,4},{4,8},{8,12},{12,16},{16,20},{20,24},{24,28},{1,5},{5,9},{9,... | collective-permute-start | bytes 3145736 | tf_op jit(solution)/shard_map/ppermute | solution.py:137
  8.2 59.4 %collective-permute-start.1 = (bf16[512,1024]{1,0:T(8,128)(2,1)}, bf16[512,1024]{1,0:T(8,128)(2,1)}, u32[]{:S(2)}, u32[]{:S(2)}) collective-permute-start(bf16[512,1024]{1,0:T(8,128)(2,1)} %own_hbm.1), channel_id=1, source_target_pairs={{4,0},{8,4},{12,8},{16,12},{20,16},{24,20},{28,24},{5,1},{9,5},{13... | collective-permute-start | bytes 3145736 | tf_op jit(solution)/shard_map/ppermute | solution.py:138
  27.6 60.1 %collective-permute-start.5 = (bf16[4,7,128,128]{3,2,1,0:T(8,128)(2,1)S(1)}, bf16[4,7,128,128]{3,2,1,0:T(8,128)(2,1)}, u32[]{:S(2)}, u32[]{:S(2)}) collective-permute-start(bf16[4,7,128,128]{3,2,1,0:T(8,128)(2,1)S(1)} %broadcast_select_fusion.mine_hbm), channel_id=1, source_target_pairs={{4,0},{0,4},{12,8},{8,12},{20,16},{16,20},{28,24},{24,28},{5,1},{1... | collective-permute-start | bytes 2752520 | tf_op jit(solution)/shard_map/ppermute | solution.py:147
  71.3 16.4 %copy-start.2 = (bf16[512,1024]{1,0:T(8,128)(2,1)S(1)}, bf16[512,1024]{1,0:T(8,128)(2,1)}, u32[]{:S(2)}) copy-start(bf16[512,1024]{1,0:T(8,128)(2,1)} %w_ref.1) | copy-start | bytes 3145732
  71.3 16.4 %copy-start.3 = (s32[4,8]{1,0:T(4,128)S(1)}, s32[4,8]{1,0:T(4,128)}, u32[]{:S(2)}) copy-start(s32[4,8]{1,0:T(4,128)} %mask_ref.1) | copy-start | bytes 388
  71.3 16.4 %copy-start.4 = (f32[512]{0:T(512)S(1)}, f32[512]{0:T(512)}, u32[]{:S(2)}) copy-start(f32[512]{0:T(512)} %param.11) | copy-start | bytes 6148
  71.4 12.2 %collective-permute-start.3 = (bf16[512,512]{1,0:T(8,128)(2,1)S(1)}, bf16[512,512]{1,0:T(8,128)(2,1)S(1)}, u32[]{:S(2)}, u32[]{:S(2)}) collective-permute-start(bf16[512,512]{1,0:T(8,128)(2,1)S(1)} %get-tuple-element.5), channel_id=1, source_target_pairs={{1,0},{2,1},{3,2},{5,4},{6,5},{7,6},{9,8},{10,9},{11,10},{13,12},{... | collective-permute-start | bytes 1572872 | tf_op jit(solution)/shard_map/ppermute | solution.py:168
  73.4 14.2 %collective-permute-start.2 = (bf16[512,512]{1,0:T(8,128)(2,1)S(1)}, bf16[512,512]{1,0:T(8,128)(2,1)S(1)}, u32[]{:S(2)}, u32[]{:S(2)}) collective-permute-start(bf16[512,512]{1,0:T(8,128)(2,1)S(1)} %get-tuple-element.6), channel_id=1, source_target_pairs={{0,1},{1,2},{2,3},{4,5},{5,6},{6,7},{8,9},{9,10},{10,11},{12,13},{... | collective-permute-start | bytes 1572872 | tf_op jit(solution)/shard_map/ppermute | solution.py:167

commit v2 on v1

--- a/solution.py
+++ b/solution.py
@@ -7,6 +7,7 @@
 from jax.experimental.pallas import tpu as pltpu
 from jax.sharding import PartitionSpec as P
 
+
 STENCIL = 7
 BAND = 4
 ANY = pl.ANY
@@ -23,15 +24,63 @@
     return c ^ (((a ^ c) - 1) % cols)
 
 
-def group_pairs(rows, cols):
+def group_steps(rows, cols):
     fan = rows // cols
-    pairs = []
-    for t in range(rows):
-        a, k = divmod(t, fan)
+
+    def at(a, k, c):
+        return (a * fan + k) * cols + c
+
+    if (cols, fan) != (4, 2):
+        pairs = []
         for c in range(cols):
-            if a != c:
-                pairs.append(((c * fan + k) * cols + source_plane(c, a, cols), t * cols + c))
-    return pairs
+            for a in range(cols):
+                if a != c:
+                    plane = source_plane(c, a, cols)
+                    pairs += [(at(c, k, plane), at(a, k, c)) for k in range(fan)]
+        return [pairs]
+    first, second = [], []
+    for c in range(cols):
+        near, side, far, plane = c ^ 1, c ^ 2, c ^ 3, c ^ 3
+        first += [
+            (at(c, 0, c), at(near, 0, c)),
+            (at(c, 1, c), at(side, 1, c)),
+            (at(c, 1, plane), at(near, 0, plane)),
+            (at(c, 0, plane), at(side, 1, plane)),
+        ]
+        second += [
+            (at(near, 0, c), at(far, 0, c)),
+            (at(side, 1, c), at(far, 1, c)),
+            (at(near, 0, plane), at(near, 1, c)),
+            (at(side, 1, plane), at(side, 0, c)),
+        ]
+    return [first, second]
+
+
+def holder_table(rows, cols):
+    table = [0] * (rows * cols)
+    for step, pairs in enumerate(group_steps(rows, cols)):
+        for _, target in pairs:
+            table[target] = step + 1
+    for a in range(cols):
+        for k in range(rows // cols):
+            table[(a * (rows // cols) + k) * cols + a] = 0
+    return table
+
+
+def pick_kernel(table, *refs):
+    *sources, out_ref, sem = refs
+    me = lax.axis_index("row") * lax.axis_size("col") + lax.axis_index("col")
+    which = 0
+    for device, step in enumerate(table):
+        if step:
+            which = jnp.where(me == device, step, which)
+    for step, source in enumerate(sources):
+
+        @pl.when(which == step)
+        def _():
+            copy = pltpu.make_async_copy(source, out_ref, sem)
+            copy.start()
+            copy.wait()
 
 
 def stage1_kernel(cols_ref, f_ref, before_hbm, own_hbm, after_hbm, out_ref, ext, sem):
@@ -123,7 +172,7 @@
         out_ref[at, :] = w_ref[at, :].astype(jnp.float32) * (spread[at] * keep) + noise
 
 
-def on_device(
+def forecast(
     p_cov, f_blocks, stencil_cols, localization_weights, block_mask, disturbance_variances
 ):
     rows, cols = lax.axis_size("row"), lax.axis_size("col")
@@ -136,11 +185,19 @@
     up, down = up_down(rows)
     before = lax.ppermute(p_cov[tall - halo :], "row", up)
     after = lax.ppermute(p_cov[:halo], "row", down)
-    mine = jnp.where(
-        lax.axis_index("row") // fan == lax.axis_index("col"),
-        f_blocks,
-        lax.ppermute(f_blocks, ("row", "col"), group_pairs(rows, cols)),
-    )
+    steps = group_steps(rows, cols)
+    held = [f_blocks]
+    for pairs in steps:
+        held.append(lax.ppermute(held[-1], ("row", "col"), pairs))
+    mine = pl.pallas_call(
+        functools.partial(pick_kernel, holder_table(rows, cols)),
+        out_shape=jax.ShapeDtypeStruct(f_blocks.shape, f_blocks.dtype),
+        in_specs=[pl.BlockSpec(memory_space=ANY)] * len(held),
+        out_specs=pl.BlockSpec(memory_space=pltpu.VMEM),
+        scratch_shapes=[pltpu.SemaphoreType.DMA],
+        compiler_params=pltpu.CompilerParams(vmem_limit_bytes=4 * 2**20),
+        name="pick",
+    )(*held)
     others = []
     for step in range(1, fan):
         turn = [(r // fan * fan + (r + step) % fan, r) for r in range(rows)]
@@ -213,5 +270,5 @@
         P("row"),
     )
     return jax.shard_map(
-        on_device, mesh=mesh, in_specs=placed, out_specs=P("row", "col"), check_vma=False
-    )
+        forecast, mesh=mesh, in_specs=placed, out_specs=P("row", "col"), check_vma=False
+    )

time: 95.8 us -> 80.4 us (0.84)
  the two profiles are of different devices: /device:TPU:19 before, /device:TPU:26 now
where the time goes in v2:
time: 80.4 us; the launch traced here: 80.1 us
  starting transfers between devices  34.8 us (43%)
  waiting for transfers between devices  32 us (40%)
  Pallas kernels  11.8 us (15%)
  local copies, waits for them, and re-layouts  1.37 us (2%)
    ppermute x2, waiting for transfers between devices, forecast(): held.append(lax.ppermute(held[-1], ('row', 'col'), pairs))  18.4 us
    ppermute x1, starting transfers between devices, forecast(): right = lax.ppermute(inter[:, :halo], 'col', down)  14 us
    ppermute x1, waiting for transfers between devices, forecast(): right = lax.ppermute(inter[:, :halo], 'col', down)  9.42 us
    pallas_call x1, Pallas kernels, forecast(): pl.pallas_call(functools.partial(stage2_kernel, fan), out_shape=jax.Shape...  7.83 us
    ppermute x2, starting transfers between devices, forecast(): held.append(lax.ppermute(held[-1], ('row', 'col'), pairs))  7.17 us
    ppermute x1, starting transfers between devices, forecast(): others.append(lax.ppermute(mine, 'row', turn))  6.05 us
    ppermute x1, starting transfers between devices, forecast(): after = lax.ppermute(p_cov[:halo], 'row', down)  4.32 us
    ppermute x1, waiting for transfers between devices, forecast(): left = lax.ppermute(inter[:, wide - halo:], 'col', up)  4.15 us
  transfers between devices with their start and end apart: 7, of which 4 were waited for; matrix products, arithmetic and copies ran while one was open for 0% of the time, Pallas kernels for 5%

profile of v2, /device:TPU:26, one launch (start us, length us, event | category | flops | bytes accessed | tf_op | source)
XLA Modules:
  0.0 80.1 jit_solution(14217664781173592101)
XLA Ops:
  0.0 1.3 %collective-permute-start.4 = (bf16[4,7,128,128]{3,2,1,0:T(8,128)(2,1)}, bf16[4,7,128,128]{3,2,1,0:T(8,128)(2,1)S(1)}, u32[]{:S(2)}, u32[]{:S(2)}) collective-permute-start(bf16[4,7,128,128]{3,2,1,0:T(8,128)(2,1)} %refs_0_.1), channel_id=1, source_target_pairs={{0,8},{4,20},{7,11},{3,23},{9,1},{13,29},{14,2},{10,30},{18,26},{2... | collective-permute-start | bytes 2752520 | tf_op jit(solution)/shard_map/ppermute | solution.py:191
  1.3 1.9 %collective-permute-start = (bf16[512,1024]{1,0:T(8,128)(2,1)}, bf16[512,1024]{1,0:T(8,128)(2,1)}, u32[]{:S(2)}, u32[]{:S(2)}) collective-permute-start(bf16[512,1024]{1,0:T(8,128)(2,1)} %own_hbm.1), channel_id=1, source_target_pairs={{0,4},{4,8},{8,12},{12,16},{16,20},{20,24},{24,28},{1,5},{5,9},{9,... | collective-permute-start | bytes 3145736 | tf_op jit(solution)/shard_map/ppermute | solution.py:186
  3.2 4.3 %collective-permute-start.1 = (bf16[512,1024]{1,0:T(8,128)(2,1)}, bf16[512,1024]{1,0:T(8,128)(2,1)}, u32[]{:S(2)}, u32[]{:S(2)}) collective-permute-start(bf16[512,1024]{1,0:T(8,128)(2,1)} %own_hbm.1), channel_id=1, source_target_pairs={{4,0},{8,4},{12,8},{16,12},{20,16},{24,20},{28,24},{5,1},{9,5},{13... | collective-permute-start | bytes 3145736 | tf_op jit(solution)/shard_map/ppermute | solution.py:187
  7.6 7.4 %collective-permute-done.4.refs_1_ = bf16[4,7,128,128]{3,2,1,0:T(8,128)(2,1)S(1)} collective-permute-done((bf16[4,7,128,128]{3,2,1,0:T(8,128)(2,1)}, bf16[4,7,128,128]{3,2,1,0:T(8,128)(2,1)S(1)}, u32[]{:S(2)}, u32[]{:S(2)}) %collective-permute-start.4) | collective-permute-done | bytes 917536 | tf_op jit(solution)/shard_map/ppermute | solution.py:191
  14.9 5.9 %collective-permute-start.5 = (bf16[4,7,128,128]{3,2,1,0:T(8,128)(2,1)S(1)}, bf16[4,7,128,128]{3,2,1,0:T(8,128)(2,1)S(1)}, u32[]{:S(2)}, u32[]{:S(2)}) collective-permute-start(bf16[4,7,128,128]{3,2,1,0:T(8,128)(2,1)S(1)} %collective-permute-done.4.refs_1_), channel_id=1, source_target_pairs={{8,24},{20,28},{11,12},{23,16},{1,17},{29,21},{2,5},{30,25},{26,10... | collective-permute-start | bytes 2752520 | tf_op jit(solution)/shard_map/ppermute | solution.py:191
  20.8 11.1 %collective-permute-done.5.refs_2_ = bf16[4,7,128,128]{3,2,1,0:T(8,128)(2,1)S(1)} collective-permute-done((bf16[4,7,128,128]{3,2,1,0:T(8,128)(2,1)S(1)}, bf16[4,7,128,128]{3,2,1,0:T(8,128)(2,1)S(1)}, u32[]{:S(2)}, u32[]{:S(2)}) %collective-permute-start.5) | collective-permute-done | bytes 917536 | tf_op jit(solution)/shard_map/ppermute | solution.py:191
  31.9 1.2 %copy-done = bf16[4,7,128,128]{3,2,1,0:T(8,128)(2,1)S(1)} copy-done((bf16[4,7,128,128]{3,2,1,0:T(8,128)(2,1)S(1)}, bf16[4,7,128,128]{3,2,1,0:T(8,128)(2,1)}, u32[]{:S(2)}) %copy-start) | copy-done | bytes 917528
  33.1 0.2 pick.1.mine_hbm
  33.3 6.1 %collective-permute-start.6 = (bf16[4,7,128,128]{3,2,1,0:T(8,128)(2,1)S(1)}, bf16[4,7,128,128]{3,2,1,0:T(8,128)(2,1)}, u32[]{:S(2)}, u32[]{:S(2)}) collective-permute-start(bf16[4,7,128,128]{3,2,1,0:T(8,128)(2,1)S(1)} %pick.1.mine_hbm), channel_id=1, source_target_pairs={{4,0},{0,4},{12,8},{8,12},{20,16},{16,20},{28,24},{24,28},{5,1},{1... | collective-permute-start | bytes 2752520 | tf_op jit(solution)/shard_map/ppermute | solution.py:204
  39.4 0.1 copy.8.cols_ref
  39.4 0.0 collective-permute-done.before_hbm
  39.4 0.0 collective-permute-done.1.after_hbm
  39.5 3.7 %stage1.1.own_hbm = bf16[512,1024]{1,0:T(8,128)(2,1)S(1)} custom-call(s32[32,7]{1,0:T(8,128)S(1)} %copy.8.cols_ref, bf16[4,7,128,128]{3,2,1,0:T(8,128)(2,1)S(1)} %copy-done.1, bf16[512,1024]{1,0:T(8,128)(2,1)} %collective-permute-done.before_hbm, bf16[512,1024]{1,0:T(8,128)(2,1)S(1)} %copy-done.2, bf16[512,1024]{1,0:T(8,128)(2,1)} %collective-permute-done.1.after_hbm), custom_call_target="tpu_custom_call" | custom-call | tf_op jit(solution)/shard_map/stage1/pallas_call | solution.py:210
  43.2 0.0 copy-start.3
  43.2 0.0 copy-start.4
  43.2 0.0 copy-start.5
  43.2 0.1 fusion
  43.3 14.0 %collective-permute-start.3 = (bf16[512,512]{1,0:T(8,128)(2,1)S(1)}, bf16[512,512]{1,0:T(8,128)(2,1)S(1)}, u32[]{:S(2)}, u32[]{:S(2)}) collective-permute-start(bf16[512,512]{1,0:T(8,128)(2,1)S(1)} %get-tuple-element.5), channel_id=1, source_target_pairs={{1,0},{2,1},{3,2},{5,4},{6,5},{7,6},{9,8},{10,9},{11,10},{13,12},{... | collective-permute-start | bytes 1572872 | tf_op jit(solution)/shard_map/ppermute | solution.py:225
  57.4 1.3 %collective-permute-start.2 = (bf16[512,512]{1,0:T(8,128)(2,1)S(1)}, bf16[512,512]{1,0:T(8,128)(2,1)S(1)}, u32[]{:S(2)}, u32[]{:S(2)}) collective-permute-start(bf16[512,512]{1,0:T(8,128)(2,1)S(1)} %get-tuple-element.6), channel_id=1, source_target_pairs={{0,1},{1,2},{2,3},{4,5},{5,6},{6,7},{8,9},{9,10},{10,11},{12,13},{... | collective-permute-start | bytes 1572872 | tf_op jit(solution)/shard_map/ppermute | solution.py:224
  58.7 9.4 %collective-permute-done.3.right_hbm = bf16[512,512]{1,0:T(8,128)(2,1)S(1)} collective-permute-done((bf16[512,512]{1,0:T(8,128)(2,1)S(1)}, bf16[512,512]{1,0:T(8,128)(2,1)S(1)}, u32[]{:S(2)}, u32[]{:S(2)}) %collective-permute-start.3) | collective-permute-done | bytes 524320 | tf_op jit(solution)/shard_map/ppermute | solution.py:225
  68.1 4.1 %collective-permute-done.2.left_hbm = bf16[512,512]{1,0:T(8,128)(2,1)S(1)} collective-permute-done((bf16[512,512]{1,0:T(8,128)(2,1)S(1)}, bf16[512,512]{1,0:T(8,128)(2,1)S(1)}, u32[]{:S(2)}, u32[]{:S(2)}) %collective-permute-start.2) | collective-permute-done | bytes 524320 | tf_op jit(solution)/shard_map/ppermute | solution.py:224
  72.2 0.0 collective-permute-done.6
  72.2 0.0 copy-done.4
  72.3 7.8 %stage2.1 = f32[512,1024]{1,0:T(8,128)} custom-call(s32[32,7]{1,0:T(8,128)S(1)} %copy.8.cols_ref, s32[4,8]{1,0:T(4,128)S(1)} %copy-done.4, f32[4,128]{1,0:T(4,128)S(1)} %bitcast.2, bf16[512,1024]{1,0:T(8,128)(2,1)S(1)} %copy-done.3, bf16[512,512]{1,0:T(8,128)(2,1)S(1)} %collective-permute-done.2.left_hbm, bf16[512,1024]{1,0:T(8,128)(2,1)S(1)} %stage1.1.own_hbm, ...), custom_call_target="tpu_custom_call" | custom-call | tf_op jit(solution)/shard_map/stage2/pallas_call | solution.py:227
  (9 shorter events, 0.0 us)
Async XLA Ops:
  0.0 14.9 %collective-permute-start.4 = (bf16[4,7,128,128]{3,2,1,0:T(8,128)(2,1)}, bf16[4,7,128,128]{3,2,1,0:T(8,128)(2,1)S(1)}, u32[]{:S(2)}, u32[]{:S(2)}) collective-permute-start(bf16[4,7,128,128]{3,2,1,0:T(8,128)(2,1)} %refs_0_.1), channel_id=1, source_target_pairs={{0,8},{4,20},{7,11},{3,23},{9,1},{13,29},{14,2},{10,30},{18,26},{2... | collective-permute-start | bytes 2752520 | tf_op jit(solution)/shard_map/ppermute | solution.py:191
  1.3 38.2 %collective-permute-start = (bf16[512,1024]{1,0:T(8,128)(2,1)}, bf16[512,1024]{1,0:T(8,128)(2,1)}, u32[]{:S(2)}, u32[]{:S(2)}) collective-permute-start(bf16[512,1024]{1,0:T(8,128)(2,1)} %own_hbm.1), channel_id=1, source_target_pairs={{0,4},{4,8},{8,12},{12,16},{16,20},{20,24},{24,28},{1,5},{5,9},{9,... | collective-permute-start | bytes 3145736 | tf_op jit(solution)/shard_map/ppermute | solution.py:186
  3.2 36.2 %collective-permute-start.1 = (bf16[512,1024]{1,0:T(8,128)(2,1)}, bf16[512,1024]{1,0:T(8,128)(2,1)}, u32[]{:S(2)}, u32[]{:S(2)}) collective-permute-start(bf16[512,1024]{1,0:T(8,128)(2,1)} %own_hbm.1), channel_id=1, source_target_pairs={{4,0},{8,4},{12,8},{16,12},{20,16},{24,20},{28,24},{5,1},{9,5},{13... | collective-permute-start | bytes 3145736 | tf_op jit(solution)/shard_map/ppermute | solution.py:187
  14.9 17.0 %collective-permute-start.5 = (bf16[4,7,128,128]{3,2,1,0:T(8,128)(2,1)S(1)}, bf16[4,7,128,128]{3,2,1,0:T(8,128)(2,1)S(1)}, u32[]{:S(2)}, u32[]{:S(2)}) collective-permute-start(bf16[4,7,128,128]{3,2,1,0:T(8,128)(2,1)S(1)} %collective-permute-done.4.refs_1_), channel_id=1, source_target_pairs={{8,24},{20,28},{11,12},{23,16},{1,17},{29,21},{2,5},{30,25},{26,10... | collective-permute-start | bytes 2752520 | tf_op jit(solution)/shard_map/ppermute | solution.py:191
  31.9 1.2 %copy-start = (bf16[4,7,128,128]{3,2,1,0:T(8,128)(2,1)S(1)}, bf16[4,7,128,128]{3,2,1,0:T(8,128)(2,1)}, u32[]{:S(2)}) copy-start(bf16[4,7,128,128]{3,2,1,0:T(8,128)(2,1)} %refs_0_.1) | copy-start | bytes 2752516
  33.1 6.3 %copy-start.6 = (s32[32,7]{0,1:T(8,128)S(1)}, s32[32,7]{0,1:T(8,128)}, u32[]{:S(2)}) copy-start(s32[32,7]{0,1:T(8,128)} %param.8) | copy-start | bytes 2692
  33.1 6.4 %copy-start.1 = (bf16[4,7,128,128]{3,2,1,0:T(8,128)(2,1)S(1)}, bf16[4,7,128,128]{3,2,1,0:T(8,128)(2,1)}, u32[]{:S(2)}) copy-start(bf16[4,7,128,128]{3,2,1,0:T(8,128)(2,1)} %refs_0_.1) | copy-start | bytes 2752516
  33.1 6.4 %copy-start.2 = (bf16[512,1024]{1,0:T(8,128)(2,1)S(1)}, bf16[512,1024]{1,0:T(8,128)(2,1)}, u32[]{:S(2)}) copy-start(bf16[512,1024]{1,0:T(8,128)(2,1)} %own_hbm.1) | copy-start | bytes 3145732
  33.3 38.9 %collective-permute-start.6 = (bf16[4,7,128,128]{3,2,1,0:T(8,128)(2,1)S(1)}, bf16[4,7,128,128]{3,2,1,0:T(8,128)(2,1)}, u32[]{:S(2)}, u32[]{:S(2)}) collective-permute-start(bf16[4,7,128,128]{3,2,1,0:T(8,128)(2,1)S(1)} %pick.1.mine_hbm), channel_id=1, source_target_pairs={{4,0},{0,4},{12,8},{8,12},{20,16},{16,20},{28,24},{24,28},{5,1},{1... | collective-permute-start | bytes 2752520 | tf_op jit(solution)/shard_map/ppermute | solution.py:204
  43.2 29.0 %copy-start.3 = (bf16[512,1024]{1,0:T(8,128)(2,1)S(1)}, bf16[512,1024]{1,0:T(8,128)(2,1)}, u32[]{:S(2)}) copy-start(bf16[512,1024]{1,0:T(8,128)(2,1)} %w_ref.1) | copy-start | bytes 3145732
  43.2 29.0 %copy-start.4 = (s32[4,8]{1,0:T(4,128)S(1)}, s32[4,8]{1,0:T(4,128)}, u32[]{:S(2)}) copy-start(s32[4,8]{1,0:T(4,128)} %mask_ref.1) | copy-start | bytes 388
  43.2 29.0 %copy-start.5 = (f32[512]{0:T(512)S(1)}, f32[512]{0:T(512)}, u32[]{:S(2)}) copy-start(f32[512]{0:T(512)} %param.11) | copy-start | bytes 6148
  43.3 24.8 %collective-permute-start.3 = (bf16[512,512]{1,0:T(8,128)(2,1)S(1)}, bf16[512,512]{1,0:T(8,128)(2,1)S(1)}, u32[]{:S(2)}, u32[]{:S(2)}) collective-permute-start(bf16[512,512]{1,0:T(8,128)(2,1)S(1)} %get-tuple-element.5), channel_id=1, source_target_pairs={{1,0},{2,1},{3,2},{5,4},{6,5},{7,6},{9,8},{10,9},{11,10},{13,12},{... | collective-permute-start | bytes 1572872 | tf_op jit(solution)/shard_map/ppermute | solution.py:225
  57.4 14.9 %collective-permute-start.2 = (bf16[512,512]{1,0:T(8,128)(2,1)S(1)}, bf16[512,512]{1,0:T(8,128)(2,1)S(1)}, u32[]{:S(2)}, u32[]{:S(2)}) collective-permute-start(bf16[512,512]{1,0:T(8,128)(2,1)S(1)} %get-tuple-element.6), channel_id=1, source_target_pairs={{0,1},{1,2},{2,3},{4,5},{5,6},{6,7},{8,9},{9,10},{10,11},{12,13},{... | collective-permute-start | bytes 1572872 | tf_op jit(solution)/shard_map/ppermute | solution.py:224

commit v3 on v2

v3 whole, which is shorter than its diff:
```python
import functools

import jax
import jax.numpy as jnp
from jax import lax
from jax.experimental import pallas as pl
from jax.experimental.pallas import tpu as pltpu
from jax.sharding import PartitionSpec as P


STENCIL = 7
BAND = 4
ANY = pl.ANY


def up_down(devices):
    up = [(i, i + 1) for i in range(devices - 1)]
    return up, [(j, i) for i, j in up]


def source_plane(c, a, cols):
    if cols & (cols - 1):
        return a
    return c ^ (((a ^ c) - 1) % cols)


def group_plan(rows, cols):
    fan = rows // cols

    def at(a, k, c):
        return (a * fan + k) * cols + c

    if (cols, fan) != (4, 2):
        pairs = []
        for c in range(cols):
            for a in range(cols):
                if a != c:
                    plane = source_plane(c, a, cols)
                    pairs += [(at(c, k, plane), at(a, k, c)) for k in range(fan)]
        return [(0, pairs)]
    first, relayed, second = [], [], []
    for c in range(cols):
        near, side, far = c ^ 1, c ^ 2, c ^ 3
        first += [(at(c, 0, c), at(near, 0, c)), (at(c, 1, c), at(side, 1, c))]
        relayed += [(at(near, 0, c), at(far, 0, c)), (at(side, 1, c), at(far, 1, c))]
        second += [(at(c, 0, c), at(side, 0, c)), (at(c, 1, c), at(near, 1, c))]
    return [(0, first), (1, relayed), (0, second)]


def holder_table(rows, cols):
    table = [0] * (rows * cols)
    for step, (_, pairs) in enumerate(group_plan(rows, cols)):
        for _, target in pairs:
            table[target] = step + 1
    return table


def pick_kernel(table, *refs):
    *sources, out_ref, sem = refs
    me = lax.axis_index("row") * lax.axis_size("col") + lax.axis_index("col")
    which = 0
    for device, step in enumerate(table):
        if step:
            which = jnp.where(me == device, step, which)
    for step, source in enumerate(sources):

        @pl.when(which == step)
        def _():
            copy = pltpu.make_async_copy(source, out_ref, sem)
            copy.start()
            copy.wait()


def fetch_kernel(p_hbm, f_hbm, p_ref, f_ref, sem):
    copies = [
        pltpu.make_async_copy(p_hbm, p_ref, sem.at[0]),
        pltpu.make_async_copy(f_hbm, f_ref, sem.at[1]),
    ]
    for copy in copies:
        copy.start()
    for copy in copies:
        copy.wait()


def stage1_kernel(
    cols_ref, f_ref, before_hbm, own_hbm, after_hbm, low_ref, high_ref, ext, sem
):
    rows, bs = f_ref.shape[0], f_ref.shape[2]
    half = low_ref.shape[1]
    first = lax.axis_index("row") * rows
    halo, tall = before_hbm.shape[0], own_hbm.shape[0]
    copies = [
        pltpu.make_async_copy(before_hbm, ext.at[pl.ds(0, halo)], sem.at[0]),
        pltpu.make_async_copy(own_hbm, ext.at[pl.ds(halo, tall)], sem.at[1]),
        pltpu.make_async_copy(after_hbm, ext.at[pl.ds(halo + tall, halo)], sem.at[2]),
    ]
    for copy in copies:
        copy.start()
    for copy in copies:
        copy.wait()
    tile = min(256, half)
    for i in range(rows):
        lhs = jnp.concatenate([f_ref[i, e] for e in range(STENCIL)], axis=1)
        starts = [
            pl.multiple_of((cols_ref[e, first + i] - first + BAND) * bs, bs)
            for e in range(STENCIL)
        ]
        for part, out_ref in enumerate((low_ref, high_ref)):
            for t in range(half // tile):
                at = part * half + t * tile
                rhs = jnp.concatenate(
                    [ext[pl.ds(s, bs), at : at + tile] for s in starts], axis=0
                )
                out_ref[i * bs : (i + 1) * bs, t * tile : (t + 1) * tile] = jnp.dot(
                    lhs, rhs, preferred_element_type=jnp.float32
                ).astype(out_ref.dtype)


def stage2_kernel(
    fan, cols_ref, mask_ref, q_ref, w_ref, left_hbm, low_hbm, high_hbm, right_hbm, mine_hbm,
    others_hbm, out_ref, ext, f_all, sem,
):
    j = pl.program_id(0)
    slab = pl.num_programs(0)
    bs = out_ref.shape[1]
    rows = out_ref.shape[0] // bs
    group = f_all.shape[0] // fan
    row_idx, col_idx = lax.axis_index("row"), lax.axis_index("col")

    @pl.when(j == 0)
    def _():
        k = lax.rem(row_idx, fan)
        copies = [pltpu.make_async_copy(mine_hbm, f_all.at[pl.ds(k * group, group)], sem.at[0])]
        for step in range(1, fan):
            at = lax.rem(k + step, fan) * group
            copies.append(
                pltpu.make_async_copy(
                    others_hbm.at[step - 1], f_all.at[pl.ds(at, group)], sem.at[step]
                )
            )
        at = 0
        for piece, part in enumerate((left_hbm, low_hbm, high_hbm, right_hbm)):
            copies.append(
                pltpu.make_async_copy(
                    part, ext.at[:, pl.ds(at, part.shape[1])], sem.at[fan + piece]
                )
            )
            at += part.shape[1]
        for copy in copies:
            copy.start()
        for copy in copies:
            copy.wait()

    col = col_idx * slab + j
    first = col_idx * slab - BAND
    lhs = jnp.concatenate(
        [
            ext[:, pl.ds(pl.multiple_of((cols_ref[e, col] - first) * bs, bs), bs)]
            for e in range(STENCIL)
        ],
        axis=1,
    )
    rhs = jnp.concatenate([f_all[j, e] for e in range(STENCIL)], axis=1)
    spread = lax.dot_general(
        lhs, rhs, (((1,), (1,)), ((), ())), preferred_element_type=jnp.float32
    )
    eye = lax.broadcasted_iota(jnp.int32, (bs, bs), 0) == lax.broadcasted_iota(
        jnp.int32, (bs, bs), 1
    )
    for i in range(rows):
        at = slice(i * bs, (i + 1) * bs)
        keep = mask_ref[i, j].astype(jnp.float32)
        on_main = (row_idx * rows + i == col).astype(jnp.float32)
        noise = jnp.where(eye, q_ref[i : i + 1, :] * on_main, 0.0)
        out_ref[at, :] = w_ref[at, :].astype(jnp.float32) * (spread[at] * keep) + noise


def forecast(
    p_cov, f_blocks, stencil_cols, localization_weights, block_mask, disturbance_variances
):
    rows, cols = lax.axis_size("row"), lax.axis_size("col")
    fan = rows // cols
    block_rows, bs = f_blocks.shape[0], f_blocks.shape[2]
    tall, wide = p_cov.shape
    slab = wide // bs
    halo = BAND * bs
    assert tall == halo and wide == 2 * halo
    cols_of = stencil_cols.T

    up, down = up_down(rows)
    before = lax.ppermute(p_cov, "row", up)
    after = lax.ppermute(p_cov, "row", down)
    held = [f_blocks]
    for source, pairs in group_plan(rows, cols):
        held.append(lax.ppermute(held[source], ("row", "col"), pairs))

    smem = pl.BlockSpec(memory_space=pltpu.SMEM)
    hbm = pl.BlockSpec(memory_space=ANY)
    vmem = pl.BlockSpec(memory_space=pltpu.VMEM)
    p_near, f_near = pl.pallas_call(
        fetch_kernel,
        out_shape=(
            jax.ShapeDtypeStruct(p_cov.shape, p_cov.dtype),
            jax.ShapeDtypeStruct(f_blocks.shape, f_blocks.dtype),
        ),
        in_specs=[hbm, hbm],
        out_specs=(vmem, vmem),
        scratch_shapes=[pltpu.SemaphoreType.DMA((2,))],
        compiler_params=pltpu.CompilerParams(vmem_limit_bytes=8 * 2**20),
        name="fetch",
    )(p_cov, f_blocks)
    half = jax.ShapeDtypeStruct((tall, halo), jnp.bfloat16)
    low, high = pl.pallas_call(
        stage1_kernel,
        out_shape=(half, half),
        in_specs=[smem, vmem, hbm, hbm, hbm],
        out_specs=(vmem, vmem),
        scratch_shapes=[
            pltpu.VMEM((tall + 2 * halo, wide), jnp.bfloat16),
            pltpu.SemaphoreType.DMA((3,)),
        ],
        compiler_params=pltpu.CompilerParams(vmem_limit_bytes=16 * 2**20),
        name="stage1",
    )(cols_of, f_near, before, p_near, after)

    up, down = up_down(cols)
    left = lax.ppermute(high, "col", up)
    right = lax.ppermute(low, "col", down)

    mine = pl.pallas_call(
        functools.partial(pick_kernel, holder_table(rows, cols)),
        out_shape=jax.ShapeDtypeStruct(f_blocks.shape, f_blocks.dtype),
        in_specs=[hbm] * len(held),
        out_specs=vmem,
        scratch_shapes=[pltpu.SemaphoreType.DMA],
        compiler_params=pltpu.CompilerParams(vmem_limit_bytes=4 * 2**20),
        name="pick",
    )(*held)
    others = []
    for step in range(1, fan):
        turn = [(r // fan * fan + (r + step) % fan, r) for r in range(rows)]
        others.append(lax.ppermute(mine, "row", turn))
    others = jnp.stack(others)

    return pl.pallas_call(
        functools.partial(stage2_kernel, fan),
        out_shape=jax.ShapeDtypeStruct((tall, wide), jnp.float32),
        grid=(slab,),
        in_specs=[
            smem,
            smem,
            pl.BlockSpec((block_rows, bs), lambda j: (0, 0)),
            pl.BlockSpec((tall, bs), lambda j: (0, j)),
        ]
        + [hbm] * 6,
        out_specs=pl.BlockSpec((tall, bs), lambda j: (0, j)),
        scratch_shapes=[
            pltpu.VMEM((tall, wide + 2 * halo), jnp.bfloat16),
            pltpu.VMEM((slab, STENCIL, bs, bs), jnp.bfloat16),
            pltpu.SemaphoreType.DMA((4 + fan,)),
        ],
        compiler_params=pltpu.CompilerParams(vmem_limit_bytes=16 * 2**20),
        name="stage2",
    )(
        cols_of,
        block_mask,
        disturbance_variances.reshape(block_rows, bs),
        localization_weights,
        left,
        low,
        high,
        right,
        mine,
        others,
    )


def solution(mesh):
    placed = (
        P("row", "col"),
        P("row", None, None, None),
        P(),
        P("row", "col"),
        P("row", "col"),
        P("row"),
    )
    return jax.shard_map(
        forecast, mesh=mesh, in_specs=placed, out_specs=P("row", "col"), check_vma=False
    )
```

time: 80.4 us -> 89.5 us (1.11)
  the two profiles are of different devices: /device:TPU:26 before, /device:TPU:6 now
where the time goes in v3:
time: 89.5 us; the launch traced here: 89.2 us
  starting transfers between devices  53 us (59%)
  waiting for transfers between devices  25.6 us (29%)
  Pallas kernels  9.29 us (10%)
  local copies, waits for them, and re-layouts  1.2 us (1%)
    ppermute x1, starting transfers between devices, forecast(): after = lax.ppermute(p_cov, 'row', down)  33.7 us
    ppermute x1, waiting for transfers between devices, forecast(): before = lax.ppermute(p_cov, 'row', up)  15.8 us
    ppermute x1, starting transfers between devices, forecast(): others.append(lax.ppermute(mine, 'row', turn))  12 us
    pallas_call x1, Pallas kernels, forecast(): pl.pallas_call(functools.partial(stage2_kernel, fan), out_shape=jax.Shape...  6.62 us
    ppermute x1, waiting for transfers between devices, forecast(): left = lax.ppermute(high, 'col', up)  5.35 us
    ppermute x1, waiting for transfers between devices, forecast(): right = lax.ppermute(low, 'col', down)  4.43 us
    ppermute x3, starting transfers between devices, forecast(): held.append(lax.ppermute(held[source], ('row', 'col'), pairs))  2.72 us
    pallas_call x1, Pallas kernels, forecast(): pl.pallas_call(stage1_kernel, out_shape=(half, half), in_specs=[smem, vme...  2.13 us
  transfers between devices with their start and end apart: 8, of which 3 were waited for; matrix products, arithmetic and copies ran while one was open for 0% of the time, Pallas kernels for 3%

profile of v3, /device:TPU:6, one launch (start us, length us, event | category | flops | bytes accessed | tf_op | source)
XLA Modules:
  0.0 89.2 jit_solution(14707854763869187926)
XLA Ops:
  0.0 0.7 collective-permute-start.4
  0.7 0.7 collective-permute-start.6
  1.4 0.0 collective-permute-done.4.refs_1_
  1.5 1.3 %collective-permute-start.5 = (bf16[4,7,128,128]{3,2,1,0:T(8,128)(2,1)S(1)}, bf16[4,7,128,128]{3,2,1,0:T(8,128)(2,1)S(1)}, u32[]{:S(2)}, u32[]{:S(2)}) collective-permute-start(bf16[4,7,128,128]{3,2,1,0:T(8,128)(2,1)S(1)} %collective-permute-done.4.refs_1_), channel_id=1, source_target_pairs={{8,24},{20,28},{1,17},{29,21},{26,10},{6,14},{19,3},{15,7}} | collective-permute-start | bytes 2752520 | tf_op jit(solution)/shard_map/ppermute | solution.py:195
  2.8 1.9 %collective-permute-start = (bf16[512,1024]{1,0:T(8,128)(2,1)}, bf16[512,1024]{1,0:T(8,128)(2,1)S(1)}, u32[]{:S(2)}, u32[]{:S(2)}) collective-permute-start(bf16[512,1024]{1,0:T(8,128)(2,1)} %p_hbm.1), channel_id=1, source_target_pairs={{0,4},{4,8},{8,12},{12,16},{16,20},{20,24},{24,28},{1,5},{5,9},{9,... | collective-permute-start | bytes 3145736 | tf_op jit(solution)/shard_map/ppermute | solution.py:191
  4.7 33.7 %collective-permute-start.1 = (bf16[512,1024]{1,0:T(8,128)(2,1)}, bf16[512,1024]{1,0:T(8,128)(2,1)S(1)}, u32[]{:S(2)}, u32[]{:S(2)}) collective-permute-start(bf16[512,1024]{1,0:T(8,128)(2,1)} %p_hbm.1), channel_id=1, source_target_pairs={{4,0},{8,4},{12,8},{16,12},{20,16},{24,20},{28,24},{5,1},{9,5},{13... | collective-permute-start | bytes 3145736 | tf_op jit(solution)/shard_map/ppermute | solution.py:192
  38.4 0.0 collective-permute-done.6.refs_3_
  38.4 0.0 collective-permute-done.5.refs_2_
  38.4 1.2 %copy-done = bf16[4,7,128,128]{3,2,1,0:T(8,128)(2,1)S(1)} copy-done((bf16[4,7,128,128]{3,2,1,0:T(8,128)(2,1)S(1)}, bf16[4,7,128,128]{3,2,1,0:T(8,128)(2,1)}, u32[]{:S(2)}) %copy-start) | copy-done | bytes 917528
  39.6 0.2 pick.1.mine_hbm
  39.8 12.0 %collective-permute-start.7 = (bf16[4,7,128,128]{3,2,1,0:T(8,128)(2,1)S(1)}, bf16[4,7,128,128]{3,2,1,0:T(8,128)(2,1)S(1)}, u32[]{:S(2)}, u32[]{:S(2)}) collective-permute-start(bf16[4,7,128,128]{3,2,1,0:T(8,128)(2,1)S(1)} %pick.1.mine_hbm), channel_id=1, source_target_pairs={{4,0},{0,4},{12,8},{8,12},{20,16},{16,20},{28,24},{24,28},{5,1},{1... | collective-permute-start | bytes 2752520 | tf_op jit(solution)/shard_map/ppermute | solution.py:242
  51.9 0.3 fetch.1
  52.2 0.0 copy-start.3
  52.2 0.0 copy-start.5
  52.2 0.0 copy-start.6
  52.3 15.8 %collective-permute-done.before_hbm = bf16[512,1024]{1,0:T(8,128)(2,1)S(1)} collective-permute-done((bf16[512,1024]{1,0:T(8,128)(2,1)}, bf16[512,1024]{1,0:T(8,128)(2,1)S(1)}, u32[]{:S(2)}, u32[]{:S(2)}) %collective-permute-start) | collective-permute-done | bytes 1048608 | tf_op jit(solution)/shard_map/ppermute | solution.py:191
  68.0 0.0 collective-permute-done.1.after_hbm
  68.0 2.1 %stage1.1 = (bf16[512,512]{1,0:T(8,128)(2,1)S(1)}, bf16[512,512]{1,0:T(8,128)(2,1)S(1)}) custom-call(s32[7,32]{1,0:T(8,128)S(1)} %bitcast.4, bf16[4,7,128,128]{3,2,1,0:T(8,128)(2,1)S(1)} %get-tuple-element.9.f_ref, bf16[512,1024]{1,0:T(8,128)(2,1)S(1)} %collective-permute-done.before_hbm, bf16[512,1024]{1,0:T(8,128)(2,1)S(1)} %get-tuple-element.10.own_hbm, ...), custom_call_target="tpu_custom_call" | custom-call | tf_op jit(solution)/shard_map/stage1/pallas_call | solution.py:213
  70.2 1.3 %collective-permute-start.2 = (bf16[512,512]{1,0:T(8,128)(2,1)S(1)}, bf16[512,512]{1,0:T(8,128)(2,1)S(1)}, u32[]{:S(2)}, u32[]{:S(2)}) collective-permute-start(bf16[512,512]{1,0:T(8,128)(2,1)S(1)} %get-tuple-element.11.high_hbm), channel_id=1, source_target_pairs={{0,1},{1,2},{2,3},{4,5},{5,6},{6,7},{8,9},{9,10},{10,11},{12,13},{... | collective-permute-start | bytes 1572872 | tf_op jit(solution)/shard_map/ppermute | solution.py:227
  71.5 1.3 %collective-permute-start.3 = (bf16[512,512]{1,0:T(8,128)(2,1)S(1)}, bf16[512,512]{1,0:T(8,128)(2,1)S(1)}, u32[]{:S(2)}, u32[]{:S(2)}) collective-permute-start(bf16[512,512]{1,0:T(8,128)(2,1)S(1)} %get-tuple-element.12.low_hbm), channel_id=1, source_target_pairs={{1,0},{2,1},{3,2},{5,4},{6,5},{7,6},{9,8},{10,9},{11,10},{13,12},{... | collective-permute-start | bytes 1572872 | tf_op jit(solution)/shard_map/ppermute | solution.py:228
  72.8 5.3 %collective-permute-done.2.left_hbm = bf16[512,512]{1,0:T(8,128)(2,1)S(1)} collective-permute-done((bf16[512,512]{1,0:T(8,128)(2,1)S(1)}, bf16[512,512]{1,0:T(8,128)(2,1)S(1)}, u32[]{:S(2)}, u32[]{:S(2)}) %collective-permute-start.2) | collective-permute-done | bytes 524320 | tf_op jit(solution)/shard_map/ppermute | solution.py:227
  78.1 4.4 %collective-permute-done.3.right_hbm = bf16[512,512]{1,0:T(8,128)(2,1)S(1)} collective-permute-done((bf16[512,512]{1,0:T(8,128)(2,1)S(1)}, bf16[512,512]{1,0:T(8,128)(2,1)S(1)}, u32[]{:S(2)}, u32[]{:S(2)}) %collective-permute-start.3) | collective-permute-done | bytes 524320 | tf_op jit(solution)/shard_map/ppermute | solution.py:228
  82.6 0.0 collective-permute-done.7
  82.6 6.6 %stage2.1 = f32[512,1024]{1,0:T(8,128)} custom-call(s32[7,32]{1,0:T(8,128)S(1)} %bitcast.5, s32[4,8]{1,0:T(4,128)S(1)} %copy-done.5, f32[4,128]{1,0:T(4,128)S(1)} %bitcast.6, bf16[512,1024]{1,0:T(8,128)(2,1)S(1)} %copy-done.3, bf16[512,512]{1,0:T(8,128)(2,1)S(1)} %collective-permute-done.2.left_hbm, bf16[512,512]{1,0:T(8,128)(2,1)S(1)} %get-tuple-element.12.low_hbm, ...), custom_call_target="tpu_custom_call" | custom-call | tf_op jit(solution)/shard_map/stage2/pallas_call | solution.py:245
  (10 shorter events, 0.0 us)
Async XLA Ops:
  0.0 1.4 %collective-permute-start.4 = (bf16[4,7,128,128]{3,2,1,0:T(8,128)(2,1)}, bf16[4,7,128,128]{3,2,1,0:T(8,128)(2,1)S(1)}, u32[]{:S(2)}, u32[]{:S(2)}) collective-permute-start(bf16[4,7,128,128]{3,2,1,0:T(8,128)(2,1)} %refs_0_.1), channel_id=1, source_target_pairs={{0,8},{4,20},{9,1},{13,29},{18,26},{22,6},{27,19},{31,15}} | collective-permute-start | bytes 2752520 | tf_op jit(solution)/shard_map/ppermute | solution.py:195
  0.7 37.7 %collective-permute-start.6 = (bf16[4,7,128,128]{3,2,1,0:T(8,128)(2,1)}, bf16[4,7,128,128]{3,2,1,0:T(8,128)(2,1)S(1)}, u32[]{:S(2)}, u32[]{:S(2)}) collective-permute-start(bf16[4,7,128,128]{3,2,1,0:T(8,128)(2,1)} %refs_0_.1), channel_id=1, source_target_pairs={{0,16},{4,12},{9,25},{13,5},{18,2},{22,30},{27,11},{31,23}} | collective-permute-start | bytes 2752520 | tf_op jit(solution)/shard_map/ppermute | solution.py:195
  1.5 37.0 %collective-permute-start.5 = (bf16[4,7,128,128]{3,2,1,0:T(8,128)(2,1)S(1)}, bf16[4,7,128,128]{3,2,1,0:T(8,128)(2,1)S(1)}, u32[]{:S(2)}, u32[]{:S(2)}) collective-permute-start(bf16[4,7,128,128]{3,2,1,0:T(8,128)(2,1)S(1)} %collective-permute-done.4.refs_1_), channel_id=1, source_target_pairs={{8,24},{20,28},{1,17},{29,21},{26,10},{6,14},{19,3},{15,7}} | collective-permute-start | bytes 2752520 | tf_op jit(solution)/shard_map/ppermute | solution.py:195
  2.8 65.3 %collective-permute-start = (bf16[512,1024]{1,0:T(8,128)(2,1)}, bf16[512,1024]{1,0:T(8,128)(2,1)S(1)}, u32[]{:S(2)}, u32[]{:S(2)}) collective-permute-start(bf16[512,1024]{1,0:T(8,128)(2,1)} %p_hbm.1), channel_id=1, source_target_pairs={{0,4},{4,8},{8,12},{12,16},{16,20},{20,24},{24,28},{1,5},{5,9},{9,... | collective-permute-start | bytes 3145736 | tf_op jit(solution)/shard_map/ppermute | solution.py:191
  4.7 63.3 %collective-permute-start.1 = (bf16[512,1024]{1,0:T(8,128)(2,1)}, bf16[512,1024]{1,0:T(8,128)(2,1)S(1)}, u32[]{:S(2)}, u32[]{:S(2)}) collective-permute-start(bf16[512,1024]{1,0:T(8,128)(2,1)} %p_hbm.1), channel_id=1, source_target_pairs={{4,0},{8,4},{12,8},{16,12},{20,16},{24,20},{28,24},{5,1},{9,5},{13... | collective-permute-start | bytes 3145736 | tf_op jit(solution)/shard_map/ppermute | solution.py:192
  38.4 1.2 %copy-start = (bf16[4,7,128,128]{3,2,1,0:T(8,128)(2,1)S(1)}, bf16[4,7,128,128]{3,2,1,0:T(8,128)(2,1)}, u32[]{:S(2)}) copy-start(bf16[4,7,128,128]{3,2,1,0:T(8,128)(2,1)} %refs_0_.1) | copy-start | bytes 2752516
  39.6 12.3 %copy-start.1 = (bf16[4,7,128,128]{3,2,1,0:T(8,128)(2,1)S(1)}, bf16[4,7,128,128]{3,2,1,0:T(8,128)(2,1)}, u32[]{:S(2)}) copy-start(bf16[4,7,128,128]{3,2,1,0:T(8,128)(2,1)} %refs_0_.1) | copy-start | bytes 2752516
  39.6 12.3 %copy-start.2 = (bf16[512,1024]{1,0:T(8,128)(2,1)S(1)}, bf16[512,1024]{1,0:T(8,128)(2,1)}, u32[]{:S(2)}) copy-start(bf16[512,1024]{1,0:T(8,128)(2,1)} %p_hbm.1) | copy-start | bytes 3145732
  39.6 28.4 %copy-start.4 = (s32[32,7]{0,1:T(8,128)S(1)}, s32[32,7]{0,1:T(8,128)}, u32[]{:S(2)}) copy-start(s32[32,7]{0,1:T(8,128)} %param.8) | copy-start | bytes 2692
  39.8 42.7 %collective-permute-start.7 = (bf16[4,7,128,128]{3,2,1,0:T(8,128)(2,1)S(1)}, bf16[4,7,128,128]{3,2,1,0:T(8,128)(2,1)S(1)}, u32[]{:S(2)}, u32[]{:S(2)}) collective-permute-start(bf16[4,7,128,128]{3,2,1,0:T(8,128)(2,1)S(1)} %pick.1.mine_hbm), channel_id=1, source_target_pairs={{4,0},{0,4},{12,8},{8,12},{20,16},{16,20},{28,24},{24,28},{5,1},{1... | collective-permute-start | bytes 2752520 | tf_op jit(solution)/shard_map/ppermute | solution.py:242
  52.2 30.4 %copy-start.3 = (bf16[512,1024]{1,0:T(8,128)(2,1)S(1)}, bf16[512,1024]{1,0:T(8,128)(2,1)}, u32[]{:S(2)}) copy-start(bf16[512,1024]{1,0:T(8,128)(2,1)} %w_ref.1) | copy-start | bytes 3145732
  52.2 30.4 %copy-start.5 = (s32[4,8]{1,0:T(4,128)S(1)}, s32[4,8]{1,0:T(4,128)}, u32[]{:S(2)}) copy-start(s32[4,8]{1,0:T(4,128)} %mask_ref.1) | copy-start | bytes 388
  52.2 30.3 %copy-start.6 = (f32[512]{0:T(512)S(1)}, f32[512]{0:T(512)}, u32[]{:S(2)}) copy-start(f32[512]{0:T(512)} %param.11) | copy-start | bytes 6148
  70.2 8.0 %collective-permute-start.2 = (bf16[512,512]{1,0:T(8,128)(2,1)S(1)}, bf16[512,512]{1,0:T(8,128)(2,1)S(1)}, u32[]{:S(2)}, u32[]{:S(2)}) collective-permute-start(bf16[512,512]{1,0:T(8,128)(2,1)S(1)} %get-tuple-element.11.high_hbm), channel_id=1, source_target_pairs={{0,1},{1,2},{2,3},{4,5},{5,6},{6,7},{8,9},{9,10},{10,11},{12,13},{... | collective-permute-start | bytes 1572872 | tf_op jit(solution)/shard_map/ppermute | solution.py:227
  71.5 11.1 %collective-permute-start.3 = (bf16[512,512]{1,0:T(8,128)(2,1)S(1)}, bf16[512,512]{1,0:T(8,128)(2,1)S(1)}, u32[]{:S(2)}, u32[]{:S(2)}) collective-permute-start(bf16[512,512]{1,0:T(8,128)(2,1)S(1)} %get-tuple-element.12.low_hbm), channel_id=1, source_target_pairs={{1,0},{2,1},{3,2},{5,4},{6,5},{7,6},{9,8},{10,9},{11,10},{13,12},{... | collective-permute-start | bytes 1572872 | tf_op jit(solution)/shard_map/ppermute | solution.py:228

commit v4 on v3

--- a/solution.py
+++ b/solution.py
@@ -116,63 +116,62 @@
                 ).astype(out_ref.dtype)
 
 
-def stage2_kernel(
-    fan, cols_ref, mask_ref, q_ref, w_ref, left_hbm, low_hbm, high_hbm, right_hbm, mine_hbm,
-    others_hbm, out_ref, ext, f_all, sem,
-):
-    j = pl.program_id(0)
-    slab = pl.num_programs(0)
-    bs = out_ref.shape[1]
-    rows = out_ref.shape[0] // bs
-    group = f_all.shape[0] // fan
+def stage2_kernel(fan, turn, cols_ref, mask_ref, q_ref, w_ref, f_hbm, *refs):
+    if turn == 0:
+        *parts, out_hbm, ext, f_ref, made, f_sem, out_sem, sem = refs
+    else:
+        ext, _, out_hbm, f_ref, made, f_sem, out_sem = refs
+        parts = []
+    group, bs = f_hbm.shape[0], f_hbm.shape[2]
+    rows, slab = mask_ref.shape
     row_idx, col_idx = lax.axis_index("row"), lax.axis_index("col")
-
-    @pl.when(j == 0)
-    def _():
-        k = lax.rem(row_idx, fan)
-        copies = [pltpu.make_async_copy(mine_hbm, f_all.at[pl.ds(k * group, group)], sem.at[0])]
-        for step in range(1, fan):
-            at = lax.rem(k + step, fan) * group
-            copies.append(
-                pltpu.make_async_copy(
-                    others_hbm.at[step - 1], f_all.at[pl.ds(at, group)], sem.at[step]
-                )
-            )
-        at = 0
-        for piece, part in enumerate((left_hbm, low_hbm, high_hbm, right_hbm)):
-            copies.append(
-                pltpu.make_async_copy(
-                    part, ext.at[:, pl.ds(at, part.shape[1])], sem.at[fan + piece]
-                )
-            )
-            at += part.shape[1]
-        for copy in copies:
-            copy.start()
-        for copy in copies:
-            copy.wait()
-
-    col = col_idx * slab + j
+    base = lax.rem(row_idx + turn, fan) * group
     first = col_idx * slab - BAND
-    lhs = jnp.concatenate(
-        [
-            ext[:, pl.ds(pl.multiple_of((cols_ref[e, col] - first) * bs, bs), bs)]
-            for e in range(STENCIL)
-        ],
-        axis=1,
-    )
-    rhs = jnp.concatenate([f_all[j, e] for e in range(STENCIL)], axis=1)
-    spread = lax.dot_general(
-        lhs, rhs, (((1,), (1,)), ((), ())), preferred_element_type=jnp.float32
-    )
+
+    fetches = [
+        pltpu.make_async_copy(f_hbm.at[n], f_ref.at[n], f_sem.at[n]) for n in range(group)
+    ]
+    joins = []
+    at = 0
+    for piece, part in enumerate(parts):
+        to = ext.at[:, pl.ds(at, part.shape[1])]
+        joins.append(pltpu.make_async_copy(part, to, sem.at[piece]))
+        at += part.shape[1]
+    for copy in joins + fetches:
+        copy.start()
+    for copy in joins + fetches:
+        copy.wait()
+
     eye = lax.broadcasted_iota(jnp.int32, (bs, bs), 0) == lax.broadcasted_iota(
         jnp.int32, (bs, bs), 1
     )
-    for i in range(rows):
-        at = slice(i * bs, (i + 1) * bs)
-        keep = mask_ref[i, j].astype(jnp.float32)
-        on_main = (row_idx * rows + i == col).astype(jnp.float32)
-        noise = jnp.where(eye, q_ref[i : i + 1, :] * on_main, 0.0)
-        out_ref[at, :] = w_ref[at, :].astype(jnp.float32) * (spread[at] * keep) + noise
+    stores = []
+    for n in range(group):
+        j = base + n
+        col = col_idx * slab + j
+        to = pl.ds(pl.multiple_of(j * bs, bs), bs)
+        lhs = jnp.concatenate(
+            [
+                ext[:, pl.ds(pl.multiple_of((cols_ref[e, col] - first) * bs, bs), bs)]
+                for e in range(STENCIL)
+            ],
+            axis=1,
+        )
+        rhs = jnp.concatenate([f_ref[n, e] for e in range(STENCIL)], axis=1)
+        spread = lax.dot_general(
+            lhs, rhs, (((1,), (1,)), ((), ())), preferred_element_type=jnp.float32
+        )
+        for i in range(rows):
+            at = slice(i * bs, (i + 1) * bs)
+            keep = mask_ref[i, j].astype(jnp.float32)
+            on_main = (row_idx * rows + i == col).astype(jnp.float32)
+            noise = jnp.where(eye, q_ref[i : i + 1, :] * on_main, 0.0)
+            made[n, at, :] = w_ref[at, to].astype(jnp.float32) * (spread[at] * keep) + noise
+        store = pltpu.make_async_copy(made.at[n], out_hbm.at[:, to], out_sem.at[n])
+        store.start()
+        stores.append(store)
+    for store in stores:
+        store.wait()
 
 
 def forecast(
@@ -236,43 +235,44 @@
         compiler_params=pltpu.CompilerParams(vmem_limit_bytes=4 * 2**20),
         name="pick",
     )(*held)
-    others = []
-    for step in range(1, fan):
-        turn = [(r // fan * fan + (r + step) % fan, r) for r in range(rows)]
-        others.append(lax.ppermute(mine, "row", turn))
-    others = jnp.stack(others)
-
-    return pl.pallas_call(
-        functools.partial(stage2_kernel, fan),
-        out_shape=jax.ShapeDtypeStruct((tall, wide), jnp.float32),
-        grid=(slab,),
-        in_specs=[
-            smem,
-            smem,
-            pl.BlockSpec((block_rows, bs), lambda j: (0, 0)),
-            pl.BlockSpec((tall, bs), lambda j: (0, j)),
-        ]
-        + [hbm] * 6,
-        out_specs=pl.BlockSpec((tall, bs), lambda j: (0, j)),
-        scratch_shapes=[
-            pltpu.VMEM((tall, wide + 2 * halo), jnp.bfloat16),
-            pltpu.VMEM((slab, STENCIL, bs, bs), jnp.bfloat16),
-            pltpu.SemaphoreType.DMA((4 + fan,)),
-        ],
-        compiler_params=pltpu.CompilerParams(vmem_limit_bytes=16 * 2**20),
-        name="stage2",
-    )(
+    fixed = (
         cols_of,
         block_mask,
         disturbance_variances.reshape(block_rows, bs),
         localization_weights,
-        left,
-        low,
-        high,
-        right,
-        mine,
-        others,
-    )
+    )
+    out_type = jax.ShapeDtypeStruct((tall, wide), jnp.float32)
+    group = slab // fan
+    scratch = [
+        pltpu.VMEM((group, STENCIL, bs, bs), jnp.bfloat16),
+        pltpu.VMEM((group, tall, bs), jnp.float32),
+        pltpu.SemaphoreType.DMA((group,)),
+        pltpu.SemaphoreType.DMA((group,)),
+    ]
+    params = pltpu.CompilerParams(vmem_limit_bytes=20 * 2**20)
+    out, ext = pl.pallas_call(
+        functools.partial(stage2_kernel, fan, 0),
+        out_shape=(out_type, jax.ShapeDtypeStruct((tall, wide + 2 * halo), jnp.bfloat16)),
+        in_specs=[smem, smem, vmem, vmem] + [hbm] * 5,
+        out_specs=(pl.BlockSpec(memory_space=pltpu.HBM), vmem),
+        scratch_shapes=scratch + [pltpu.SemaphoreType.DMA((4,))],
+        compiler_params=params,
+        name="stage2",
+    )(*fixed, mine, left, low, high, right)
+    for turn in range(1, fan):
+        pairs = [(r // fan * fan + (r + turn) % fan, r) for r in range(rows)]
+        other = lax.ppermute(mine, "row", pairs)
+        out = pl.pallas_call(
+            functools.partial(stage2_kernel, fan, turn),
+            out_shape=out_type,
+            in_specs=[smem, smem, vmem, vmem, hbm, vmem, pl.BlockSpec(memory_space=pltpu.HBM)],
+            out_specs=pl.BlockSpec(memory_space=pltpu.HBM),
+            scratch_shapes=scratch,
+            input_output_aliases={6: 0},
+            compiler_params=params,
+            name="stage3",
+        )(*fixed, other, ext, out)
+    return out
 
 
 def solution(mesh):

time: 89.5 us -> 91 us (1.017)
  Pallas kernels: 9.29 us -> 10.8 us
    pallas_call x1 -> x2, Pallas kernels: 6.62 us -> 8.08 us  [the longest x1 4.21 us: forecast(): pl.pallas_call(functools.partial(stage2_kernel, fan, 0), out_shape=(out_t...]
  transfers between devices with their start and end apart: 8 -> 8, of which waited for: 3 -> 3; matrix products, arithmetic and copies ran while one was open for 0% -> 0% of each run, Pallas kernels for 3% -> 8%
where the time goes in v4:
time: 91 us; the launch traced here: 90.7 us
  starting transfers between devices  53 us (58%)
  waiting for transfers between devices  25.6 us (28%)
  Pallas kernels  10.8 us (12%)
  local copies, waits for them, and re-layouts  1.2 us (1%)
    ppermute x1, starting transfers between devices, forecast(): after = lax.ppermute(p_cov, 'row', down)  33.7 us
    ppermute x1, waiting for transfers between devices, forecast(): before = lax.ppermute(p_cov, 'row', up)  15.8 us
    ppermute x1, starting transfers between devices, forecast(): other = lax.ppermute(mine, 'row', pairs)  12 us
    ppermute x1, waiting for transfers between devices, forecast(): left = lax.ppermute(high, 'col', up)  5.35 us
    ppermute x1, waiting for transfers between devices, forecast(): right = lax.ppermute(low, 'col', down)  4.43 us
    pallas_call x1, Pallas kernels, forecast(): pl.pallas_call(functools.partial(stage2_kernel, fan, 0), out_shape=(out_t...  4.21 us
    pallas_call x1, Pallas kernels, forecast(): pl.pallas_call(functools.partial(stage2_kernel, fan, turn), out_shape=out...  3.87 us
    ppermute x3, starting transfers between devices, forecast(): held.append(lax.ppermute(held[source], ('row', 'col'), pairs))  2.72 us
  transfers between devices with their start and end apart: 8, of which 3 were waited for; matrix products, arithmetic and copies ran while one was open for 0% of the time, Pallas kernels for 8%

profile of v4, /device:TPU:6, one launch (start us, length us, event | category | flops | bytes accessed | tf_op | source)
XLA Modules:
  0.0 90.7 jit_solution(18095666143262202413)
XLA Ops:
  0.0 0.7 collective-permute-start
  0.7 0.7 collective-permute-start.2
  1.4 0.0 collective-permute-done.refs_1_
  1.5 1.3 %collective-permute-start.1 = (bf16[4,7,128,128]{3,2,1,0:T(8,128)(2,1)S(1)}, bf16[4,7,128,128]{3,2,1,0:T(8,128)(2,1)S(1)}, u32[]{:S(2)}, u32[]{:S(2)}) collective-permute-start(bf16[4,7,128,128]{3,2,1,0:T(8,128)(2,1)S(1)} %collective-permute-done.refs_1_), channel_id=1, source_target_pairs={{8,24},{20,28},{1,17},{29,21},{26,10},{6,14},{19,3},{15,7}} | collective-permute-start | bytes 2752520 | tf_op jit(solution)/shard_map/ppermute | solution.py:194
  2.8 1.9 %collective-permute-start.4 = (bf16[512,1024]{1,0:T(8,128)(2,1)}, bf16[512,1024]{1,0:T(8,128)(2,1)S(1)}, u32[]{:S(2)}, u32[]{:S(2)}) collective-permute-start(bf16[512,1024]{1,0:T(8,128)(2,1)} %p_hbm.1), channel_id=1, source_target_pairs={{0,4},{4,8},{8,12},{12,16},{16,20},{20,24},{24,28},{1,5},{5,9},{9,... | collective-permute-start | bytes 3145736 | tf_op jit(solution)/shard_map/ppermute | solution.py:190
  4.7 33.7 %collective-permute-start.5 = (bf16[512,1024]{1,0:T(8,128)(2,1)}, bf16[512,1024]{1,0:T(8,128)(2,1)S(1)}, u32[]{:S(2)}, u32[]{:S(2)}) collective-permute-start(bf16[512,1024]{1,0:T(8,128)(2,1)} %p_hbm.1), channel_id=1, source_target_pairs={{4,0},{8,4},{12,8},{16,12},{20,16},{24,20},{28,24},{5,1},{9,5},{13... | collective-permute-start | bytes 3145736 | tf_op jit(solution)/shard_map/ppermute | solution.py:191
  38.4 0.0 collective-permute-done.2.refs_3_
  38.4 0.0 collective-permute-done.1.refs_2_
  38.4 1.2 %copy-done.1 = bf16[4,7,128,128]{3,2,1,0:T(8,128)(2,1)S(1)} copy-done((bf16[4,7,128,128]{3,2,1,0:T(8,128)(2,1)S(1)}, bf16[4,7,128,128]{3,2,1,0:T(8,128)(2,1)}, u32[]{:S(2)}) %copy-start.1) | copy-done | bytes 917528
  39.6 0.2 pick.1.f_hbm
  39.8 12.0 %collective-permute-start.3 = (bf16[4,7,128,128]{3,2,1,0:T(8,128)(2,1)S(1)}, bf16[4,7,128,128]{3,2,1,0:T(8,128)(2,1)S(1)}, u32[]{:S(2)}, u32[]{:S(2)}) collective-permute-start(bf16[4,7,128,128]{3,2,1,0:T(8,128)(2,1)S(1)} %pick.1.f_hbm), channel_id=1, source_target_pairs={{4,0},{0,4},{12,8},{8,12},{20,16},{16,20},{28,24},{24,28},{5,1},{1... | collective-permute-start | bytes 2752520 | tf_op jit(solution)/shard_map/ppermute | solution.py:264
  51.9 0.3 fetch.1
  52.2 0.0 copy-start
  52.2 0.0 copy-start.5
  52.2 0.0 copy-start.6
  52.3 15.8 %collective-permute-done.4.before_hbm = bf16[512,1024]{1,0:T(8,128)(2,1)S(1)} collective-permute-done((bf16[512,1024]{1,0:T(8,128)(2,1)}, bf16[512,1024]{1,0:T(8,128)(2,1)S(1)}, u32[]{:S(2)}, u32[]{:S(2)}) %collective-permute-start.4) | collective-permute-done | bytes 1048608 | tf_op jit(solution)/shard_map/ppermute | solution.py:190
  68.0 2.1 %stage1.1 = (bf16[512,512]{1,0:T(8,128)(2,1)S(1)}, bf16[512,512]{1,0:T(8,128)(2,1)S(1)}) custom-call(s32[7,32]{1,0:T(8,128)S(1)} %bitcast.2, bf16[4,7,128,128]{3,2,1,0:T(8,128)(2,1)S(1)} %get-tuple-element.11.f_ref, bf16[512,1024]{1,0:T(8,128)(2,1)S(1)} %collective-permute-done.4.before_hbm, bf16[512,1024]{1,0:T(8,128)(2,1)S(1)} %get-tuple-element.12.own_hbm, ...), custom_call_target="tpu_custom_call" | custom-call | tf_op jit(solution)/shard_map/stage1/pallas_call | solution.py:212
  70.2 1.3 %collective-permute-start.6 = (bf16[512,512]{1,0:T(8,128)(2,1)S(1)}, bf16[512,512]{1,0:T(8,128)(2,1)S(1)}, u32[]{:S(2)}, u32[]{:S(2)}) collective-permute-start(bf16[512,512]{1,0:T(8,128)(2,1)S(1)} %get-tuple-element.13.refs_2_), channel_id=1, source_target_pairs={{0,1},{1,2},{2,3},{4,5},{5,6},{6,7},{8,9},{9,10},{10,11},{12,13},{... | collective-permute-start | bytes 1572872 | tf_op jit(solution)/shard_map/ppermute | solution.py:226
  71.5 1.3 %collective-permute-start.7 = (bf16[512,512]{1,0:T(8,128)(2,1)S(1)}, bf16[512,512]{1,0:T(8,128)(2,1)S(1)}, u32[]{:S(2)}, u32[]{:S(2)}) collective-permute-start(bf16[512,512]{1,0:T(8,128)(2,1)S(1)} %get-tuple-element.14.refs_1_), channel_id=1, source_target_pairs={{1,0},{2,1},{3,2},{5,4},{6,5},{7,6},{9,8},{10,9},{11,10},{13,12},{... | collective-permute-start | bytes 1572872 | tf_op jit(solution)/shard_map/ppermute | solution.py:227
  72.8 5.3 %collective-permute-done.6.refs_0_ = bf16[512,512]{1,0:T(8,128)(2,1)S(1)} collective-permute-done((bf16[512,512]{1,0:T(8,128)(2,1)S(1)}, bf16[512,512]{1,0:T(8,128)(2,1)S(1)}, u32[]{:S(2)}, u32[]{:S(2)}) %collective-permute-start.6) | collective-permute-done | bytes 524320 | tf_op jit(solution)/shard_map/ppermute | solution.py:226
  78.1 4.4 %collective-permute-done.7.refs_3_ = bf16[512,512]{1,0:T(8,128)(2,1)S(1)} collective-permute-done((bf16[512,512]{1,0:T(8,128)(2,1)S(1)}, bf16[512,512]{1,0:T(8,128)(2,1)S(1)}, u32[]{:S(2)}, u32[]{:S(2)}) %collective-permute-start.7) | collective-permute-done | bytes 524320 | tf_op jit(solution)/shard_map/ppermute | solution.py:227
  82.6 4.2 %stage2.1 = (f32[512,1024]{1,0:T(8,128)}, bf16[512,2048]{1,0:T(8,128)(2,1)S(1)}) custom-call(s32[7,32]{1,0:T(8,128)S(1)} %bitcast.3, s32[4,8]{1,0:T(4,128)S(1)} %copy-done.5, f32[4,128]{1,0:T(4,128)S(1)} %bitcast.5, bf16[512,1024]{1,0:T(8,128)(2,1)S(1)} %copy-done, bf16[4,7,128,128]{3,2,1,0:T(8,128)(2,1)S(1)} %pick.1.f_hbm, ...), custom_call_target="tpu_custom_call" | custom-call | tf_op jit(solution)/shard_map/stage2/pallas_call | solution.py:253
  86.8 0.0 collective-permute-done.3.f_hbm
  86.8 3.9 %stage3.1 = f32[512,1024]{1,0:T(8,128)} custom-call(s32[7,32]{1,0:T(8,128)S(1)} %bitcast.4, s32[4,8]{1,0:T(4,128)S(1)} %copy-done.5, f32[4,128]{1,0:T(4,128)S(1)} %bitcast.6, bf16[512,1024]{1,0:T(8,128)(2,1)S(1)} %copy-done, bf16[4,7,128,128]{3,2,1,0:T(8,128)(2,1)S(1)} %collective-permute-done.3.f_hbm, ...), custom_call_target="tpu_custom_call", output_to_operand_aliasing={{}: (6, {})} | custom-call | tf_op jit(solution)/shard_map/stage3/pallas_call | solution.py:265
  (11 shorter events, 0.0 us)
Async XLA Ops:
  0.0 1.4 %collective-permute-start = (bf16[4,7,128,128]{3,2,1,0:T(8,128)(2,1)}, bf16[4,7,128,128]{3,2,1,0:T(8,128)(2,1)S(1)}, u32[]{:S(2)}, u32[]{:S(2)}) collective-permute-start(bf16[4,7,128,128]{3,2,1,0:T(8,128)(2,1)} %f_hbm.1), channel_id=1, source_target_pairs={{0,8},{4,20},{9,1},{13,29},{18,26},{22,6},{27,19},{31,15}} | collective-permute-start | bytes 2752520 | tf_op jit(solution)/shard_map/ppermute | solution.py:194
  0.7 37.7 %collective-permute-start.2 = (bf16[4,7,128,128]{3,2,1,0:T(8,128)(2,1)}, bf16[4,7,128,128]{3,2,1,0:T(8,128)(2,1)S(1)}, u32[]{:S(2)}, u32[]{:S(2)}) collective-permute-start(bf16[4,7,128,128]{3,2,1,0:T(8,128)(2,1)} %f_hbm.1), channel_id=1, source_target_pairs={{0,16},{4,12},{9,25},{13,5},{18,2},{22,30},{27,11},{31,23}} | collective-permute-start | bytes 2752520 | tf_op jit(solution)/shard_map/ppermute | solution.py:194
  1.5 37.0 %collective-permute-start.1 = (bf16[4,7,128,128]{3,2,1,0:T(8,128)(2,1)S(1)}, bf16[4,7,128,128]{3,2,1,0:T(8,128)(2,1)S(1)}, u32[]{:S(2)}, u32[]{:S(2)}) collective-permute-start(bf16[4,7,128,128]{3,2,1,0:T(8,128)(2,1)S(1)} %collective-permute-done.refs_1_), channel_id=1, source_target_pairs={{8,24},{20,28},{1,17},{29,21},{26,10},{6,14},{19,3},{15,7}} | collective-permute-start | bytes 2752520 | tf_op jit(solution)/shard_map/ppermute | solution.py:194
  2.8 65.3 %collective-permute-start.4 = (bf16[512,1024]{1,0:T(8,128)(2,1)}, bf16[512,1024]{1,0:T(8,128)(2,1)S(1)}, u32[]{:S(2)}, u32[]{:S(2)}) collective-permute-start(bf16[512,1024]{1,0:T(8,128)(2,1)} %p_hbm.1), channel_id=1, source_target_pairs={{0,4},{4,8},{8,12},{12,16},{16,20},{20,24},{24,28},{1,5},{5,9},{9,... | collective-permute-start | bytes 3145736 | tf_op jit(solution)/shard_map/ppermute | solution.py:190
  4.7 63.3 %collective-permute-start.5 = (bf16[512,1024]{1,0:T(8,128)(2,1)}, bf16[512,1024]{1,0:T(8,128)(2,1)S(1)}, u32[]{:S(2)}, u32[]{:S(2)}) collective-permute-start(bf16[512,1024]{1,0:T(8,128)(2,1)} %p_hbm.1), channel_id=1, source_target_pairs={{4,0},{8,4},{12,8},{16,12},{20,16},{24,20},{28,24},{5,1},{9,5},{13... | collective-permute-start | bytes 3145736 | tf_op jit(solution)/shard_map/ppermute | solution.py:191
  38.4 1.2 %copy-start.1 = (bf16[4,7,128,128]{3,2,1,0:T(8,128)(2,1)S(1)}, bf16[4,7,128,128]{3,2,1,0:T(8,128)(2,1)}, u32[]{:S(2)}) copy-start(bf16[4,7,128,128]{3,2,1,0:T(8,128)(2,1)} %f_hbm.1) | copy-start | bytes 2752516
  39.6 12.3 %copy-start.2 = (bf16[4,7,128,128]{3,2,1,0:T(8,128)(2,1)S(1)}, bf16[4,7,128,128]{3,2,1,0:T(8,128)(2,1)}, u32[]{:S(2)}) copy-start(bf16[4,7,128,128]{3,2,1,0:T(8,128)(2,1)} %f_hbm.1) | copy-start | bytes 2752516
  39.6 12.3 %copy-start.3 = (bf16[512,1024]{1,0:T(8,128)(2,1)S(1)}, bf16[512,1024]{1,0:T(8,128)(2,1)}, u32[]{:S(2)}) copy-start(bf16[512,1024]{1,0:T(8,128)(2,1)} %p_hbm.1) | copy-start | bytes 3145732
  39.6 28.4 %copy-start.4 = (s32[32,7]{0,1:T(8,128)S(1)}, s32[32,7]{0,1:T(8,128)}, u32[]{:S(2)}) copy-start(s32[32,7]{0,1:T(8,128)} %param.8) | copy-start | bytes 2692
  39.8 47.0 %collective-permute-start.3 = (bf16[4,7,128,128]{3,2,1,0:T(8,128)(2,1)S(1)}, bf16[4,7,128,128]{3,2,1,0:T(8,128)(2,1)S(1)}, u32[]{:S(2)}, u32[]{:S(2)}) collective-permute-start(bf16[4,7,128,128]{3,2,1,0:T(8,128)(2,1)S(1)} %pick.1.f_hbm), channel_id=1, source_target_pairs={{4,0},{0,4},{12,8},{8,12},{20,16},{16,20},{28,24},{24,28},{5,1},{1... | collective-permute-start | bytes 2752520 | tf_op jit(solution)/shard_map/ppermute | solution.py:264
  52.2 30.4 %copy-start = (bf16[512,1024]{1,0:T(8,128)(2,1)S(1)}, bf16[512,1024]{1,0:T(8,128)(2,1)}, u32[]{:S(2)}) copy-start(bf16[512,1024]{1,0:T(8,128)(2,1)} %w_ref.3) | copy-start | bytes 3145732
  52.2 30.3 %copy-start.5 = (s32[4,8]{1,0:T(4,128)S(1)}, s32[4,8]{1,0:T(4,128)}, u32[]{:S(2)}) copy-start(s32[4,8]{1,0:T(4,128)} %mask_ref.3) | copy-start | bytes 388
  52.2 30.3 %copy-start.6 = (f32[512]{0:T(512)S(1)}, f32[512]{0:T(512)}, u32[]{:S(2)}) copy-start(f32[512]{0:T(512)} %param.11) | copy-start | bytes 6148
  70.2 8.0 %collective-permute-start.6 = (bf16[512,512]{1,0:T(8,128)(2,1)S(1)}, bf16[512,512]{1,0:T(8,128)(2,1)S(1)}, u32[]{:S(2)}, u32[]{:S(2)}) collective-permute-start(bf16[512,512]{1,0:T(8,128)(2,1)S(1)} %get-tuple-element.13.refs_2_), channel_id=1, source_target_pairs={{0,1},{1,2},{2,3},{4,5},{5,6},{6,7},{8,9},{9,10},{10,11},{12,13},{... | collective-permute-start | bytes 1572872 | tf_op jit(solution)/shard_map/ppermute | solution.py:226
  71.5 11.1 %collective-permute-start.7 = (bf16[512,512]{1,0:T(8,128)(2,1)S(1)}, bf16[512,512]{1,0:T(8,128)(2,1)S(1)}, u32[]{:S(2)}, u32[]{:S(2)}) collective-permute-start(bf16[512,512]{1,0:T(8,128)(2,1)S(1)} %get-tuple-element.14.refs_1_), channel_id=1, source_target_pairs={{1,0},{2,1},{3,2},{5,4},{6,5},{7,6},{9,8},{10,9},{11,10},{13,12},{... | collective-permute-start | bytes 1572872 | tf_op jit(solution)/shard_map/ppermute | solution.py:227

commit v5 on v4

--- a/solution.py
+++ b/solution.py
@@ -71,10 +71,11 @@
             copy.wait()
 
 
-def fetch_kernel(p_hbm, f_hbm, p_ref, f_ref, sem):
+def fetch_kernel(*refs):
+    *ends, sem = refs
+    count = len(ends) // 2
     copies = [
-        pltpu.make_async_copy(p_hbm, p_ref, sem.at[0]),
-        pltpu.make_async_copy(f_hbm, f_ref, sem.at[1]),
+        pltpu.make_async_copy(ends[n], ends[count + n], sem.at[n]) for n in range(count)
     ]
     for copy in copies:
         copy.start()
@@ -116,30 +117,27 @@
                 ).astype(out_ref.dtype)
 
 
-def stage2_kernel(fan, turn, cols_ref, mask_ref, q_ref, w_ref, f_hbm, *refs):
+def stage2_kernel(fan, turn, cols_ref, mask_ref, q_ref, w_ref, f_ref, *refs):
     if turn == 0:
-        *parts, out_hbm, ext, f_ref, made, f_sem, out_sem, sem = refs
+        *parts, out_hbm, ext, made, out_sem, sem = refs
     else:
-        ext, _, out_hbm, f_ref, made, f_sem, out_sem = refs
+        ext, _, out_hbm, made, out_sem = refs
         parts = []
-    group, bs = f_hbm.shape[0], f_hbm.shape[2]
+    group, bs = f_ref.shape[0], f_ref.shape[2]
     rows, slab = mask_ref.shape
     row_idx, col_idx = lax.axis_index("row"), lax.axis_index("col")
     base = lax.rem(row_idx + turn, fan) * group
     first = col_idx * slab - BAND
 
-    fetches = [
-        pltpu.make_async_copy(f_hbm.at[n], f_ref.at[n], f_sem.at[n]) for n in range(group)
-    ]
     joins = []
     at = 0
     for piece, part in enumerate(parts):
         to = ext.at[:, pl.ds(at, part.shape[1])]
         joins.append(pltpu.make_async_copy(part, to, sem.at[piece]))
         at += part.shape[1]
-    for copy in joins + fetches:
+    for copy in joins:
         copy.start()
-    for copy in joins + fetches:
+    for copy in joins:
         copy.wait()
 
     eye = lax.broadcasted_iota(jnp.int32, (bs, bs), 0) == lax.broadcasted_iota(
@@ -196,18 +194,16 @@
     smem = pl.BlockSpec(memory_space=pltpu.SMEM)
     hbm = pl.BlockSpec(memory_space=ANY)
     vmem = pl.BlockSpec(memory_space=pltpu.VMEM)
-    p_near, f_near = pl.pallas_call(
+    wanted = (p_cov, f_blocks, cols_of)
+    p_near, f_near, cols_of = pl.pallas_call(
         fetch_kernel,
-        out_shape=(
-            jax.ShapeDtypeStruct(p_cov.shape, p_cov.dtype),
-            jax.ShapeDtypeStruct(f_blocks.shape, f_blocks.dtype),
-        ),
-        in_specs=[hbm, hbm],
-        out_specs=(vmem, vmem),
-        scratch_shapes=[pltpu.SemaphoreType.DMA((2,))],
+        out_shape=tuple(jax.ShapeDtypeStruct(x.shape, x.dtype) for x in wanted),
+        in_specs=[hbm] * len(wanted),
+        out_specs=(vmem,) * len(wanted),
+        scratch_shapes=[pltpu.SemaphoreType.DMA((len(wanted),))],
         compiler_params=pltpu.CompilerParams(vmem_limit_bytes=8 * 2**20),
         name="fetch",
-    )(p_cov, f_blocks)
+    )(*wanted)
     half = jax.ShapeDtypeStruct((tall, halo), jnp.bfloat16)
     low, high = pl.pallas_call(
         stage1_kernel,
@@ -244,16 +240,14 @@
     out_type = jax.ShapeDtypeStruct((tall, wide), jnp.float32)
     group = slab // fan
     scratch = [
-        pltpu.VMEM((group, STENCIL, bs, bs), jnp.bfloat16),
         pltpu.VMEM((group, tall, bs), jnp.float32),
-        pltpu.SemaphoreType.DMA((group,)),
         pltpu.SemaphoreType.DMA((group,)),
     ]
     params = pltpu.CompilerParams(vmem_limit_bytes=20 * 2**20)
     out, ext = pl.pallas_call(
         functools.partial(stage2_kernel, fan, 0),
         out_shape=(out_type, jax.ShapeDtypeStruct((tall, wide + 2 * halo), jnp.bfloat16)),
-        in_specs=[smem, smem, vmem, vmem] + [hbm] * 5,
+        in_specs=[smem, smem, vmem, vmem, vmem] + [hbm] * 4,
         out_specs=(pl.BlockSpec(memory_space=pltpu.HBM), vmem),
         scratch_shapes=scratch + [pltpu.SemaphoreType.DMA((4,))],
         compiler_params=params,
@@ -265,7 +259,7 @@
         out = pl.pallas_call(
             functools.partial(stage2_kernel, fan, turn),
             out_shape=out_type,
-            in_specs=[smem, smem, vmem, vmem, hbm, vmem, pl.BlockSpec(memory_space=pltpu.HBM)],
+            in_specs=[smem, smem, vmem, vmem, vmem, vmem, pl.BlockSpec(memory_space=pltpu.HBM)],
             out_specs=pl.BlockSpec(memory_space=pltpu.HBM),
             scratch_shapes=scratch,
             input_output_aliases={6: 0},

time: 91 us -> 88.5 us (0.973)
  Pallas kernels: 10.8 us -> 8.33 us
    pallas_call x1, Pallas kernels: 3.87 us -> 2.64 us  [forecast(): pl.pallas_call(functools.partial(stage2_kernel, fan, turn), out_shape=out...]
    pallas_call x1, Pallas kernels: 4.21 us -> 3.01 us  [forecast(): pl.pallas_call(functools.partial(stage2_kernel, fan, 0), out_shape=(out_t...]
  transfers between devices with their start and end apart: 8 -> 8, of which waited for: 3 -> 3; matrix products, arithmetic and copies ran while one was open for 0% -> 0% of each run, Pallas kernels for 8% -> 6%
where the time goes in v5:
time: 88.5 us; the launch traced here: 88.2 us
  starting transfers between devices  53 us (60%)
  waiting for transfers between devices  25.5 us (29%)
  Pallas kernels  8.33 us (9%)
  local copies, waits for them, and re-layouts  1.2 us (1%)
    ppermute x1, starting transfers between devices, forecast(): after = lax.ppermute(p_cov, 'row', down)  33.7 us
    ppermute x1, waiting for transfers between devices, forecast(): before = lax.ppermute(p_cov, 'row', up)  15.8 us
    ppermute x1, starting transfers between devices, forecast(): other = lax.ppermute(mine, 'row', pairs)  12 us
    ppermute x1, waiting for transfers between devices, forecast(): left = lax.ppermute(high, 'col', up)  5.35 us
    ppermute x1, waiting for transfers between devices, forecast(): right = lax.ppermute(low, 'col', down)  4.43 us
    pallas_call x1, Pallas kernels, forecast(): pl.pallas_call(functools.partial(stage2_kernel, fan, 0), out_shape=(out_t...  3.01 us
    ppermute x3, starting transfers between devices, forecast(): held.append(lax.ppermute(held[source], ('row', 'col'), pairs))  2.72 us
    pallas_call x1, Pallas kernels, forecast(): pl.pallas_call(functools.partial(stage2_kernel, fan, turn), out_shape=out...  2.64 us
  transfers between devices with their start and end apart: 8, of which 3 were waited for; matrix products, arithmetic and copies ran while one was open for 0% of the time, Pallas kernels for 6%

profile of v5, /device:TPU:6, one launch (start us, length us, event | category | flops | bytes accessed | tf_op | source)
XLA Modules:
  0.0 88.2 jit_solution(8248203737424646098)
XLA Ops:
  0.0 0.7 collective-permute-start
  0.7 0.7 collective-permute-start.2
  1.4 0.0 collective-permute-done.refs_1_
  1.5 1.3 %collective-permute-start.1 = (bf16[4,7,128,128]{3,2,1,0:T(8,128)(2,1)S(1)}, bf16[4,7,128,128]{3,2,1,0:T(8,128)(2,1)S(1)}, u32[]{:S(2)}, u32[]{:S(2)}) collective-permute-start(bf16[4,7,128,128]{3,2,1,0:T(8,128)(2,1)S(1)} %collective-permute-done.refs_1_), channel_id=1, source_target_pairs={{8,24},{20,28},{1,17},{29,21},{26,10},{6,14},{19,3},{15,7}} | collective-permute-start | bytes 2752520 | tf_op jit(solution)/shard_map/ppermute | solution.py:192
  2.8 1.9 %collective-permute-start.4 = (bf16[512,1024]{1,0:T(8,128)(2,1)}, bf16[512,1024]{1,0:T(8,128)(2,1)S(1)}, u32[]{:S(2)}, u32[]{:S(2)}) collective-permute-start(bf16[512,1024]{1,0:T(8,128)(2,1)} %refs_0_.2), channel_id=1, source_target_pairs={{0,4},{4,8},{8,12},{12,16},{16,20},{20,24},{24,28},{1,5},{5,9},{9,... | collective-permute-start | bytes 3145736 | tf_op jit(solution)/shard_map/ppermute | solution.py:188
  4.7 33.7 %collective-permute-start.5 = (bf16[512,1024]{1,0:T(8,128)(2,1)}, bf16[512,1024]{1,0:T(8,128)(2,1)S(1)}, u32[]{:S(2)}, u32[]{:S(2)}) collective-permute-start(bf16[512,1024]{1,0:T(8,128)(2,1)} %refs_0_.2), channel_id=1, source_target_pairs={{4,0},{8,4},{12,8},{16,12},{20,16},{24,20},{28,24},{5,1},{9,5},{13... | collective-permute-start | bytes 3145736 | tf_op jit(solution)/shard_map/ppermute | solution.py:189
  38.4 0.0 collective-permute-done.2.refs_3_
  38.4 0.0 collective-permute-done.1.refs_2_
  38.4 1.2 %copy-done.1 = bf16[4,7,128,128]{3,2,1,0:T(8,128)(2,1)S(1)} copy-done((bf16[4,7,128,128]{3,2,1,0:T(8,128)(2,1)S(1)}, bf16[4,7,128,128]{3,2,1,0:T(8,128)(2,1)}, u32[]{:S(2)}) %copy-start.1) | copy-done | bytes 917528
  39.6 0.2 pick.1.f_ref
  39.8 12.0 %collective-permute-start.3 = (bf16[4,7,128,128]{3,2,1,0:T(8,128)(2,1)S(1)}, bf16[4,7,128,128]{3,2,1,0:T(8,128)(2,1)S(1)}, u32[]{:S(2)}, u32[]{:S(2)}) collective-permute-start(bf16[4,7,128,128]{3,2,1,0:T(8,128)(2,1)S(1)} %pick.1.f_ref), channel_id=1, source_target_pairs={{4,0},{0,4},{12,8},{8,12},{20,16},{16,20},{28,24},{24,28},{5,1},{1... | collective-permute-start | bytes 2752520 | tf_op jit(solution)/shard_map/ppermute | solution.py:258
  51.9 0.3 fetch.1
  52.2 0.0 copy-start
  52.2 0.0 copy-start.4
  52.3 0.0 copy-start.5
  52.3 15.8 %collective-permute-done.4.before_hbm = bf16[512,1024]{1,0:T(8,128)(2,1)S(1)} collective-permute-done((bf16[512,1024]{1,0:T(8,128)(2,1)}, bf16[512,1024]{1,0:T(8,128)(2,1)S(1)}, u32[]{:S(2)}, u32[]{:S(2)}) %collective-permute-start.4) | collective-permute-done | bytes 1048608 | tf_op jit(solution)/shard_map/ppermute | solution.py:188
  68.0 2.1 %stage1.1 = (bf16[512,512]{1,0:T(8,128)(2,1)S(1)}, bf16[512,512]{1,0:T(8,128)(2,1)S(1)}) custom-call(s32[7,32]{1,0:T(8,128)S(1)} %get-tuple-element.12.cols_ref, bf16[4,7,128,128]{3,2,1,0:T(8,128)(2,1)S(1)} %get-tuple-element.13.f_ref, bf16[512,1024]{1,0:T(8,128)(2,1)S(1)} %collective-permute-done.4.before_hbm, ...), custom_call_target="tpu_custom_call" | custom-call | tf_op jit(solution)/shard_map/stage1/pallas_call | solution.py:208
  70.2 1.3 %collective-permute-start.6 = (bf16[512,512]{1,0:T(8,128)(2,1)S(1)}, bf16[512,512]{1,0:T(8,128)(2,1)S(1)}, u32[]{:S(2)}, u32[]{:S(2)}) collective-permute-start(bf16[512,512]{1,0:T(8,128)(2,1)S(1)} %get-tuple-element.15.refs_2_), channel_id=1, source_target_pairs={{0,1},{1,2},{2,3},{4,5},{5,6},{6,7},{8,9},{9,10},{10,11},{12,13},{... | collective-permute-start | bytes 1572872 | tf_op jit(solution)/shard_map/ppermute | solution.py:222
  71.5 1.3 %collective-permute-start.7 = (bf16[512,512]{1,0:T(8,128)(2,1)S(1)}, bf16[512,512]{1,0:T(8,128)(2,1)S(1)}, u32[]{:S(2)}, u32[]{:S(2)}) collective-permute-start(bf16[512,512]{1,0:T(8,128)(2,1)S(1)} %get-tuple-element.16.refs_1_), channel_id=1, source_target_pairs={{1,0},{2,1},{3,2},{5,4},{6,5},{7,6},{9,8},{10,9},{11,10},{13,12},{... | collective-permute-start | bytes 1572872 | tf_op jit(solution)/shard_map/ppermute | solution.py:223
  72.8 5.3 %collective-permute-done.6.refs_0_ = bf16[512,512]{1,0:T(8,128)(2,1)S(1)} collective-permute-done((bf16[512,512]{1,0:T(8,128)(2,1)S(1)}, bf16[512,512]{1,0:T(8,128)(2,1)S(1)}, u32[]{:S(2)}, u32[]{:S(2)}) %collective-permute-start.6) | collective-permute-done | bytes 524320 | tf_op jit(solution)/shard_map/ppermute | solution.py:222
  78.1 4.4 %collective-permute-done.7.refs_3_ = bf16[512,512]{1,0:T(8,128)(2,1)S(1)} collective-permute-done((bf16[512,512]{1,0:T(8,128)(2,1)S(1)}, bf16[512,512]{1,0:T(8,128)(2,1)S(1)}, u32[]{:S(2)}, u32[]{:S(2)}) %collective-permute-start.7) | collective-permute-done | bytes 524320 | tf_op jit(solution)/shard_map/ppermute | solution.py:223
  82.6 3.0 %stage2.1 = (f32[512,1024]{1,0:T(8,128)}, bf16[512,2048]{1,0:T(8,128)(2,1)S(1)}) custom-call(s32[7,32]{1,0:T(8,128)S(1)} %get-tuple-element.12.cols_ref, s32[4,8]{1,0:T(4,128)S(1)} %copy-done.4, f32[4,128]{1,0:T(4,128)S(1)} %bitcast.2, bf16[512,1024]{1,0:T(8,128)(2,1)S(1)} %copy-done, bf16[4,7,128,128]{3,2,1,0:T(8,128)(2,1)S(1)} %pick.1.f_ref, ...), custom_call_target="tpu_custom_call" | custom-call | tf_op jit(solution)/shard_map/stage2/pallas_call | solution.py:247
  85.6 0.0 collective-permute-done.3.f_ref
  85.6 2.6 %stage3.1 = f32[512,1024]{1,0:T(8,128)} custom-call(s32[7,32]{1,0:T(8,128)S(1)} %get-tuple-element.12.cols_ref, s32[4,8]{1,0:T(4,128)S(1)} %copy-done.4, f32[4,128]{1,0:T(4,128)S(1)} %bitcast.3, bf16[512,1024]{1,0:T(8,128)(2,1)S(1)} %copy-done, bf16[4,7,128,128]{3,2,1,0:T(8,128)(2,1)S(1)} %collective-permute-done.3.f_ref, ...), custom_call_target="tpu_custom_call", output_to_operand_aliasing={{}: (6, {})} | custom-call | tf_op jit(solution)/shard_map/stage3/pallas_call | solution.py:259
  (11 shorter events, 0.0 us)
Async XLA Ops:
  0.0 1.4 %collective-permute-start = (bf16[4,7,128,128]{3,2,1,0:T(8,128)(2,1)}, bf16[4,7,128,128]{3,2,1,0:T(8,128)(2,1)S(1)}, u32[]{:S(2)}, u32[]{:S(2)}) collective-permute-start(bf16[4,7,128,128]{3,2,1,0:T(8,128)(2,1)} %refs_0_.3), channel_id=1, source_target_pairs={{0,8},{4,20},{9,1},{13,29},{18,26},{22,6},{27,19},{31,15}} | collective-permute-start | bytes 2752520 | tf_op jit(solution)/shard_map/ppermute | solution.py:192
  0.7 37.7 %collective-permute-start.2 = (bf16[4,7,128,128]{3,2,1,0:T(8,128)(2,1)}, bf16[4,7,128,128]{3,2,1,0:T(8,128)(2,1)S(1)}, u32[]{:S(2)}, u32[]{:S(2)}) collective-permute-start(bf16[4,7,128,128]{3,2,1,0:T(8,128)(2,1)} %refs_0_.3), channel_id=1, source_target_pairs={{0,16},{4,12},{9,25},{13,5},{18,2},{22,30},{27,11},{31,23}} | collective-permute-start | bytes 2752520 | tf_op jit(solution)/shard_map/ppermute | solution.py:192
  1.5 37.0 %collective-permute-start.1 = (bf16[4,7,128,128]{3,2,1,0:T(8,128)(2,1)S(1)}, bf16[4,7,128,128]{3,2,1,0:T(8,128)(2,1)S(1)}, u32[]{:S(2)}, u32[]{:S(2)}) collective-permute-start(bf16[4,7,128,128]{3,2,1,0:T(8,128)(2,1)S(1)} %collective-permute-done.refs_1_), channel_id=1, source_target_pairs={{8,24},{20,28},{1,17},{29,21},{26,10},{6,14},{19,3},{15,7}} | collective-permute-start | bytes 2752520 | tf_op jit(solution)/shard_map/ppermute | solution.py:192
  2.8 65.3 %collective-permute-start.4 = (bf16[512,1024]{1,0:T(8,128)(2,1)}, bf16[512,1024]{1,0:T(8,128)(2,1)S(1)}, u32[]{:S(2)}, u32[]{:S(2)}) collective-permute-start(bf16[512,1024]{1,0:T(8,128)(2,1)} %refs_0_.2), channel_id=1, source_target_pairs={{0,4},{4,8},{8,12},{12,16},{16,20},{20,24},{24,28},{1,5},{5,9},{9,... | collective-permute-start | bytes 3145736 | tf_op jit(solution)/shard_map/ppermute | solution.py:188
  4.7 63.3 %collective-permute-start.5 = (bf16[512,1024]{1,0:T(8,128)(2,1)}, bf16[512,1024]{1,0:T(8,128)(2,1)S(1)}, u32[]{:S(2)}, u32[]{:S(2)}) collective-permute-start(bf16[512,1024]{1,0:T(8,128)(2,1)} %refs_0_.2), channel_id=1, source_target_pairs={{4,0},{8,4},{12,8},{16,12},{20,16},{24,20},{28,24},{5,1},{9,5},{13... | collective-permute-start | bytes 3145736 | tf_op jit(solution)/shard_map/ppermute | solution.py:189
  38.4 1.2 %copy-start.1 = (bf16[4,7,128,128]{3,2,1,0:T(8,128)(2,1)S(1)}, bf16[4,7,128,128]{3,2,1,0:T(8,128)(2,1)}, u32[]{:S(2)}) copy-start(bf16[4,7,128,128]{3,2,1,0:T(8,128)(2,1)} %refs_0_.3) | copy-start | bytes 2752516
  39.6 12.3 %copy-start.2 = (bf16[4,7,128,128]{3,2,1,0:T(8,128)(2,1)S(1)}, bf16[4,7,128,128]{3,2,1,0:T(8,128)(2,1)}, u32[]{:S(2)}) copy-start(bf16[4,7,128,128]{3,2,1,0:T(8,128)(2,1)} %refs_0_.3) | copy-start | bytes 2752516
  39.6 12.3 %copy-start.3 = (bf16[512,1024]{1,0:T(8,128)(2,1)S(1)}, bf16[512,1024]{1,0:T(8,128)(2,1)}, u32[]{:S(2)}) copy-start(bf16[512,1024]{1,0:T(8,128)(2,1)} %refs_0_.2) | copy-start | bytes 3145732
  39.6 12.3 %copy-start.6 = (s32[32,7]{0,1:T(8,128)S(1)}, s32[32,7]{0,1:T(8,128)}, u32[]{:S(2)}) copy-start(s32[32,7]{0,1:T(8,128)} %param.8) | copy-start | bytes 2692
  39.8 45.8 %collective-permute-start.3 = (bf16[4,7,128,128]{3,2,1,0:T(8,128)(2,1)S(1)}, bf16[4,7,128,128]{3,2,1,0:T(8,128)(2,1)S(1)}, u32[]{:S(2)}, u32[]{:S(2)}) collective-permute-start(bf16[4,7,128,128]{3,2,1,0:T(8,128)(2,1)S(1)} %pick.1.f_ref), channel_id=1, source_target_pairs={{4,0},{0,4},{12,8},{8,12},{20,16},{16,20},{28,24},{24,28},{5,1},{1... | collective-permute-start | bytes 2752520 | tf_op jit(solution)/shard_map/ppermute | solution.py:258
  52.2 30.3 %copy-start = (bf16[512,1024]{1,0:T(8,128)(2,1)S(1)}, bf16[512,1024]{1,0:T(8,128)(2,1)}, u32[]{:S(2)}) copy-start(bf16[512,1024]{1,0:T(8,128)(2,1)} %w_ref.3) | copy-start | bytes 3145732
  52.2 30.3 %copy-start.4 = (s32[4,8]{1,0:T(4,128)S(1)}, s32[4,8]{1,0:T(4,128)}, u32[]{:S(2)}) copy-start(s32[4,8]{1,0:T(4,128)} %mask_ref.3) | copy-start | bytes 388
  52.3 30.3 %copy-start.5 = (f32[512]{0:T(512)S(1)}, f32[512]{0:T(512)}, u32[]{:S(2)}) copy-start(f32[512]{0:T(512)} %param.11) | copy-start | bytes 6148
  70.2 8.0 %collective-permute-start.6 = (bf16[512,512]{1,0:T(8,128)(2,1)S(1)}, bf16[512,512]{1,0:T(8,128)(2,1)S(1)}, u32[]{:S(2)}, u32[]{:S(2)}) collective-permute-start(bf16[512,512]{1,0:T(8,128)(2,1)S(1)} %get-tuple-element.15.refs_2_), channel_id=1, source_target_pairs={{0,1},{1,2},{2,3},{4,5},{5,6},{6,7},{8,9},{9,10},{10,11},{12,13},{... | collective-permute-start | bytes 1572872 | tf_op jit(solution)/shard_map/ppermute | solution.py:222
  71.5 11.1 %collective-permute-start.7 = (bf16[512,512]{1,0:T(8,128)(2,1)S(1)}, bf16[512,512]{1,0:T(8,128)(2,1)S(1)}, u32[]{:S(2)}, u32[]{:S(2)}) collective-permute-start(bf16[512,512]{1,0:T(8,128)(2,1)S(1)} %get-tuple-element.16.refs_1_), channel_id=1, source_target_pairs={{1,0},{2,1},{3,2},{5,4},{6,5},{7,6},{9,8},{10,9},{11,10},{13,12},{... | collective-permute-start | bytes 1572872 | tf_op jit(solution)/shard_map/ppermute | solution.py:223

commit v6 on v5

--- a/solution.py
+++ b/solution.py
@@ -71,11 +71,13 @@
             copy.wait()
 
 
-def fetch_kernel(*refs):
-    *ends, sem = refs
-    count = len(ends) // 2
+def fetch_kernel(p_hbm, f_hbm, cols_hbm, top_ref, bottom_ref, f_ref, cols_ref, sem):
+    half = top_ref.shape[0]
     copies = [
-        pltpu.make_async_copy(ends[n], ends[count + n], sem.at[n]) for n in range(count)
+        pltpu.make_async_copy(p_hbm.at[:half], top_ref, sem.at[0]),
+        pltpu.make_async_copy(p_hbm.at[half:], bottom_ref, sem.at[1]),
+        pltpu.make_async_copy(f_hbm, f_ref, sem.at[2]),
+        pltpu.make_async_copy(cols_hbm, cols_ref, sem.at[3]),
     ]
     for copy in copies:
         copy.start()
@@ -83,22 +85,40 @@
         copy.wait()
 
 
-def stage1_kernel(
-    cols_ref, f_ref, before_hbm, own_hbm, after_hbm, low_ref, high_ref, ext, sem
-):
+def stage1_kernel(bent, cols_ref, f_ref, top_hbm, bottom_hbm, before_hbm, after_hbm, *refs):
+    *halves, low_ref, high_ref, ext, sem = refs
     rows, bs = f_ref.shape[0], f_ref.shape[2]
     half = low_ref.shape[1]
-    first = lax.axis_index("row") * rows
-    halo, tall = before_hbm.shape[0], own_hbm.shape[0]
-    copies = [
-        pltpu.make_async_copy(before_hbm, ext.at[pl.ds(0, halo)], sem.at[0]),
-        pltpu.make_async_copy(own_hbm, ext.at[pl.ds(halo, tall)], sem.at[1]),
-        pltpu.make_async_copy(after_hbm, ext.at[pl.ds(halo + tall, halo)], sem.at[2]),
-    ]
-    for copy in copies:
-        copy.start()
-    for copy in copies:
-        copy.wait()
+    row_idx = lax.axis_index("row")
+    first = row_idx * rows
+    halo, part = before_hbm.shape[0], top_hbm.shape[0]
+
+    def copies(at, pieces, sems):
+        for piece, n in zip(pieces, sems):
+            yield pltpu.make_async_copy(piece, ext.at[pl.ds(at, piece.shape[0])], sem.at[n])
+            at += piece.shape[0]
+
+    def all_copies(act):
+        for copy in copies(halo, (top_hbm, bottom_hbm), (0, 1)):
+            act(copy)
+        for at, whole, device, n in ((0, before_hbm, 0, 2), (halo + 2 * part, after_hbm, 1, 4)):
+            if not halves:
+                for copy in copies(at, (whole,), (n,)):
+                    act(copy)
+                continue
+
+            @pl.when(row_idx != bent[device])
+            def _():
+                for copy in copies(at, (whole,), (n,)):
+                    act(copy)
+
+            @pl.when(row_idx == bent[device])
+            def _():
+                for copy in copies(at, halves, (n, n + 1)):
+                    act(copy)
+
+    all_copies(lambda copy: copy.start())
+    all_copies(lambda copy: copy.wait())
     tile = min(256, half)
     for i in range(rows):
         lhs = jnp.concatenate([f_ref[i, e] for e in range(STENCIL)], axis=1)
@@ -184,39 +204,56 @@
     assert tall == halo and wide == 2 * halo
     cols_of = stencil_cols.T
 
+    smem = pl.BlockSpec(memory_space=pltpu.SMEM)
+    hbm = pl.BlockSpec(memory_space=ANY)
+    vmem = pl.BlockSpec(memory_space=pltpu.VMEM)
+    wanted = (
+        jax.ShapeDtypeStruct((tall // 2, wide), p_cov.dtype),
+        jax.ShapeDtypeStruct((tall // 2, wide), p_cov.dtype),
+        jax.ShapeDtypeStruct(f_blocks.shape, f_blocks.dtype),
+        jax.ShapeDtypeStruct(cols_of.shape, cols_of.dtype),
+    )
+    top, bottom, f_near, cols_of = pl.pallas_call(
+        fetch_kernel,
+        out_shape=wanted,
+        in_specs=[hbm] * 3,
+        out_specs=(vmem,) * 4,
+        scratch_shapes=[pltpu.SemaphoreType.DMA((4,))],
+        compiler_params=pltpu.CompilerParams(vmem_limit_bytes=8 * 2**20),
+        name="fetch",
+    )(p_cov, f_blocks, cols_of)
+
     up, down = up_down(rows)
+    bent, halves = (rows // 2, rows // 2 - 1), ()
+    if (cols, fan) == (4, 2):
+        lower, upper = bent
+        across = [(upper, lower), (lower, upper)]
+        up, down = (
+            [pair for pair in pairs if pair not in across] for pairs in (up, down)
+        )
+        straight = lax.ppermute(top, "row", across)
+        turn = lax.ppermute(bottom, "row", [(upper, rows - 1), (lower, 0)])
+        turned = lax.ppermute(turn, "row", [(rows - 1, lower), (0, upper)])
+        halves = (straight, turned)
     before = lax.ppermute(p_cov, "row", up)
     after = lax.ppermute(p_cov, "row", down)
     held = [f_blocks]
     for source, pairs in group_plan(rows, cols):
         held.append(lax.ppermute(held[source], ("row", "col"), pairs))
 
-    smem = pl.BlockSpec(memory_space=pltpu.SMEM)
-    hbm = pl.BlockSpec(memory_space=ANY)
-    vmem = pl.BlockSpec(memory_space=pltpu.VMEM)
-    wanted = (p_cov, f_blocks, cols_of)
-    p_near, f_near, cols_of = pl.pallas_call(
-        fetch_kernel,
-        out_shape=tuple(jax.ShapeDtypeStruct(x.shape, x.dtype) for x in wanted),
-        in_specs=[hbm] * len(wanted),
-        out_specs=(vmem,) * len(wanted),
-        scratch_shapes=[pltpu.SemaphoreType.DMA((len(wanted),))],
-        compiler_params=pltpu.CompilerParams(vmem_limit_bytes=8 * 2**20),
-        name="fetch",
-    )(*wanted)
     half = jax.ShapeDtypeStruct((tall, halo), jnp.bfloat16)
     low, high = pl.pallas_call(
-        stage1_kernel,
+        functools.partial(stage1_kernel, bent),
         out_shape=(half, half),
-        in_specs=[smem, vmem, hbm, hbm, hbm],
+        in_specs=[smem, vmem] + [hbm] * (4 + len(halves)),
         out_specs=(vmem, vmem),
         scratch_shapes=[
             pltpu.VMEM((tall + 2 * halo, wide), jnp.bfloat16),
-            pltpu.SemaphoreType.DMA((3,)),
+            pltpu.SemaphoreType.DMA((6,)),
         ],
         compiler_params=pltpu.CompilerParams(vmem_limit_bytes=16 * 2**20),
         name="stage1",
-    )(cols_of, f_near, before, p_near, after)
+    )(cols_of, f_near, top, bottom, before, after, *halves)
 
     up, down = up_down(cols)
     left = lax.ppermute(high, "col", up)

time: 88.5 us -> 81.9 us (0.925)
  the two profiles are of different devices: /device:TPU:6 before, /device:TPU:29 now
where the time goes in v6:
time: 81.9 us; the launch traced here: 81.5 us
  starting transfers between devices  54.6 us (67%)
  waiting for transfers between devices  15.1 us (18%)
  Pallas kernels  8.44 us (10%)
  local copies, waits for them, and re-layouts  3.09 us (4%)
    ppermute x1, starting transfers between devices, forecast(): before = lax.ppermute(p_cov, 'row', up)  24.9 us
    ppermute x1, starting transfers between devices, forecast(): other = lax.ppermute(mine, 'row', pairs)  10.3 us
    ppermute x1, waiting for transfers between devices, forecast(): right = lax.ppermute(low, 'col', down)  10 us
    ppermute x1, starting transfers between devices, forecast(): right = lax.ppermute(low, 'col', down)  9.98 us
    ppermute x1, waiting for transfers between devices, forecast(): left = lax.ppermute(high, 'col', up)  4.34 us
    ppermute x1, starting transfers between devices, forecast(): after = lax.ppermute(p_cov, 'row', down)  3.36 us
    unnamed x12, local copies, waits for them, and re-layouts  3.09 us
    pallas_call x1, Pallas kernels, forecast(): pl.pallas_call(functools.partial(stage2_kernel, fan, 0), out_shape=(out_t...  3 us
  transfers between devices with their start and end apart: 11, of which 3 were waited for; matrix products, arithmetic and copies ran while one was open for 0% of the time, Pallas kernels for 7%

profile of v6, /device:TPU:29, one launch (start us, length us, event | category | flops | bytes accessed | tf_op | source)
XLA Modules:
  0.0 81.5 jit_solution(16622137326554137826)
XLA Ops:
  0.0 0.7 collective-permute-start
  0.7 1.3 %collective-permute-start.2 = (bf16[4,7,128,128]{3,2,1,0:T(8,128)(2,1)}, bf16[4,7,128,128]{3,2,1,0:T(8,128)(2,1)S(1)}, u32[]{:S(2)}, u32[]{:S(2)}) collective-permute-start(bf16[4,7,128,128]{3,2,1,0:T(8,128)(2,1)} %refs_0_.1), channel_id=1, source_target_pairs={{0,16},{4,12},{9,25},{13,5},{18,2},{22,30},{27,11},{31,23}} | collective-permute-start | bytes 2752520 | tf_op jit(solution)/shard_map/ppermute | solution.py:242
  2.0 0.0 collective-permute-done.refs_1_
  2.0 0.7 collective-permute-start.1
  2.8 1.2 %copy-done.1 = bf16[4,7,128,128]{3,2,1,0:T(8,128)(2,1)S(1)} copy-done((bf16[4,7,128,128]{3,2,1,0:T(8,128)(2,1)S(1)}, bf16[4,7,128,128]{3,2,1,0:T(8,128)(2,1)}, u32[]{:S(2)}) %copy-start.1) | copy-done | bytes 917528
  3.9 1.2 %copy-done.2 = bf16[512,1024]{1,0:T(8,128)(2,1)S(1)} copy-done((bf16[512,1024]{1,0:T(8,128)(2,1)S(1)}, bf16[512,1024]{1,0:T(8,128)(2,1)}, u32[]{:S(2)}) %copy-start.2) | copy-done | bytes 1048600
  5.2 0.7 copy-done.5
  5.8 0.3 fetch.1
  6.2 0.7 collective-permute-start.7
  6.9 24.9 %collective-permute-start.4 = (bf16[512,1024]{1,0:T(8,128)(2,1)S(1)}, bf16[512,1024]{1,0:T(8,128)(2,1)S(1)}, u32[]{:S(2)}, u32[]{:S(2)}) collective-permute-start(bf16[512,1024]{1,0:T(8,128)(2,1)S(1)} %copy-done.2), channel_id=1, source_target_pairs={{0,4},{4,8},{8,12},{16,20},{20,24},{24,28},{1,5},{5,9},{9,13},{17,... | collective-permute-start | bytes 3145736 | tf_op jit(solution)/shard_map/ppermute | solution.py:238
  31.8 3.4 %collective-permute-start.5 = (bf16[512,1024]{1,0:T(8,128)(2,1)S(1)}, bf16[512,1024]{1,0:T(8,128)(2,1)S(1)}, u32[]{:S(2)}, u32[]{:S(2)}) collective-permute-start(bf16[512,1024]{1,0:T(8,128)(2,1)S(1)} %copy-done.2), channel_id=1, source_target_pairs={{4,0},{8,4},{12,8},{20,16},{24,20},{28,24},{5,1},{9,5},{13,9},{21,... | collective-permute-start | bytes 3145736 | tf_op jit(solution)/shard_map/ppermute | solution.py:239
  35.2 0.0 collective-permute-done.7
  35.2 0.7 collective-permute-start.6
  35.9 0.7 collective-permute-start.8
  36.6 0.3 pick.1.f_ref
  36.9 10.3 %collective-permute-start.3 = (bf16[4,7,128,128]{3,2,1,0:T(8,128)(2,1)S(1)}, bf16[4,7,128,128]{3,2,1,0:T(8,128)(2,1)S(1)}, u32[]{:S(2)}, u32[]{:S(2)}) collective-permute-start(bf16[4,7,128,128]{3,2,1,0:T(8,128)(2,1)S(1)} %pick.1.f_ref), channel_id=1, source_target_pairs={{4,0},{0,4},{12,8},{8,12},{20,16},{16,20},{28,24},{24,28},{5,1},{1... | collective-permute-start | bytes 2752520 | tf_op jit(solution)/shard_map/ppermute | solution.py:295
  47.2 0.7 collective-permute-done.5.after_hbm
  47.9 2.2 %stage1.1 = (bf16[512,512]{1,0:T(8,128)(2,1)S(1)}, bf16[512,512]{1,0:T(8,128)(2,1)S(1)}) custom-call(s32[7,32]{1,0:T(8,128)S(1)} %get-tuple-element.13.cols_ref, bf16[4,7,128,128]{3,2,1,0:T(8,128)(2,1)S(1)} %get-tuple-element.14.f_ref, bf16[256,1024]{1,0:T(8,128)(2,1)S(1)} %get-tuple-element.15.top_hbm, bf16[256,1024]{1,0:T(8,128)(2,1)S(1)} %get-tuple-element.16.bottom_hbm, ...), custom_call_target="tpu_custom_call" | custom-call | tf_op jit(solution)/shard_map/stage1/pallas_call | solution.py:245
  50.1 10.0 %collective-permute-start.10 = (bf16[512,512]{1,0:T(8,128)(2,1)S(1)}, bf16[512,512]{1,0:T(8,128)(2,1)S(1)}, u32[]{:S(2)}, u32[]{:S(2)}) collective-permute-start(bf16[512,512]{1,0:T(8,128)(2,1)S(1)} %get-tuple-element.18.refs_1_), channel_id=1, source_target_pairs={{1,0},{2,1},{3,2},{5,4},{6,5},{7,6},{9,8},{10,9},{11,10},{13,12},{... | collective-permute-start | bytes 1572872 | tf_op jit(solution)/shard_map/ppermute | solution.py:260
  60.1 1.3 %collective-permute-start.9 = (bf16[512,512]{1,0:T(8,128)(2,1)S(1)}, bf16[512,512]{1,0:T(8,128)(2,1)S(1)}, u32[]{:S(2)}, u32[]{:S(2)}) collective-permute-start(bf16[512,512]{1,0:T(8,128)(2,1)S(1)} %get-tuple-element.17.refs_2_), channel_id=1, source_target_pairs={{0,1},{1,2},{2,3},{4,5},{5,6},{6,7},{8,9},{9,10},{10,11},{12,13},{... | collective-permute-start | bytes 1572872 | tf_op jit(solution)/shard_map/ppermute | solution.py:259
  61.4 10.0 %collective-permute-done.10.refs_3_ = bf16[512,512]{1,0:T(8,128)(2,1)S(1)} collective-permute-done((bf16[512,512]{1,0:T(8,128)(2,1)S(1)}, bf16[512,512]{1,0:T(8,128)(2,1)S(1)}, u32[]{:S(2)}, u32[]{:S(2)}) %collective-permute-start.10) | collective-permute-done | bytes 524320 | tf_op jit(solution)/shard_map/ppermute | solution.py:260
  71.5 4.3 %collective-permute-done.9.refs_0_ = bf16[512,512]{1,0:T(8,128)(2,1)S(1)} collective-permute-done((bf16[512,512]{1,0:T(8,128)(2,1)S(1)}, bf16[512,512]{1,0:T(8,128)(2,1)S(1)}, u32[]{:S(2)}, u32[]{:S(2)}) %collective-permute-start.9) | collective-permute-done | bytes 524320 | tf_op jit(solution)/shard_map/ppermute | solution.py:259
  75.8 3.0 %stage2.1 = (f32[512,1024]{1,0:T(8,128)}, bf16[512,2048]{1,0:T(8,128)(2,1)S(1)}) custom-call(s32[7,32]{1,0:T(8,128)S(1)} %get-tuple-element.13.cols_ref, s32[4,8]{1,0:T(4,128)S(1)} %copy-done.3, f32[4,128]{1,0:T(4,128)S(1)} %bitcast.2, bf16[512,1024]{1,0:T(8,128)(2,1)S(1)} %copy-done, bf16[4,7,128,128]{3,2,1,0:T(8,128)(2,1)S(1)} %pick.1.f_ref, ...), custom_call_target="tpu_custom_call" | custom-call | tf_op jit(solution)/shard_map/stage2/pallas_call | solution.py:284
  78.8 2.6 %stage3.1 = f32[512,1024]{1,0:T(8,128)} custom-call(s32[7,32]{1,0:T(8,128)S(1)} %get-tuple-element.13.cols_ref, s32[4,8]{1,0:T(4,128)S(1)} %copy-done.3, f32[4,128]{1,0:T(4,128)S(1)} %bitcast.3, bf16[512,1024]{1,0:T(8,128)(2,1)S(1)} %copy-done, bf16[4,7,128,128]{3,2,1,0:T(8,128)(2,1)S(1)} %collective-permute-done.3.f_ref, ...), custom_call_target="tpu_custom_call", output_to_operand_aliasing={{}: (6, {})} | custom-call | tf_op jit(solution)/shard_map/stage3/pallas_call | solution.py:296
  (15 shorter events, 0.0 us)
Async XLA Ops:
  0.0 2.0 %collective-permute-start = (bf16[4,7,128,128]{3,2,1,0:T(8,128)(2,1)}, bf16[4,7,128,128]{3,2,1,0:T(8,128)(2,1)S(1)}, u32[]{:S(2)}, u32[]{:S(2)}) collective-permute-start(bf16[4,7,128,128]{3,2,1,0:T(8,128)(2,1)} %refs_0_.1), channel_id=1, source_target_pairs={{0,8},{4,20},{9,1},{13,29},{18,26},{22,6},{27,19},{31,15}} | collective-permute-start | bytes 2752520 | tf_op jit(solution)/shard_map/ppermute | solution.py:242
  0.7 35.2 %collective-permute-start.2 = (bf16[4,7,128,128]{3,2,1,0:T(8,128)(2,1)}, bf16[4,7,128,128]{3,2,1,0:T(8,128)(2,1)S(1)}, u32[]{:S(2)}, u32[]{:S(2)}) collective-permute-start(bf16[4,7,128,128]{3,2,1,0:T(8,128)(2,1)} %refs_0_.1), channel_id=1, source_target_pairs={{0,16},{4,12},{9,25},{13,5},{18,2},{22,30},{27,11},{31,23}} | collective-permute-start | bytes 2752520 | tf_op jit(solution)/shard_map/ppermute | solution.py:242
  2.0 34.6 %collective-permute-start.1 = (bf16[4,7,128,128]{3,2,1,0:T(8,128)(2,1)S(1)}, bf16[4,7,128,128]{3,2,1,0:T(8,128)(2,1)S(1)}, u32[]{:S(2)}, u32[]{:S(2)}) collective-permute-start(bf16[4,7,128,128]{3,2,1,0:T(8,128)(2,1)S(1)} %collective-permute-done.refs_1_), channel_id=1, source_target_pairs={{8,24},{20,28},{1,17},{29,21},{26,10},{6,14},{19,3},{15,7}} | collective-permute-start | bytes 2752520 | tf_op jit(solution)/shard_map/ppermute | solution.py:242
  2.8 1.2 %copy-start.1 = (bf16[4,7,128,128]{3,2,1,0:T(8,128)(2,1)S(1)}, bf16[4,7,128,128]{3,2,1,0:T(8,128)(2,1)}, u32[]{:S(2)}) copy-start(bf16[4,7,128,128]{3,2,1,0:T(8,128)(2,1)} %refs_0_.1) | copy-start | bytes 2752516
  3.9 1.2 %copy-start.2 = (bf16[512,1024]{1,0:T(8,128)(2,1)S(1)}, bf16[512,1024]{1,0:T(8,128)(2,1)}, u32[]{:S(2)}) copy-start(bf16[512,1024]{1,0:T(8,128)(2,1)} %p_hbm.1) | copy-start | bytes 3145732
  5.2 0.7 copy-start.5
  6.2 29.0 %collective-permute-start.7 = (bf16[256,1024]{1,0:T(8,128)(2,1)S(1)}, bf16[256,1024]{1,0:T(8,128)(2,1)S(1)}, u32[]{:S(2)}, u32[]{:S(2)}) collective-permute-start(bf16[256,1024]{1,0:T(8,128)(2,1)S(1)} %get-tuple-element.16.bottom_hbm), channel_id=1, source_target_pairs={{12,28},{16,0},{13,29},{17,1},{14,30},{18,2},{15,31},{19,3}} | collective-permute-start | bytes 1572872 | tf_op jit(solution)/shard_map/ppermute | solution.py:235
  6.9 40.3 %collective-permute-start.4 = (bf16[512,1024]{1,0:T(8,128)(2,1)S(1)}, bf16[512,1024]{1,0:T(8,128)(2,1)S(1)}, u32[]{:S(2)}, u32[]{:S(2)}) collective-permute-start(bf16[512,1024]{1,0:T(8,128)(2,1)S(1)} %copy-done.2), channel_id=1, source_target_pairs={{0,4},{4,8},{8,12},{16,20},{20,24},{24,28},{1,5},{5,9},{9,13},{17,... | collective-permute-start | bytes 3145736 | tf_op jit(solution)/shard_map/ppermute | solution.py:238
  31.8 16.1 %collective-permute-start.5 = (bf16[512,1024]{1,0:T(8,128)(2,1)S(1)}, bf16[512,1024]{1,0:T(8,128)(2,1)S(1)}, u32[]{:S(2)}, u32[]{:S(2)}) collective-permute-start(bf16[512,1024]{1,0:T(8,128)(2,1)S(1)} %copy-done.2), channel_id=1, source_target_pairs={{4,0},{8,4},{12,8},{20,16},{24,20},{28,24},{5,1},{9,5},{13,9},{21,... | collective-permute-start | bytes 3145736 | tf_op jit(solution)/shard_map/ppermute | solution.py:239
  35.2 12.0 %collective-permute-start.6 = (bf16[256,1024]{1,0:T(8,128)(2,1)S(1)}, bf16[256,1024]{1,0:T(8,128)(2,1)S(1)}, u32[]{:S(2)}, u32[]{:S(2)}) collective-permute-start(bf16[256,1024]{1,0:T(8,128)(2,1)S(1)} %get-tuple-element.15.top_hbm), channel_id=1, source_target_pairs={{12,16},{16,12},{13,17},{17,13},{14,18},{18,14},{15,19},{19,15}} | collective-permute-start | bytes 1572872 | tf_op jit(solution)/shard_map/ppermute | solution.py:234
  35.9 11.3 %collective-permute-start.8 = (bf16[256,1024]{1,0:T(8,128)(2,1)S(1)}, bf16[256,1024]{1,0:T(8,128)(2,1)S(1)}, u32[]{:S(2)}, u32[]{:S(2)}) collective-permute-start(bf16[256,1024]{1,0:T(8,128)(2,1)S(1)} %collective-permute-done.7), channel_id=1, source_target_pairs={{28,16},{0,12},{29,17},{1,13},{30,18},{2,14},{31,19},{3,15}} | collective-permute-start | bytes 1572872 | tf_op jit(solution)/shard_map/ppermute | solution.py:236
  36.9 41.9 %collective-permute-start.3 = (bf16[4,7,128,128]{3,2,1,0:T(8,128)(2,1)S(1)}, bf16[4,7,128,128]{3,2,1,0:T(8,128)(2,1)S(1)}, u32[]{:S(2)}, u32[]{:S(2)}) collective-permute-start(bf16[4,7,128,128]{3,2,1,0:T(8,128)(2,1)S(1)} %pick.1.f_ref), channel_id=1, source_target_pairs={{4,0},{0,4},{12,8},{8,12},{20,16},{16,20},{28,24},{24,28},{5,1},{1... | collective-permute-start | bytes 2752520 | tf_op jit(solution)/shard_map/ppermute | solution.py:295
  47.9 27.9 %copy-start = (bf16[512,1024]{1,0:T(8,128)(2,1)S(1)}, bf16[512,1024]{1,0:T(8,128)(2,1)}, u32[]{:S(2)}) copy-start(bf16[512,1024]{1,0:T(8,128)(2,1)} %w_ref.3) | copy-start | bytes 3145732
  47.9 27.9 %copy-start.3 = (s32[4,8]{1,0:T(4,128)S(1)}, s32[4,8]{1,0:T(4,128)}, u32[]{:S(2)}) copy-start(s32[4,8]{1,0:T(4,128)} %mask_ref.3) | copy-start | bytes 388
  47.9 27.9 %copy-start.4 = (f32[512]{0:T(512)S(1)}, f32[512]{0:T(512)}, u32[]{:S(2)}) copy-start(f32[512]{0:T(512)} %param.11) | copy-start | bytes 6148
  50.1 21.3 %collective-permute-start.10 = (bf16[512,512]{1,0:T(8,128)(2,1)S(1)}, bf16[512,512]{1,0:T(8,128)(2,1)S(1)}, u32[]{:S(2)}, u32[]{:S(2)}) collective-permute-start(bf16[512,512]{1,0:T(8,128)(2,1)S(1)} %get-tuple-element.18.refs_1_), channel_id=1, source_target_pairs={{1,0},{2,1},{3,2},{5,4},{6,5},{7,6},{9,8},{10,9},{11,10},{13,12},{... | collective-permute-start | bytes 1572872 | tf_op jit(solution)/shard_map/ppermute | solution.py:260
  60.1 15.7 %collective-permute-start.9 = (bf16[512,512]{1,0:T(8,128)(2,1)S(1)}, bf16[512,512]{1,0:T(8,128)(2,1)S(1)}, u32[]{:S(2)}, u32[]{:S(2)}) collective-permute-start(bf16[512,512]{1,0:T(8,128)(2,1)S(1)} %get-tuple-element.17.refs_2_), channel_id=1, source_target_pairs={{0,1},{1,2},{2,3},{4,5},{5,6},{6,7},{8,9},{9,10},{10,11},{12,13},{... | collective-permute-start | bytes 1572872 | tf_op jit(solution)/shard_map/ppermute | solution.py:259

commit v7 on v6

--- a/solution.py
+++ b/solution.py
@@ -71,13 +71,10 @@
             copy.wait()
 
 
-def fetch_kernel(p_hbm, f_hbm, cols_hbm, top_ref, bottom_ref, f_ref, cols_ref, sem):
-    half = top_ref.shape[0]
+def fetch_kernel(f_hbm, cols_hbm, f_ref, cols_ref, sem):
     copies = [
-        pltpu.make_async_copy(p_hbm.at[:half], top_ref, sem.at[0]),
-        pltpu.make_async_copy(p_hbm.at[half:], bottom_ref, sem.at[1]),
-        pltpu.make_async_copy(f_hbm, f_ref, sem.at[2]),
-        pltpu.make_async_copy(cols_hbm, cols_ref, sem.at[3]),
+        pltpu.make_async_copy(f_hbm, f_ref, sem.at[0]),
+        pltpu.make_async_copy(cols_hbm, cols_ref, sem.at[1]),
     ]
     for copy in copies:
         copy.start()
@@ -207,21 +204,16 @@
     smem = pl.BlockSpec(memory_space=pltpu.SMEM)
     hbm = pl.BlockSpec(memory_space=ANY)
     vmem = pl.BlockSpec(memory_space=pltpu.VMEM)
-    wanted = (
-        jax.ShapeDtypeStruct((tall // 2, wide), p_cov.dtype),
-        jax.ShapeDtypeStruct((tall // 2, wide), p_cov.dtype),
-        jax.ShapeDtypeStruct(f_blocks.shape, f_blocks.dtype),
-        jax.ShapeDtypeStruct(cols_of.shape, cols_of.dtype),
-    )
-    top, bottom, f_near, cols_of = pl.pallas_call(
+    top, bottom = p_cov[: tall // 2], p_cov[tall // 2 :]
+    f_near, cols_of = pl.pallas_call(
         fetch_kernel,
-        out_shape=wanted,
-        in_specs=[hbm] * 3,
-        out_specs=(vmem,) * 4,
-        scratch_shapes=[pltpu.SemaphoreType.DMA((4,))],
+        out_shape=tuple(jax.ShapeDtypeStruct(x.shape, x.dtype) for x in (f_blocks, cols_of)),
+        in_specs=[hbm, hbm],
+        out_specs=(vmem, vmem),
+        scratch_shapes=[pltpu.SemaphoreType.DMA((2,))],
         compiler_params=pltpu.CompilerParams(vmem_limit_bytes=8 * 2**20),
         name="fetch",
-    )(p_cov, f_blocks, cols_of)
+    )(f_blocks, cols_of)
 
     up, down = up_down(rows)
     bent, halves = (rows // 2, rows // 2 - 1), ()

time: 81.9 us -> 79.7 us (0.973)
  the two profiles are of different devices: /device:TPU:29 before, /device:TPU:28 now
where the time goes in v7:
time: 79.7 us; the launch traced here: 79.4 us
  waiting for transfers between devices  56 us (70%)
  starting transfers between devices  13.5 us (17%)
  Pallas kernels  8.39 us (11%)
  local copies, waits for them, and re-layouts  1.3 us (2%)
    ppermute x3, waiting for transfers between devices, forecast(): held.append(lax.ppermute(held[source], ('row', 'col'), pairs))  23.1 us
    ppermute x1, waiting for transfers between devices, forecast(): turn = lax.ppermute(bottom, 'row', [(upper, rows - 1), (lower, 0)])  11.2 us
    ppermute x1, waiting for transfers between devices, forecast(): right = lax.ppermute(low, 'col', down)  9.05 us
    ppermute x1, waiting for transfers between devices, forecast(): straight = lax.ppermute(top, 'row', across)  7.51 us
    ppermute x1, waiting for transfers between devices, forecast(): left = lax.ppermute(high, 'col', up)  4.15 us
    ppermute x3, starting transfers between devices, forecast(): held.append(lax.ppermute(held[source], ('row', 'col'), pairs))  3.47 us
    pallas_call x1, Pallas kernels, forecast(): pl.pallas_call(functools.partial(stage2_kernel, fan, 0), out_shape=(out_t...  3 us
    pallas_call x1, Pallas kernels, forecast(): pl.pallas_call(functools.partial(stage2_kernel, fan, turn), out_shape=out...  2.67 us
  transfers between devices with their start and end apart: 11, of which 6 were waited for; matrix products, arithmetic and copies ran while one was open for 2% of the time, Pallas kernels for 7%

profile of v7, /device:TPU:28, one launch (start us, length us, event | category | flops | bytes accessed | tf_op | source)
XLA Modules:
  0.0 79.4 jit_solution(15094828953560799093)
XLA Ops:
  0.0 1.4 %collective-permute-start = (bf16[4,7,128,128]{3,2,1,0:T(8,128)(2,1)}, bf16[4,7,128,128]{3,2,1,0:T(8,128)(2,1)S(1)}, u32[]{:S(2)}, u32[]{:S(2)}) collective-permute-start(bf16[4,7,128,128]{3,2,1,0:T(8,128)(2,1)} %refs_0_.1), channel_id=1, source_target_pairs={{0,8},{4,20},{9,1},{13,29},{18,26},{22,6},{27,19},{31,15}} | collective-permute-start | bytes 2752520 | tf_op jit(solution)/shard_map/ppermute | solution.py:234
  1.4 0.7 collective-permute-start.2
  2.2 23.1 %collective-permute-done.refs_1_ = bf16[4,7,128,128]{3,2,1,0:T(8,128)(2,1)S(1)} collective-permute-done((bf16[4,7,128,128]{3,2,1,0:T(8,128)(2,1)}, bf16[4,7,128,128]{3,2,1,0:T(8,128)(2,1)S(1)}, u32[]{:S(2)}, u32[]{:S(2)}) %collective-permute-start) | collective-permute-done | bytes 917536 | tf_op jit(solution)/shard_map/ppermute | solution.py:234
  25.3 1.3 %collective-permute-start.1 = (bf16[4,7,128,128]{3,2,1,0:T(8,128)(2,1)S(1)}, bf16[4,7,128,128]{3,2,1,0:T(8,128)(2,1)S(1)}, u32[]{:S(2)}, u32[]{:S(2)}) collective-permute-start(bf16[4,7,128,128]{3,2,1,0:T(8,128)(2,1)S(1)} %collective-permute-done.refs_1_), channel_id=1, source_target_pairs={{8,24},{20,28},{1,17},{29,21},{26,10},{6,14},{19,3},{15,7}} | collective-permute-start | bytes 2752520 | tf_op jit(solution)/shard_map/ppermute | solution.py:234
  26.6 1.3 %fusion = (bf16[256,1024]{1,0:T(8,128)(2,1)S(1)}, bf16[256,1024]{1,0:T(8,128)(2,1)S(1)}) fusion(bf16[512,1024]{1,0:T(8,128)(2,1)} %param.6), kind=kLoop, calls=%fused_computation | loop fusion | bytes 2097152 | tf_op jit(solution)/shard_map/slice | solution.py:207
  27.9 1.3 %collective-permute-start.7 = (bf16[256,1024]{1,0:T(8,128)(2,1)S(1)}, bf16[256,1024]{1,0:T(8,128)(2,1)S(1)}, u32[]{:S(2)}, u32[]{:S(2)}) collective-permute-start(bf16[256,1024]{1,0:T(8,128)(2,1)S(1)} %get-tuple-element.17.bottom_hbm), channel_id=1, source_target_pairs={{12,28},{16,0},{13,29},{17,1},{14,30},{18,2},{15,31},{19,3}} | collective-permute-start | bytes 1572872 | tf_op jit(solution)/shard_map/ppermute | solution.py:227
  29.2 1.4 %collective-permute-start.4 = (bf16[512,1024]{1,0:T(8,128)(2,1)S(1)}, bf16[512,1024]{1,0:T(8,128)(2,1)S(1)}, u32[]{:S(2)}, u32[]{:S(2)}) collective-permute-start(bf16[512,1024]{1,0:T(8,128)(2,1)S(1)} %copy-done.5), channel_id=1, source_target_pairs={{0,4},{4,8},{8,12},{16,20},{20,24},{24,28},{1,5},{5,9},{9,13},{17,... | collective-permute-start | bytes 3145736 | tf_op jit(solution)/shard_map/ppermute | solution.py:230
  30.6 1.3 %collective-permute-start.5 = (bf16[512,1024]{1,0:T(8,128)(2,1)S(1)}, bf16[512,1024]{1,0:T(8,128)(2,1)S(1)}, u32[]{:S(2)}, u32[]{:S(2)}) collective-permute-start(bf16[512,1024]{1,0:T(8,128)(2,1)S(1)} %copy-done.5), channel_id=1, source_target_pairs={{4,0},{8,4},{12,8},{20,16},{24,20},{28,24},{5,1},{9,5},{13,9},{21,... | collective-permute-start | bytes 3145736 | tf_op jit(solution)/shard_map/ppermute | solution.py:231
  31.9 11.2 %collective-permute-done.7 = bf16[256,1024]{1,0:T(8,128)(2,1)S(1)} collective-permute-done((bf16[256,1024]{1,0:T(8,128)(2,1)S(1)}, bf16[256,1024]{1,0:T(8,128)(2,1)S(1)}, u32[]{:S(2)}, u32[]{:S(2)}) %collective-permute-start.7) | collective-permute-done | bytes 524320 | tf_op jit(solution)/shard_map/ppermute | solution.py:227
  43.1 2.0 %collective-permute-start.6 = (bf16[256,1024]{1,0:T(8,128)(2,1)S(1)}, bf16[256,1024]{1,0:T(8,128)(2,1)S(1)}, u32[]{:S(2)}, u32[]{:S(2)}) collective-permute-start(bf16[256,1024]{1,0:T(8,128)(2,1)S(1)} %get-tuple-element.18.top_hbm), channel_id=1, source_target_pairs={{12,16},{16,12},{13,17},{17,13},{14,18},{18,14},{15,19},{19,15}} | collective-permute-start | bytes 1572872 | tf_op jit(solution)/shard_map/ppermute | solution.py:226
  45.1 1.3 %collective-permute-start.8 = (bf16[256,1024]{1,0:T(8,128)(2,1)S(1)}, bf16[256,1024]{1,0:T(8,128)(2,1)S(1)}, u32[]{:S(2)}, u32[]{:S(2)}) collective-permute-start(bf16[256,1024]{1,0:T(8,128)(2,1)S(1)} %collective-permute-done.7), channel_id=1, source_target_pairs={{28,16},{0,12},{29,17},{1,13},{30,18},{2,14},{31,19},{3,15}} | collective-permute-start | bytes 1572872 | tf_op jit(solution)/shard_map/ppermute | solution.py:228
  46.4 0.3 pick.1.f_ref
  46.7 0.1 collective-permute-start.3
  46.8 0.2 fetch.1
  47.1 7.5 %collective-permute-done.6.refs_0_ = bf16[256,1024]{1,0:T(8,128)(2,1)S(1)} collective-permute-done((bf16[256,1024]{1,0:T(8,128)(2,1)S(1)}, bf16[256,1024]{1,0:T(8,128)(2,1)S(1)}, u32[]{:S(2)}, u32[]{:S(2)}) %collective-permute-start.6) | collective-permute-done | bytes 524320 | tf_op jit(solution)/shard_map/ppermute | solution.py:226
  54.6 1.0 %collective-permute-done.8.refs_1_ = bf16[256,1024]{1,0:T(8,128)(2,1)S(1)} collective-permute-done((bf16[256,1024]{1,0:T(8,128)(2,1)S(1)}, bf16[256,1024]{1,0:T(8,128)(2,1)S(1)}, u32[]{:S(2)}, u32[]{:S(2)}) %collective-permute-start.8) | collective-permute-done | bytes 524320 | tf_op jit(solution)/shard_map/ppermute | solution.py:228
  55.6 0.0 copy-start.2
  55.7 2.2 %stage1.1 = (bf16[512,512]{1,0:T(8,128)(2,1)S(1)}, bf16[512,512]{1,0:T(8,128)(2,1)S(1)}) custom-call(s32[7,32]{1,0:T(8,128)S(1)} %get-tuple-element.11.cols_ref, bf16[4,7,128,128]{3,2,1,0:T(8,128)(2,1)S(1)} %get-tuple-element.12.f_ref, bf16[256,1024]{1,0:T(8,128)(2,1)S(1)} %get-tuple-element.18.top_hbm, bf16[256,1024]{1,0:T(8,128)(2,1)S(1)} %get-tuple-element.17.bottom_hbm, ...), custom_call_target="tpu_custom_call" | custom-call | tf_op jit(solution)/shard_map/stage1/pallas_call | solution.py:237
  57.9 1.3 %collective-permute-start.10 = (bf16[512,512]{1,0:T(8,128)(2,1)S(1)}, bf16[512,512]{1,0:T(8,128)(2,1)S(1)}, u32[]{:S(2)}, u32[]{:S(2)}) collective-permute-start(bf16[512,512]{1,0:T(8,128)(2,1)S(1)} %get-tuple-element.14.refs_1_), channel_id=1, source_target_pairs={{1,0},{2,1},{3,2},{5,4},{6,5},{7,6},{9,8},{10,9},{11,10},{13,12},{... | collective-permute-start | bytes 1572872 | tf_op jit(solution)/shard_map/ppermute | solution.py:252
  59.2 1.3 %collective-permute-start.9 = (bf16[512,512]{1,0:T(8,128)(2,1)S(1)}, bf16[512,512]{1,0:T(8,128)(2,1)S(1)}, u32[]{:S(2)}, u32[]{:S(2)}) collective-permute-start(bf16[512,512]{1,0:T(8,128)(2,1)S(1)} %get-tuple-element.13.refs_2_), channel_id=1, source_target_pairs={{0,1},{1,2},{2,3},{4,5},{5,6},{6,7},{8,9},{9,10},{10,11},{12,13},{... | collective-permute-start | bytes 1572872 | tf_op jit(solution)/shard_map/ppermute | solution.py:251
  60.5 9.0 %collective-permute-done.10.refs_3_ = bf16[512,512]{1,0:T(8,128)(2,1)S(1)} collective-permute-done((bf16[512,512]{1,0:T(8,128)(2,1)S(1)}, bf16[512,512]{1,0:T(8,128)(2,1)S(1)}, u32[]{:S(2)}, u32[]{:S(2)}) %collective-permute-start.10) | collective-permute-done | bytes 524320 | tf_op jit(solution)/shard_map/ppermute | solution.py:252
  69.5 4.1 %collective-permute-done.9.refs_0_ = bf16[512,512]{1,0:T(8,128)(2,1)S(1)} collective-permute-done((bf16[512,512]{1,0:T(8,128)(2,1)S(1)}, bf16[512,512]{1,0:T(8,128)(2,1)S(1)}, u32[]{:S(2)}, u32[]{:S(2)}) %collective-permute-start.9) | collective-permute-done | bytes 524320 | tf_op jit(solution)/shard_map/ppermute | solution.py:251
  73.7 3.0 %stage2.1 = (f32[512,1024]{1,0:T(8,128)}, bf16[512,2048]{1,0:T(8,128)(2,1)S(1)}) custom-call(s32[7,32]{1,0:T(8,128)S(1)} %get-tuple-element.11.cols_ref, s32[4,8]{1,0:T(4,128)S(1)} %copy-done.2, f32[4,128]{1,0:T(4,128)S(1)} %bitcast.2, bf16[512,1024]{1,0:T(8,128)(2,1)S(1)} %copy-done, bf16[4,7,128,128]{3,2,1,0:T(8,128)(2,1)S(1)} %pick.1.f_ref, ...), custom_call_target="tpu_custom_call" | custom-call | tf_op jit(solution)/shard_map/stage2/pallas_call | solution.py:276
  76.7 2.7 %stage3.1 = f32[512,1024]{1,0:T(8,128)} custom-call(s32[7,32]{1,0:T(8,128)S(1)} %get-tuple-element.11.cols_ref, s32[4,8]{1,0:T(4,128)S(1)} %copy-done.2, f32[4,128]{1,0:T(4,128)S(1)} %bitcast.3, bf16[512,1024]{1,0:T(8,128)(2,1)S(1)} %copy-done, bf16[4,7,128,128]{3,2,1,0:T(8,128)(2,1)S(1)} %collective-permute-done.3.f_ref, ...), custom_call_target="tpu_custom_call", output_to_operand_aliasing={{}: (6, {})} | custom-call | tf_op jit(solution)/shard_map/stage3/pallas_call | solution.py:288
  (16 shorter events, 0.0 us)
Async XLA Ops:
  0.0 46.4 %copy-start.1 = (bf16[4,7,128,128]{3,2,1,0:T(8,128)(2,1)S(1)}, bf16[4,7,128,128]{3,2,1,0:T(8,128)(2,1)}, u32[]{:S(2)}) copy-start(bf16[4,7,128,128]{3,2,1,0:T(8,128)(2,1)} %refs_0_.1) | copy-start | bytes 2752516
  0.0 29.2 %copy-start.5 = (bf16[512,1024]{1,0:T(8,128)(2,1)S(1)}, bf16[512,1024]{1,0:T(8,128)(2,1)}, u32[]{:S(2)}) copy-start(bf16[512,1024]{1,0:T(8,128)(2,1)} %param.6) | copy-start | bytes 3145732
  0.0 25.3 %collective-permute-start = (bf16[4,7,128,128]{3,2,1,0:T(8,128)(2,1)}, bf16[4,7,128,128]{3,2,1,0:T(8,128)(2,1)S(1)}, u32[]{:S(2)}, u32[]{:S(2)}) collective-permute-start(bf16[4,7,128,128]{3,2,1,0:T(8,128)(2,1)} %refs_0_.1), channel_id=1, source_target_pairs={{0,8},{4,20},{9,1},{13,29},{18,26},{22,6},{27,19},{31,15}} | collective-permute-start | bytes 2752520 | tf_op jit(solution)/shard_map/ppermute | solution.py:234
  1.4 43.7 %collective-permute-start.2 = (bf16[4,7,128,128]{3,2,1,0:T(8,128)(2,1)}, bf16[4,7,128,128]{3,2,1,0:T(8,128)(2,1)S(1)}, u32[]{:S(2)}, u32[]{:S(2)}) collective-permute-start(bf16[4,7,128,128]{3,2,1,0:T(8,128)(2,1)} %refs_0_.1), channel_id=1, source_target_pairs={{0,16},{4,12},{9,25},{13,5},{18,2},{22,30},{27,11},{31,23}} | collective-permute-start | bytes 2752520 | tf_op jit(solution)/shard_map/ppermute | solution.py:234
  25.3 21.2 %collective-permute-start.1 = (bf16[4,7,128,128]{3,2,1,0:T(8,128)(2,1)S(1)}, bf16[4,7,128,128]{3,2,1,0:T(8,128)(2,1)S(1)}, u32[]{:S(2)}, u32[]{:S(2)}) collective-permute-start(bf16[4,7,128,128]{3,2,1,0:T(8,128)(2,1)S(1)} %collective-permute-done.refs_1_), channel_id=1, source_target_pairs={{8,24},{20,28},{1,17},{29,21},{26,10},{6,14},{19,3},{15,7}} | collective-permute-start | bytes 2752520 | tf_op jit(solution)/shard_map/ppermute | solution.py:234
  27.9 15.2 %collective-permute-start.7 = (bf16[256,1024]{1,0:T(8,128)(2,1)S(1)}, bf16[256,1024]{1,0:T(8,128)(2,1)S(1)}, u32[]{:S(2)}, u32[]{:S(2)}) collective-permute-start(bf16[256,1024]{1,0:T(8,128)(2,1)S(1)} %get-tuple-element.17.bottom_hbm), channel_id=1, source_target_pairs={{12,28},{16,0},{13,29},{17,1},{14,30},{18,2},{15,31},{19,3}} | collective-permute-start | bytes 1572872 | tf_op jit(solution)/shard_map/ppermute | solution.py:227
  29.2 26.4 %collective-permute-start.4 = (bf16[512,1024]{1,0:T(8,128)(2,1)S(1)}, bf16[512,1024]{1,0:T(8,128)(2,1)S(1)}, u32[]{:S(2)}, u32[]{:S(2)}) collective-permute-start(bf16[512,1024]{1,0:T(8,128)(2,1)S(1)} %copy-done.5), channel_id=1, source_target_pairs={{0,4},{4,8},{8,12},{16,20},{20,24},{24,28},{1,5},{5,9},{9,13},{17,... | collective-permute-start | bytes 3145736 | tf_op jit(solution)/shard_map/ppermute | solution.py:230
  30.6 25.0 %collective-permute-start.5 = (bf16[512,1024]{1,0:T(8,128)(2,1)S(1)}, bf16[512,1024]{1,0:T(8,128)(2,1)S(1)}, u32[]{:S(2)}, u32[]{:S(2)}) collective-permute-start(bf16[512,1024]{1,0:T(8,128)(2,1)S(1)} %copy-done.5), channel_id=1, source_target_pairs={{4,0},{8,4},{12,8},{20,16},{24,20},{28,24},{5,1},{9,5},{13,9},{21,... | collective-permute-start | bytes 3145736 | tf_op jit(solution)/shard_map/ppermute | solution.py:231
  43.1 3.7 %copy-start.4 = (s32[32,7]{0,1:T(8,128)S(1)}, s32[32,7]{0,1:T(8,128)}, u32[]{:S(2)}) copy-start(s32[32,7]{0,1:T(8,128)} %param.8) | copy-start | bytes 2692
  43.1 11.5 %collective-permute-start.6 = (bf16[256,1024]{1,0:T(8,128)(2,1)S(1)}, bf16[256,1024]{1,0:T(8,128)(2,1)S(1)}, u32[]{:S(2)}, u32[]{:S(2)}) collective-permute-start(bf16[256,1024]{1,0:T(8,128)(2,1)S(1)} %get-tuple-element.18.top_hbm), channel_id=1, source_target_pairs={{12,16},{16,12},{13,17},{17,13},{14,18},{18,14},{15,19},{19,15}} | collective-permute-start | bytes 1572872 | tf_op jit(solution)/shard_map/ppermute | solution.py:226
  45.1 10.5 %collective-permute-start.8 = (bf16[256,1024]{1,0:T(8,128)(2,1)S(1)}, bf16[256,1024]{1,0:T(8,128)(2,1)S(1)}, u32[]{:S(2)}, u32[]{:S(2)}) collective-permute-start(bf16[256,1024]{1,0:T(8,128)(2,1)S(1)} %collective-permute-done.7), channel_id=1, source_target_pairs={{28,16},{0,12},{29,17},{1,13},{30,18},{2,14},{31,19},{3,15}} | collective-permute-start | bytes 1572872 | tf_op jit(solution)/shard_map/ppermute | solution.py:228
  46.7 30.0 %collective-permute-start.3 = (bf16[4,7,128,128]{3,2,1,0:T(8,128)(2,1)S(1)}, bf16[4,7,128,128]{3,2,1,0:T(8,128)(2,1)S(1)}, u32[]{:S(2)}, u32[]{:S(2)}) collective-permute-start(bf16[4,7,128,128]{3,2,1,0:T(8,128)(2,1)S(1)} %pick.1.f_ref), channel_id=1, source_target_pairs={{4,0},{0,4},{12,8},{8,12},{20,16},{16,20},{28,24},{24,28},{5,1},{1... | collective-permute-start | bytes 2752520 | tf_op jit(solution)/shard_map/ppermute | solution.py:287
  55.6 18.1 %copy-start = (bf16[512,1024]{1,0:T(8,128)(2,1)S(1)}, bf16[512,1024]{1,0:T(8,128)(2,1)}, u32[]{:S(2)}) copy-start(bf16[512,1024]{1,0:T(8,128)(2,1)} %w_ref.3) | copy-start | bytes 3145732
  55.6 18.1 %copy-start.2 = (s32[4,8]{1,0:T(4,128)S(1)}, s32[4,8]{1,0:T(4,128)}, u32[]{:S(2)}) copy-start(s32[4,8]{1,0:T(4,128)} %mask_ref.3) | copy-start | bytes 388
  55.6 18.0 %copy-start.3 = (f32[512]{0:T(512)S(1)}, f32[512]{0:T(512)}, u32[]{:S(2)}) copy-start(f32[512]{0:T(512)} %param.11) | copy-start | bytes 6148
  57.9 11.7 %collective-permute-start.10 = (bf16[512,512]{1,0:T(8,128)(2,1)S(1)}, bf16[512,512]{1,0:T(8,128)(2,1)S(1)}, u32[]{:S(2)}, u32[]{:S(2)}) collective-permute-start(bf16[512,512]{1,0:T(8,128)(2,1)S(1)} %get-tuple-element.14.refs_1_), channel_id=1, source_target_pairs={{1,0},{2,1},{3,2},{5,4},{6,5},{7,6},{9,8},{10,9},{11,10},{13,12},{... | collective-permute-start | bytes 1572872 | tf_op jit(solution)/shard_map/ppermute | solution.py:252
  59.2 14.5 %collective-permute-start.9 = (bf16[512,512]{1,0:T(8,128)(2,1)S(1)}, bf16[512,512]{1,0:T(8,128)(2,1)S(1)}, u32[]{:S(2)}, u32[]{:S(2)}) collective-permute-start(bf16[512,512]{1,0:T(8,128)(2,1)S(1)} %get-tuple-element.13.refs_2_), channel_id=1, source_target_pairs={{0,1},{1,2},{2,3},{4,5},{5,6},{6,7},{8,9},{9,10},{10,11},{12,13},{... | collective-permute-start | bytes 1572872 | tf_op jit(solution)/shard_map/ppermute | solution.py:251

commit v8 on v7

--- a/solution.py
+++ b/solution.py
@@ -13,9 +13,12 @@
 ANY = pl.ANY
 
 
-def up_down(devices):
-    up = [(i, i + 1) for i in range(devices - 1)]
-    return up, [(j, i) for i, j in up]
+def exchanges(devices):
+    both = []
+    for start in (0, 1):
+        pairs = [(i, i + 1) for i in range(start, devices - 1, 2)]
+        both.append(pairs + [(j, i) for i, j in pairs])
+    return both
 
 
 def source_plane(c, a, cols):
@@ -82,13 +85,17 @@
         copy.wait()
 
 
-def stage1_kernel(bent, cols_ref, f_ref, top_hbm, bottom_hbm, before_hbm, after_hbm, *refs):
-    *halves, low_ref, high_ref, ext, sem = refs
+def stage1_kernel(bent, cols_ref, f_ref, top_hbm, bottom_hbm, inner_hbm, outer_hbm, *refs):
+    *halves, first_ref, second_ref, ext, sem = refs
     rows, bs = f_ref.shape[0], f_ref.shape[2]
-    half = low_ref.shape[1]
-    row_idx = lax.axis_index("row")
-    first = row_idx * rows
-    halo, part = before_hbm.shape[0], top_hbm.shape[0]
+    half = first_ref.shape[1]
+    row_idx, col_idx = lax.axis_index("row"), lax.axis_index("col")
+    base = row_idx * rows
+    halo, part = inner_hbm.shape[0], top_hbm.shape[0]
+    below = halo + 2 * part
+    odd = lax.rem(row_idx, 2)
+    inner_at = pl.multiple_of((1 - odd) * below, bs)
+    outer_at = pl.multiple_of(odd * below, bs)
 
     def copies(at, pieces, sems):
         for piece, n in zip(pieces, sems):
@@ -98,37 +105,38 @@
     def all_copies(act):
         for copy in copies(halo, (top_hbm, bottom_hbm), (0, 1)):
             act(copy)
-        for at, whole, device, n in ((0, before_hbm, 0, 2), (halo + 2 * part, after_hbm, 1, 4)):
-            if not halves:
-                for copy in copies(at, (whole,), (n,)):
-                    act(copy)
-                continue
-
-            @pl.when(row_idx != bent[device])
-            def _():
-                for copy in copies(at, (whole,), (n,)):
-                    act(copy)
-
-            @pl.when(row_idx == bent[device])
-            def _():
-                for copy in copies(at, halves, (n, n + 1)):
-                    act(copy)
+        for copy in copies(inner_at, (inner_hbm,), (2,)):
+            act(copy)
+        if not halves:
+            for copy in copies(outer_at, (outer_hbm,), (3,)):
+                act(copy)
+            return
+        is_bent = (row_idx == bent[0]) | (row_idx == bent[1])
+
+        @pl.when(jnp.logical_not(is_bent))
+        def _():
+            for copy in copies(outer_at, (outer_hbm,), (3,)):
+                act(copy)
+
+        @pl.when(is_bent)
+        def _():
+            for copy in copies(outer_at, halves, (3, 4)):
+                act(copy)
 
     all_copies(lambda copy: copy.start())
     all_copies(lambda copy: copy.wait())
     tile = min(256, half)
+    odd = lax.rem(col_idx, 2)
     for i in range(rows):
         lhs = jnp.concatenate([f_ref[i, e] for e in range(STENCIL)], axis=1)
         starts = [
-            pl.multiple_of((cols_ref[e, first + i] - first + BAND) * bs, bs)
+            pl.multiple_of((cols_ref[e, base + i] - base + BAND) * bs, bs)
             for e in range(STENCIL)
         ]
-        for part, out_ref in enumerate((low_ref, high_ref)):
+        for part, out_ref in ((1 - odd, first_ref), (odd, second_ref)):
             for t in range(half // tile):
-                at = part * half + t * tile
-                rhs = jnp.concatenate(
-                    [ext[pl.ds(s, bs), at : at + tile] for s in starts], axis=0
-                )
+                at = pl.ds(pl.multiple_of(part * half + t * tile, bs), tile)
+                rhs = jnp.concatenate([ext[pl.ds(s, bs), at] for s in starts], axis=0)
                 out_ref[i * bs : (i + 1) * bs, t * tile : (t + 1) * tile] = jnp.dot(
                     lhs, rhs, preferred_element_type=jnp.float32
                 ).astype(out_ref.dtype)
@@ -147,11 +155,12 @@
     first = col_idx * slab - BAND
 
     joins = []
-    at = 0
+    odd = lax.rem(col_idx, 2)
     for piece, part in enumerate(parts):
-        to = ext.at[:, pl.ds(at, part.shape[1])]
+        width = part.shape[1]
+        at = odd * piece + (1 - odd) * (len(parts) - 1 - piece)
+        to = ext.at[:, pl.ds(pl.multiple_of(at * width, width), width)]
         joins.append(pltpu.make_async_copy(part, to, sem.at[piece]))
-        at += part.shape[1]
     for copy in joins:
         copy.start()
     for copy in joins:
@@ -215,41 +224,39 @@
         name="fetch",
     )(f_blocks, cols_of)
 
-    up, down = up_down(rows)
+    inner_pairs, outer_pairs = exchanges(rows)
     bent, halves = (rows // 2, rows // 2 - 1), ()
     if (cols, fan) == (4, 2):
         lower, upper = bent
         across = [(upper, lower), (lower, upper)]
-        up, down = (
-            [pair for pair in pairs if pair not in across] for pairs in (up, down)
-        )
+        outer_pairs = [pair for pair in outer_pairs if pair not in across]
         straight = lax.ppermute(top, "row", across)
         turn = lax.ppermute(bottom, "row", [(upper, rows - 1), (lower, 0)])
         turned = lax.ppermute(turn, "row", [(rows - 1, lower), (0, upper)])
         halves = (straight, turned)
-    before = lax.ppermute(p_cov, "row", up)
-    after = lax.ppermute(p_cov, "row", down)
+    inner = lax.ppermute(p_cov, "row", inner_pairs)
+    outer = lax.ppermute(p_cov, "row", outer_pairs)
     held = [f_blocks]
     for source, pairs in group_plan(rows, cols):
         held.append(lax.ppermute(held[source], ("row", "col"), pairs))
 
     half = jax.ShapeDtypeStruct((tall, halo), jnp.bfloat16)
-    low, high = pl.pallas_call(
+    first, second = pl.pallas_call(
         functools.partial(stage1_kernel, bent),
         out_shape=(half, half),
         in_specs=[smem, vmem] + [hbm] * (4 + len(halves)),
         out_specs=(vmem, vmem),
         scratch_shapes=[
             pltpu.VMEM((tall + 2 * halo, wide), jnp.bfloat16),
-            pltpu.SemaphoreType.DMA((6,)),
+            pltpu.SemaphoreType.DMA((5,)),
         ],
         compiler_params=pltpu.CompilerParams(vmem_limit_bytes=16 * 2**20),
         name="stage1",
-    )(cols_of, f_near, top, bottom, before, after, *halves)
-
-    up, down = up_down(cols)
-    left = lax.ppermute(high, "col", up)
-    right = lax.ppermute(low, "col", down)
+    )(cols_of, f_near, top, bottom, inner, outer, *halves)
+
+    inner_pairs, outer_pairs = exchanges(cols)
+    nearer = lax.ppermute(first, "col", inner_pairs)
+    further = lax.ppermute(second, "col", outer_pairs)
 
     mine = pl.pallas_call(
         functools.partial(pick_kernel, holder_table(rows, cols)),
@@ -281,7 +288,7 @@
         scratch_shapes=scratch + [pltpu.SemaphoreType.DMA((4,))],
         compiler_params=params,
         name="stage2",
-    )(*fixed, mine, left, low, high, right)
+    )(*fixed, mine, nearer, first, second, further)
     for turn in range(1, fan):
         pairs = [(r // fan * fan + (r + turn) % fan, r) for r in range(rows)]
         other = lax.ppermute(mine, "row", pairs)

time: 79.7 us -> 75.8 us (0.951)
  the two profiles are of different devices: /device:TPU:28 before, /device:TPU:20 now
where the time goes in v8:
time: 75.8 us; the launch traced here: 75.6 us
  waiting for transfers between devices  46.8 us (62%)
  starting transfers between devices  18.9 us (25%)
  Pallas kernels  8.37 us (11%)
  local copies, waits for them, and re-layouts  1.3 us (2%)
    ppermute x3, waiting for transfers between devices, forecast(): held.append(lax.ppermute(held[source], ('row', 'col'), pairs))  19.2 us
    ppermute x1, waiting for transfers between devices, forecast(): straight = lax.ppermute(top, 'row', across)  10.3 us
    ppermute x1, waiting for transfers between devices, forecast(): further = lax.ppermute(second, 'col', outer_pairs)  8.13 us
    ppermute x1, waiting for transfers between devices, forecast(): turn = lax.ppermute(bottom, 'row', [(upper, rows - 1), (lower, 0)])  5.82 us
    ppermute x3, starting transfers between devices, forecast(): held.append(lax.ppermute(held[source], ('row', 'col'), pairs))  5.63 us
    ppermute x1, starting transfers between devices, forecast(): further = lax.ppermute(second, 'col', outer_pairs)  4.99 us
    pallas_call x1, Pallas kernels, forecast(): pl.pallas_call(functools.partial(stage2_kernel, fan, 0), out_shape=(out_t...  3.01 us
    ppermute x1, starting transfers between devices, forecast(): nearer = lax.ppermute(first, 'col', inner_pairs)  2.74 us
  transfers between devices with their start and end apart: 11, of which 6 were waited for; matrix products, arithmetic and copies ran while one was open for 2% of the time, Pallas kernels for 8%

profile of v8, /device:TPU:20, one launch (start us, length us, event | category | flops | bytes accessed | tf_op | source)
XLA Modules:
  0.0 75.6 jit_solution(15289252785803848322)
XLA Ops:
  0.0 3.6 %collective-permute-start = (bf16[4,7,128,128]{3,2,1,0:T(8,128)(2,1)}, bf16[4,7,128,128]{3,2,1,0:T(8,128)(2,1)S(1)}, u32[]{:S(2)}, u32[]{:S(2)}) collective-permute-start(bf16[4,7,128,128]{3,2,1,0:T(8,128)(2,1)} %refs_0_.1), channel_id=1, source_target_pairs={{0,8},{4,20},{9,1},{13,29},{18,26},{22,6},{27,19},{31,15}} | collective-permute-start | bytes 2752520 | tf_op jit(solution)/shard_map/ppermute | solution.py:241
  3.6 1.3 %collective-permute-start.2 = (bf16[4,7,128,128]{3,2,1,0:T(8,128)(2,1)}, bf16[4,7,128,128]{3,2,1,0:T(8,128)(2,1)S(1)}, u32[]{:S(2)}, u32[]{:S(2)}) collective-permute-start(bf16[4,7,128,128]{3,2,1,0:T(8,128)(2,1)} %refs_0_.1), channel_id=1, source_target_pairs={{0,16},{4,12},{9,25},{13,5},{18,2},{22,30},{27,11},{31,23}} | collective-permute-start | bytes 2752520 | tf_op jit(solution)/shard_map/ppermute | solution.py:241
  4.9 19.2 %collective-permute-done.refs_1_ = bf16[4,7,128,128]{3,2,1,0:T(8,128)(2,1)S(1)} collective-permute-done((bf16[4,7,128,128]{3,2,1,0:T(8,128)(2,1)}, bf16[4,7,128,128]{3,2,1,0:T(8,128)(2,1)S(1)}, u32[]{:S(2)}, u32[]{:S(2)}) %collective-permute-start) | collective-permute-done | bytes 917536 | tf_op jit(solution)/shard_map/ppermute | solution.py:241
  24.2 0.7 collective-permute-start.1
  24.9 1.3 %fusion = (bf16[256,1024]{1,0:T(8,128)(2,1)S(1)}, bf16[256,1024]{1,0:T(8,128)(2,1)S(1)}) fusion(bf16[512,1024]{1,0:T(8,128)(2,1)} %param.6), kind=kLoop, calls=%fused_computation | loop fusion | bytes 2097152 | tf_op jit(solution)/shard_map/slice | solution.py:216
  26.1 1.3 %collective-permute-start.7 = (bf16[256,1024]{1,0:T(8,128)(2,1)S(1)}, bf16[256,1024]{1,0:T(8,128)(2,1)S(1)}, u32[]{:S(2)}, u32[]{:S(2)}) collective-permute-start(bf16[256,1024]{1,0:T(8,128)(2,1)S(1)} %get-tuple-element.17.bottom_hbm), channel_id=1, source_target_pairs={{12,28},{16,0},{13,29},{17,1},{14,30},{18,2},{15,31},{19,3}} | collective-permute-start | bytes 1572872 | tf_op jit(solution)/shard_map/ppermute | solution.py:234
  27.5 0.1 collective-permute-start.4
  27.6 0.7 collective-permute-start.5
  28.3 5.8 %collective-permute-done.7 = bf16[256,1024]{1,0:T(8,128)(2,1)S(1)} collective-permute-done((bf16[256,1024]{1,0:T(8,128)(2,1)S(1)}, bf16[256,1024]{1,0:T(8,128)(2,1)S(1)}, u32[]{:S(2)}, u32[]{:S(2)}) %collective-permute-start.7) | collective-permute-done | bytes 524320 | tf_op jit(solution)/shard_map/ppermute | solution.py:234
  34.1 2.0 %collective-permute-start.6 = (bf16[256,1024]{1,0:T(8,128)(2,1)S(1)}, bf16[256,1024]{1,0:T(8,128)(2,1)S(1)}, u32[]{:S(2)}, u32[]{:S(2)}) collective-permute-start(bf16[256,1024]{1,0:T(8,128)(2,1)S(1)} %get-tuple-element.18.top_hbm), channel_id=1, source_target_pairs={{12,16},{16,12},{13,17},{17,13},{14,18},{18,14},{15,19},{19,15}} | collective-permute-start | bytes 1572872 | tf_op jit(solution)/shard_map/ppermute | solution.py:233
  36.2 1.3 %collective-permute-start.8 = (bf16[256,1024]{1,0:T(8,128)(2,1)S(1)}, bf16[256,1024]{1,0:T(8,128)(2,1)S(1)}, u32[]{:S(2)}, u32[]{:S(2)}) collective-permute-start(bf16[256,1024]{1,0:T(8,128)(2,1)S(1)} %collective-permute-done.7), channel_id=1, source_target_pairs={{28,16},{0,12},{29,17},{1,13},{30,18},{2,14},{31,19},{3,15}} | collective-permute-start | bytes 1572872 | tf_op jit(solution)/shard_map/ppermute | solution.py:235
  37.5 0.3 pick.1.f_ref
  37.8 0.1 collective-permute-start.3
  37.9 0.2 fetch.1
  38.1 10.3 %collective-permute-done.6.refs_0_ = bf16[256,1024]{1,0:T(8,128)(2,1)S(1)} collective-permute-done((bf16[256,1024]{1,0:T(8,128)(2,1)S(1)}, bf16[256,1024]{1,0:T(8,128)(2,1)S(1)}, u32[]{:S(2)}, u32[]{:S(2)}) %collective-permute-start.6) | collective-permute-done | bytes 524320 | tf_op jit(solution)/shard_map/ppermute | solution.py:233
  48.5 1.8 %collective-permute-done.8.refs_1_ = bf16[256,1024]{1,0:T(8,128)(2,1)S(1)} collective-permute-done((bf16[256,1024]{1,0:T(8,128)(2,1)S(1)}, bf16[256,1024]{1,0:T(8,128)(2,1)S(1)}, u32[]{:S(2)}, u32[]{:S(2)}) %collective-permute-start.8) | collective-permute-done | bytes 524320 | tf_op jit(solution)/shard_map/ppermute | solution.py:235
  50.3 0.0 copy-start.2
  50.3 2.2 %stage1.1 = (bf16[512,512]{1,0:T(8,128)(2,1)S(1)}, bf16[512,512]{1,0:T(8,128)(2,1)S(1)}) custom-call(s32[7,32]{1,0:T(8,128)S(1)} %get-tuple-element.11.cols_ref, bf16[4,7,128,128]{3,2,1,0:T(8,128)(2,1)S(1)} %get-tuple-element.12.f_ref, bf16[256,1024]{1,0:T(8,128)(2,1)S(1)} %get-tuple-element.18.top_hbm, bf16[256,1024]{1,0:T(8,128)(2,1)S(1)} %get-tuple-element.17.bottom_hbm, ...), custom_call_target="tpu_custom_call" | custom-call | tf_op jit(solution)/shard_map/stage1/pallas_call | solution.py:244
  52.5 5.0 %collective-permute-start.10 = (bf16[512,512]{1,0:T(8,128)(2,1)S(1)}, bf16[512,512]{1,0:T(8,128)(2,1)S(1)}, u32[]{:S(2)}, u32[]{:S(2)}) collective-permute-start(bf16[512,512]{1,0:T(8,128)(2,1)S(1)} %get-tuple-element.14.refs_2_), channel_id=1, source_target_pairs={{1,2},{2,1},{5,6},{6,5},{9,10},{10,9},{13,14},{14,13},{17,18},{18,... | collective-permute-start | bytes 1572872 | tf_op jit(solution)/shard_map/ppermute | solution.py:259
  57.5 2.7 %collective-permute-start.9 = (bf16[512,512]{1,0:T(8,128)(2,1)S(1)}, bf16[512,512]{1,0:T(8,128)(2,1)S(1)}, u32[]{:S(2)}, u32[]{:S(2)}) collective-permute-start(bf16[512,512]{1,0:T(8,128)(2,1)S(1)} %get-tuple-element.13.refs_1_), channel_id=1, source_target_pairs={{0,1},{2,3},{1,0},{3,2},{4,5},{6,7},{5,4},{7,6},{8,9},{10,11},{9,8... | collective-permute-start | bytes 1572872 | tf_op jit(solution)/shard_map/ppermute | solution.py:258
  60.2 8.1 %collective-permute-done.10.refs_3_ = bf16[512,512]{1,0:T(8,128)(2,1)S(1)} collective-permute-done((bf16[512,512]{1,0:T(8,128)(2,1)S(1)}, bf16[512,512]{1,0:T(8,128)(2,1)S(1)}, u32[]{:S(2)}, u32[]{:S(2)}) %collective-permute-start.10) | collective-permute-done | bytes 524320 | tf_op jit(solution)/shard_map/ppermute | solution.py:259
  68.3 1.5 %collective-permute-done.9.refs_0_ = bf16[512,512]{1,0:T(8,128)(2,1)S(1)} collective-permute-done((bf16[512,512]{1,0:T(8,128)(2,1)S(1)}, bf16[512,512]{1,0:T(8,128)(2,1)S(1)}, u32[]{:S(2)}, u32[]{:S(2)}) %collective-permute-start.9) | collective-permute-done | bytes 524320 | tf_op jit(solution)/shard_map/ppermute | solution.py:258
  69.9 3.0 %stage2.1 = (f32[512,1024]{1,0:T(8,128)}, bf16[512,2048]{1,0:T(8,128)(2,1)S(1)}) custom-call(s32[7,32]{1,0:T(8,128)S(1)} %get-tuple-element.11.cols_ref, s32[4,8]{1,0:T(4,128)S(1)} %copy-done.2, f32[4,128]{1,0:T(4,128)S(1)} %bitcast.2, bf16[512,1024]{1,0:T(8,128)(2,1)S(1)} %copy-done, bf16[4,7,128,128]{3,2,1,0:T(8,128)(2,1)S(1)} %pick.1.f_ref, ...), custom_call_target="tpu_custom_call" | custom-call | tf_op jit(solution)/shard_map/stage2/pallas_call | solution.py:283
  72.9 2.6 %stage3.1 = f32[512,1024]{1,0:T(8,128)} custom-call(s32[7,32]{1,0:T(8,128)S(1)} %get-tuple-element.11.cols_ref, s32[4,8]{1,0:T(4,128)S(1)} %copy-done.2, f32[4,128]{1,0:T(4,128)S(1)} %bitcast.3, bf16[512,1024]{1,0:T(8,128)(2,1)S(1)} %copy-done, bf16[4,7,128,128]{3,2,1,0:T(8,128)(2,1)S(1)} %collective-permute-done.3.f_ref, ...), custom_call_target="tpu_custom_call", output_to_operand_aliasing={{}: (6, {})} | custom-call | tf_op jit(solution)/shard_map/stage3/pallas_call | solution.py:295
  (16 shorter events, 0.0 us)
Async XLA Ops:
  0.0 37.5 %copy-start.1 = (bf16[4,7,128,128]{3,2,1,0:T(8,128)(2,1)S(1)}, bf16[4,7,128,128]{3,2,1,0:T(8,128)(2,1)}, u32[]{:S(2)}) copy-start(bf16[4,7,128,128]{3,2,1,0:T(8,128)(2,1)} %refs_0_.1) | copy-start | bytes 2752516
  0.0 27.5 %copy-start.5 = (bf16[512,1024]{1,0:T(8,128)(2,1)S(1)}, bf16[512,1024]{1,0:T(8,128)(2,1)}, u32[]{:S(2)}) copy-start(bf16[512,1024]{1,0:T(8,128)(2,1)} %param.6) | copy-start | bytes 3145732
  0.0 24.2 %collective-permute-start = (bf16[4,7,128,128]{3,2,1,0:T(8,128)(2,1)}, bf16[4,7,128,128]{3,2,1,0:T(8,128)(2,1)S(1)}, u32[]{:S(2)}, u32[]{:S(2)}) collective-permute-start(bf16[4,7,128,128]{3,2,1,0:T(8,128)(2,1)} %refs_0_.1), channel_id=1, source_target_pairs={{0,8},{4,20},{9,1},{13,29},{18,26},{22,6},{27,19},{31,15}} | collective-permute-start | bytes 2752520 | tf_op jit(solution)/shard_map/ppermute | solution.py:241
  3.6 32.6 %collective-permute-start.2 = (bf16[4,7,128,128]{3,2,1,0:T(8,128)(2,1)}, bf16[4,7,128,128]{3,2,1,0:T(8,128)(2,1)S(1)}, u32[]{:S(2)}, u32[]{:S(2)}) collective-permute-start(bf16[4,7,128,128]{3,2,1,0:T(8,128)(2,1)} %refs_0_.1), channel_id=1, source_target_pairs={{0,16},{4,12},{9,25},{13,5},{18,2},{22,30},{27,11},{31,23}} | collective-permute-start | bytes 2752520 | tf_op jit(solution)/shard_map/ppermute | solution.py:241
  24.2 13.3 %collective-permute-start.1 = (bf16[4,7,128,128]{3,2,1,0:T(8,128)(2,1)S(1)}, bf16[4,7,128,128]{3,2,1,0:T(8,128)(2,1)S(1)}, u32[]{:S(2)}, u32[]{:S(2)}) collective-permute-start(bf16[4,7,128,128]{3,2,1,0:T(8,128)(2,1)S(1)} %collective-permute-done.refs_1_), channel_id=1, source_target_pairs={{8,24},{20,28},{1,17},{29,21},{26,10},{6,14},{19,3},{15,7}} | collective-permute-start | bytes 2752520 | tf_op jit(solution)/shard_map/ppermute | solution.py:241
  26.1 8.0 %collective-permute-start.7 = (bf16[256,1024]{1,0:T(8,128)(2,1)S(1)}, bf16[256,1024]{1,0:T(8,128)(2,1)S(1)}, u32[]{:S(2)}, u32[]{:S(2)}) collective-permute-start(bf16[256,1024]{1,0:T(8,128)(2,1)S(1)} %get-tuple-element.17.bottom_hbm), channel_id=1, source_target_pairs={{12,28},{16,0},{13,29},{17,1},{14,30},{18,2},{15,31},{19,3}} | collective-permute-start | bytes 1572872 | tf_op jit(solution)/shard_map/ppermute | solution.py:234
  27.5 22.8 %collective-permute-start.4 = (bf16[512,1024]{1,0:T(8,128)(2,1)S(1)}, bf16[512,1024]{1,0:T(8,128)(2,1)S(1)}, u32[]{:S(2)}, u32[]{:S(2)}) collective-permute-start(bf16[512,1024]{1,0:T(8,128)(2,1)S(1)} %copy-done.5), channel_id=1, source_target_pairs={{0,4},{8,12},{16,20},{24,28},{4,0},{12,8},{20,16},{28,24},{1,5},{9... | collective-permute-start | bytes 3145736 | tf_op jit(solution)/shard_map/ppermute | solution.py:237
  27.6 22.7 %collective-permute-start.5 = (bf16[512,1024]{1,0:T(8,128)(2,1)S(1)}, bf16[512,1024]{1,0:T(8,128)(2,1)S(1)}, u32[]{:S(2)}, u32[]{:S(2)}) collective-permute-start(bf16[512,1024]{1,0:T(8,128)(2,1)S(1)} %copy-done.5), channel_id=1, source_target_pairs={{4,8},{20,24},{8,4},{24,20},{5,9},{21,25},{9,5},{25,21},{6,10},{22... | collective-permute-start | bytes 3145736 | tf_op jit(solution)/shard_map/ppermute | solution.py:238
  34.1 3.7 %copy-start.4 = (s32[32,7]{0,1:T(8,128)S(1)}, s32[32,7]{0,1:T(8,128)}, u32[]{:S(2)}) copy-start(s32[32,7]{0,1:T(8,128)} %param.8) | copy-start | bytes 2692
  34.1 14.3 %collective-permute-start.6 = (bf16[256,1024]{1,0:T(8,128)(2,1)S(1)}, bf16[256,1024]{1,0:T(8,128)(2,1)S(1)}, u32[]{:S(2)}, u32[]{:S(2)}) collective-permute-start(bf16[256,1024]{1,0:T(8,128)(2,1)S(1)} %get-tuple-element.18.top_hbm), channel_id=1, source_target_pairs={{12,16},{16,12},{13,17},{17,13},{14,18},{18,14},{15,19},{19,15}} | collective-permute-start | bytes 1572872 | tf_op jit(solution)/shard_map/ppermute | solution.py:233
  36.2 14.1 %collective-permute-start.8 = (bf16[256,1024]{1,0:T(8,128)(2,1)S(1)}, bf16[256,1024]{1,0:T(8,128)(2,1)S(1)}, u32[]{:S(2)}, u32[]{:S(2)}) collective-permute-start(bf16[256,1024]{1,0:T(8,128)(2,1)S(1)} %collective-permute-done.7), channel_id=1, source_target_pairs={{28,16},{0,12},{29,17},{1,13},{30,18},{2,14},{31,19},{3,15}} | collective-permute-start | bytes 1572872 | tf_op jit(solution)/shard_map/ppermute | solution.py:235
  37.8 35.1 %collective-permute-start.3 = (bf16[4,7,128,128]{3,2,1,0:T(8,128)(2,1)S(1)}, bf16[4,7,128,128]{3,2,1,0:T(8,128)(2,1)S(1)}, u32[]{:S(2)}, u32[]{:S(2)}) collective-permute-start(bf16[4,7,128,128]{3,2,1,0:T(8,128)(2,1)S(1)} %pick.1.f_ref), channel_id=1, source_target_pairs={{4,0},{0,4},{12,8},{8,12},{20,16},{16,20},{28,24},{24,28},{5,1},{1... | collective-permute-start | bytes 2752520 | tf_op jit(solution)/shard_map/ppermute | solution.py:294
  50.2 19.6 %copy-start = (bf16[512,1024]{1,0:T(8,128)(2,1)S(1)}, bf16[512,1024]{1,0:T(8,128)(2,1)}, u32[]{:S(2)}) copy-start(bf16[512,1024]{1,0:T(8,128)(2,1)} %w_ref.3) | copy-start | bytes 3145732
  50.3 19.6 %copy-start.2 = (s32[4,8]{1,0:T(4,128)S(1)}, s32[4,8]{1,0:T(4,128)}, u32[]{:S(2)}) copy-start(s32[4,8]{1,0:T(4,128)} %mask_ref.3) | copy-start | bytes 388
  50.3 19.6 %copy-start.3 = (f32[512]{0:T(512)S(1)}, f32[512]{0:T(512)}, u32[]{:S(2)}) copy-start(f32[512]{0:T(512)} %param.11) | copy-start | bytes 6148
  52.5 15.9 %collective-permute-start.10 = (bf16[512,512]{1,0:T(8,128)(2,1)S(1)}, bf16[512,512]{1,0:T(8,128)(2,1)S(1)}, u32[]{:S(2)}, u32[]{:S(2)}) collective-permute-start(bf16[512,512]{1,0:T(8,128)(2,1)S(1)} %get-tuple-element.14.refs_2_), channel_id=1, source_target_pairs={{1,2},{2,1},{5,6},{6,5},{9,10},{10,9},{13,14},{14,13},{17,18},{18,... | collective-permute-start | bytes 1572872 | tf_op jit(solution)/shard_map/ppermute | solution.py:259
  57.5 12.4 %collective-permute-start.9 = (bf16[512,512]{1,0:T(8,128)(2,1)S(1)}, bf16[512,512]{1,0:T(8,128)(2,1)S(1)}, u32[]{:S(2)}, u32[]{:S(2)}) collective-permute-start(bf16[512,512]{1,0:T(8,128)(2,1)S(1)} %get-tuple-element.13.refs_1_), channel_id=1, source_target_pairs={{0,1},{2,3},{1,0},{3,2},{4,5},{6,7},{5,4},{7,6},{8,9},{10,11},{9,8... | collective-permute-start | bytes 1572872 | tf_op jit(solution)/shard_map/ppermute | solution.py:258

commit v9 on v8

--- a/solution.py
+++ b/solution.py
@@ -33,45 +33,57 @@
     def at(a, k, c):
         return (a * fan + k) * cols + c
 
-    if (cols, fan) != (4, 2):
+    if not relayed(rows, cols):
         pairs = []
         for c in range(cols):
             for a in range(cols):
                 if a != c:
                     plane = source_plane(c, a, cols)
                     pairs += [(at(c, k, plane), at(a, k, c)) for k in range(fan)]
-        return [(0, pairs)]
-    first, relayed, second = [], [], []
+        return [pairs]
+    first, second = [], []
     for c in range(cols):
         near, side, far = c ^ 1, c ^ 2, c ^ 3
         first += [(at(c, 0, c), at(near, 0, c)), (at(c, 1, c), at(side, 1, c))]
-        relayed += [(at(near, 0, c), at(far, 0, c)), (at(side, 1, c), at(far, 1, c))]
-        second += [(at(c, 0, c), at(side, 0, c)), (at(c, 1, c), at(near, 1, c))]
-    return [(0, first), (1, relayed), (0, second)]
-
-
-def holder_table(rows, cols):
-    table = [0] * (rows * cols)
-    for step, (_, pairs) in enumerate(group_plan(rows, cols)):
-        for _, target in pairs:
-            table[target] = step + 1
-    return table
-
-
-def pick_kernel(table, *refs):
-    *sources, out_ref, sem = refs
-    me = lax.axis_index("row") * lax.axis_size("col") + lax.axis_index("col")
-    which = 0
-    for device, step in enumerate(table):
-        if step:
-            which = jnp.where(me == device, step, which)
-    for step, source in enumerate(sources):
-
-        @pl.when(which == step)
+        second += [
+            (at(near, 0, c), at(far, 0, c)),
+            (at(side, 1, c), at(far, 1, c)),
+            (at(c, 0, c), at(side, 0, c)),
+            (at(c, 1, c), at(near, 1, c)),
+        ]
+    return [first, second]
+
+
+def relayed(rows, cols):
+    return (rows, cols) == (8, 4)
+
+
+def held_early(row, col, rows, cols):
+    fan = rows // cols
+    if isinstance(row, int):
+        chip, core = divmod(row, fan)
+    else:
+        chip, core = lax.div(row, fan), lax.rem(row, fan)
+    if not relayed(rows, cols):
+        return chip == col
+    way = chip ^ col
+    return (way == 0) | ((way == 1) & (core == 0)) | ((way == 2) & (core == 1))
+
+
+def pick_kernel(fan, own_hbm, got_hbm, out_ref, sem):
+    own = lax.div(lax.axis_index("row"), fan) == lax.axis_index("col")
+    for source, wanted in ((own_hbm, own), (got_hbm, jnp.logical_not(own))):
+
+        @pl.when(wanted)
         def _():
-            copy = pltpu.make_async_copy(source, out_ref, sem)
-            copy.start()
-            copy.wait()
+            copies = [
+                pltpu.make_async_copy(source.at[n], out_ref.at[n], sem.at[n])
+                for n in range(out_ref.shape[0])
+            ]
+            for copy in copies:
+                copy.start()
+            for copy in copies:
+                copy.wait()
 
 
 def fetch_kernel(f_hbm, cols_hbm, f_ref, cols_ref, sem):
@@ -142,18 +154,39 @@
                 ).astype(out_ref.dtype)
 
 
-def stage2_kernel(fan, turn, cols_ref, mask_ref, q_ref, w_ref, f_ref, *refs):
+def stage2_kernel(
+    sizes, turn, cols_ref, mask_ref, q_ref, w_ref, early_ref, late_ref, *refs
+):
+    fan = sizes[0] // sizes[1]
+    ready = []
     if turn == 0:
-        *parts, out_hbm, ext, made, out_sem, sem = refs
+        *parts, made, ext, sem = refs
     else:
-        ext, _, out_hbm, made, out_sem = refs
+        ext, *ready = refs[:-4] if turn == fan - 1 else refs[:-1]
         parts = []
-    group, bs = f_ref.shape[0], f_ref.shape[2]
+        if turn == fan - 1:
+            out_hbm, made, out_sem, ready_sem = refs[-4:]
+        else:
+            made = refs[-1]
+    group, bs = early_ref.shape[0], early_ref.shape[2]
     rows, slab = mask_ref.shape
     row_idx, col_idx = lax.axis_index("row"), lax.axis_index("col")
-    base = lax.rem(row_idx + turn, fan) * group
     first = col_idx * slab - BAND
-
+    core = lax.rem(row_idx, fan)
+    owner = row_idx - core + lax.rem(core + turn, fan)
+    early = held_early(owner, col_idx, *sizes)
+
+    def column(turn, n):
+        return lax.rem(row_idx + turn, fan) * group + n
+
+    def place(j):
+        return pl.ds(pl.multiple_of(j * bs, bs), bs)
+
+    stores = []
+    for before, done in enumerate(ready):
+        for n in range(group):
+            to = out_hbm.at[:, place(column(before, n))]
+            stores.append(pltpu.make_async_copy(done.at[n], to, ready_sem.at[before, n]))
     joins = []
     odd = lax.rem(col_idx, 2)
     for piece, part in enumerate(parts):
@@ -161,7 +194,7 @@
         at = odd * piece + (1 - odd) * (len(parts) - 1 - piece)
         to = ext.at[:, pl.ds(pl.multiple_of(at * width, width), width)]
         joins.append(pltpu.make_async_copy(part, to, sem.at[piece]))
-    for copy in joins:
+    for copy in joins + stores:
         copy.start()
     for copy in joins:
         copy.wait()
@@ -169,11 +202,10 @@
     eye = lax.broadcasted_iota(jnp.int32, (bs, bs), 0) == lax.broadcasted_iota(
         jnp.int32, (bs, bs), 1
     )
-    stores = []
     for n in range(group):
-        j = base + n
+        j = column(turn, n)
         col = col_idx * slab + j
-        to = pl.ds(pl.multiple_of(j * bs, bs), bs)
+        to = place(j)
         lhs = jnp.concatenate(
             [
                 ext[:, pl.ds(pl.multiple_of((cols_ref[e, col] - first) * bs, bs), bs)]
@@ -181,7 +213,9 @@
             ],
             axis=1,
         )
-        rhs = jnp.concatenate([f_ref[n, e] for e in range(STENCIL)], axis=1)
+        rhs = jnp.concatenate(
+            [jnp.where(early, early_ref[n, e], late_ref[n, e]) for e in range(STENCIL)], axis=1
+        )
         spread = lax.dot_general(
             lhs, rhs, (((1,), (1,)), ((), ())), preferred_element_type=jnp.float32
         )
@@ -191,9 +225,10 @@
             on_main = (row_idx * rows + i == col).astype(jnp.float32)
             noise = jnp.where(eye, q_ref[i : i + 1, :] * on_main, 0.0)
             made[n, at, :] = w_ref[at, to].astype(jnp.float32) * (spread[at] * keep) + noise
-        store = pltpu.make_async_copy(made.at[n], out_hbm.at[:, to], out_sem.at[n])
-        store.start()
-        stores.append(store)
+        if turn == fan - 1:
+            store = pltpu.make_async_copy(made.at[n], out_hbm.at[:, to], out_sem.at[n])
+            store.start()
+            stores.append(store)
     for store in stores:
         store.wait()
 
@@ -236,10 +271,19 @@
         halves = (straight, turned)
     inner = lax.ppermute(p_cov, "row", inner_pairs)
     outer = lax.ppermute(p_cov, "row", outer_pairs)
-    held = [f_blocks]
-    for source, pairs in group_plan(rows, cols):
-        held.append(lax.ppermute(held[source], ("row", "col"), pairs))
-
+    plan = group_plan(rows, cols)
+    early, late = f_blocks, lax.ppermute(f_blocks, ("row", "col"), plan[0])
+    if len(plan) > 1:
+        early = pl.pallas_call(
+            functools.partial(pick_kernel, fan),
+            out_shape=jax.ShapeDtypeStruct(f_blocks.shape, f_blocks.dtype),
+            in_specs=[hbm, hbm],
+            out_specs=vmem,
+            scratch_shapes=[pltpu.SemaphoreType.DMA((block_rows,))],
+            compiler_params=pltpu.CompilerParams(vmem_limit_bytes=4 * 2**20),
+            name="pick",
+        )(f_blocks, late)
+        late = lax.ppermute(early, ("row", "col"), plan[1])
     half = jax.ShapeDtypeStruct((tall, halo), jnp.bfloat16)
     first, second = pl.pallas_call(
         functools.partial(stage1_kernel, bent),
@@ -258,51 +302,53 @@
     nearer = lax.ppermute(first, "col", inner_pairs)
     further = lax.ppermute(second, "col", outer_pairs)
 
-    mine = pl.pallas_call(
-        functools.partial(pick_kernel, holder_table(rows, cols)),
-        out_shape=jax.ShapeDtypeStruct(f_blocks.shape, f_blocks.dtype),
-        in_specs=[hbm] * len(held),
-        out_specs=vmem,
-        scratch_shapes=[pltpu.SemaphoreType.DMA],
-        compiler_params=pltpu.CompilerParams(vmem_limit_bytes=4 * 2**20),
-        name="pick",
-    )(*held)
     fixed = (
         cols_of,
         block_mask,
         disturbance_variances.reshape(block_rows, bs),
         localization_weights,
     )
-    out_type = jax.ShapeDtypeStruct((tall, wide), jnp.float32)
+    assert fan > 1
     group = slab // fan
-    scratch = [
-        pltpu.VMEM((group, tall, bs), jnp.float32),
-        pltpu.SemaphoreType.DMA((group,)),
-    ]
+    made_type = jax.ShapeDtypeStruct((group, tall, bs), jnp.float32)
     params = pltpu.CompilerParams(vmem_limit_bytes=20 * 2**20)
-    out, ext = pl.pallas_call(
-        functools.partial(stage2_kernel, fan, 0),
-        out_shape=(out_type, jax.ShapeDtypeStruct((tall, wide + 2 * halo), jnp.bfloat16)),
-        in_specs=[smem, smem, vmem, vmem, vmem] + [hbm] * 4,
-        out_specs=(pl.BlockSpec(memory_space=pltpu.HBM), vmem),
-        scratch_shapes=scratch + [pltpu.SemaphoreType.DMA((4,))],
+    made, ext = pl.pallas_call(
+        functools.partial(stage2_kernel, (rows, cols), 0),
+        out_shape=(made_type, jax.ShapeDtypeStruct((tall, wide + 2 * halo), jnp.bfloat16)),
+        in_specs=[smem, smem] + [vmem] * 4 + [hbm] * 4,
+        out_specs=(vmem, vmem),
+        scratch_shapes=[pltpu.SemaphoreType.DMA((4,))],
         compiler_params=params,
         name="stage2",
-    )(*fixed, mine, nearer, first, second, further)
+    )(*fixed, early, late, nearer, first, second, further)
+    ready = [made]
     for turn in range(1, fan):
-        pairs = [(r // fan * fan + (r + turn) % fan, r) for r in range(rows)]
-        other = lax.ppermute(mine, "row", pairs)
-        out = pl.pallas_call(
-            functools.partial(stage2_kernel, fan, turn),
-            out_shape=out_type,
-            in_specs=[smem, smem, vmem, vmem, vmem, vmem, pl.BlockSpec(memory_space=pltpu.HBM)],
-            out_specs=pl.BlockSpec(memory_space=pltpu.HBM),
-            scratch_shapes=scratch,
-            input_output_aliases={6: 0},
-            compiler_params=params,
-            name="stage3",
-        )(*fixed, other, ext, out)
-    return out
+        last = turn == fan - 1
+        pairs = {True: [], False: []}
+        for r in range(rows):
+            source = r // fan * fan + (r + turn) % fan
+            for c in range(cols):
+                pair = (source * cols + c, r * cols + c)
+                pairs[held_early(source, c, rows, cols)].append(pair)
+        sent_early = lax.ppermute(early, ("row", "col"), pairs[True])
+        sent_late = lax.ppermute(late, ("row", "col"), pairs[False])
+        ready.append(
+            pl.pallas_call(
+                functools.partial(stage2_kernel, (rows, cols), turn),
+                out_shape=jax.ShapeDtypeStruct((tall, wide), jnp.float32) if last else made_type,
+                in_specs=[smem, smem] + [vmem] * (5 + len(ready) * last),
+                out_specs=pl.BlockSpec(memory_space=pltpu.HBM) if last else vmem,
+                scratch_shapes=[
+                    pltpu.VMEM(made_type.shape, made_type.dtype),
+                    pltpu.SemaphoreType.DMA((group,)),
+                    pltpu.SemaphoreType.DMA((turn, group)),
+                ]
+                * last,
+                compiler_params=params,
+                name="stage3",
+            )(*fixed, sent_early, sent_late, ext, *(ready * last))
+        )
+    return ready[-1]
 
 
 def solution(mesh):

time: 75.8 us -> 72.9 us (0.962)
  the two profiles are of different devices: /device:TPU:20 before, /device:TPU:29 now
where the time goes in v9:
time: 72.9 us; the launch traced here: 72.6 us
  starting transfers between devices  44.2 us (61%)
  waiting for transfers between devices  18.1 us (25%)
  Pallas kernels  8.78 us (12%)
  local copies, waits for them, and re-layouts  1.27 us (2%)
    ppermute x1, starting transfers between devices, forecast(): sent_late = lax.ppermute(late, ('row', 'col'), pairs[False])  20 us
    ppermute x1, starting transfers between devices, forecast(): inner = lax.ppermute(p_cov, 'row', inner_pairs)  16.2 us
    ppermute x1, waiting for transfers between devices, forecast(): nearer = lax.ppermute(first, 'col', inner_pairs)  13.5 us
    ppermute x1, waiting for transfers between devices, forecast(): late = lax.ppermute(early, ('row', 'col'), plan[1])  4.55 us
    pallas_call x1, Pallas kernels, forecast(): pl.pallas_call(functools.partial(stage2_kernel, (rows, cols), turn), out_...  2.78 us
    pallas_call x1, Pallas kernels, forecast(): pl.pallas_call(functools.partial(stage2_kernel, (rows, cols), 0), out_sha...  2.34 us
    pallas_call x1, Pallas kernels, forecast(): pl.pallas_call(functools.partial(stage1_kernel, bent), out_shape=(half, h...  2.2 us
    ppermute x1, starting transfers between devices, forecast(): outer = lax.ppermute(p_cov, 'row', outer_pairs)  1.91 us
  transfers between devices with their start and end apart: 11, of which 2 were waited for; matrix products, arithmetic and copies ran while one was open for 0% of the time, Pallas kernels for 7%

profile of v9, /device:TPU:29, one launch (start us, length us, event | category | flops | bytes accessed | tf_op | source)
XLA Modules:
  0.0 72.6 jit_solution(16206955911048016584)
XLA Ops:
  0.0 0.7 collective-permute-start
  0.7 0.0 collective-permute-done.got_hbm
  0.7 1.2 %copy-done.1 = bf16[4,7,128,128]{3,2,1,0:T(8,128)(2,1)S(1)} copy-done((bf16[4,7,128,128]{3,2,1,0:T(8,128)(2,1)S(1)}, bf16[4,7,128,128]{3,2,1,0:T(8,128)(2,1)}, u32[]{:S(2)}) %copy-start.1) | copy-done | bytes 917528
  1.9 1.2 %pick.1.early_ref = bf16[4,7,128,128]{3,2,1,0:T(8,128)(2,1)S(1)} custom-call(bf16[4,7,128,128]{3,2,1,0:T(8,128)(2,1)S(1)} %copy-done.1, bf16[4,7,128,128]{3,2,1,0:T(8,128)(2,1)S(1)} %collective-permute-done.got_hbm), custom_call_target="tpu_custom_call" | custom-call | tf_op jit(solution)/shard_map/pick/pallas_call | solution.py:277
  3.1 1.3 %collective-permute-start.2 = (bf16[4,7,128,128]{3,2,1,0:T(8,128)(2,1)S(1)}, bf16[4,7,128,128]{3,2,1,0:T(8,128)(2,1)S(1)}, u32[]{:S(2)}, u32[]{:S(2)}) collective-permute-start(bf16[4,7,128,128]{3,2,1,0:T(8,128)(2,1)S(1)} %pick.1.early_ref), channel_id=1, source_target_pairs={{8,24},{20,28},{0,16},{4,12},{1,17},{29,21},{9,25},{13,5},{26,10},... | collective-permute-start | bytes 2752520 | tf_op jit(solution)/shard_map/ppermute | solution.py:286
  4.4 0.1 fusion
  4.5 0.7 collective-permute-start.7
  5.2 16.2 %collective-permute-start.4 = (bf16[512,1024]{1,0:T(8,128)(2,1)S(1)}, bf16[512,1024]{1,0:T(8,128)(2,1)S(1)}, u32[]{:S(2)}, u32[]{:S(2)}) collective-permute-start(bf16[512,1024]{1,0:T(8,128)(2,1)S(1)} %copy-done.6), channel_id=1, source_target_pairs={{0,4},{8,12},{16,20},{24,28},{4,0},{12,8},{20,16},{28,24},{1,5},{9... | collective-permute-start | bytes 3145736 | tf_op jit(solution)/shard_map/ppermute | solution.py:272
  21.4 1.9 %collective-permute-start.5 = (bf16[512,1024]{1,0:T(8,128)(2,1)S(1)}, bf16[512,1024]{1,0:T(8,128)(2,1)S(1)}, u32[]{:S(2)}, u32[]{:S(2)}) collective-permute-start(bf16[512,1024]{1,0:T(8,128)(2,1)S(1)} %copy-done.6), channel_id=1, source_target_pairs={{4,8},{20,24},{8,4},{24,20},{5,9},{21,25},{9,5},{25,21},{6,10},{22... | collective-permute-start | bytes 3145736 | tf_op jit(solution)/shard_map/ppermute | solution.py:273
  23.3 0.7 collective-permute-start.6
  24.0 0.7 collective-permute-start.8
  24.8 1.3 %collective-permute-start.1 = (bf16[4,7,128,128]{3,2,1,0:T(8,128)(2,1)S(1)}, bf16[4,7,128,128]{3,2,1,0:T(8,128)(2,1)S(1)}, u32[]{:S(2)}, u32[]{:S(2)}) collective-permute-start(bf16[4,7,128,128]{3,2,1,0:T(8,128)(2,1)S(1)} %pick.1.early_ref), channel_id=1, source_target_pairs={{4,0},{6,2},{0,4},{1,5},{13,9},{15,11},{8,12},{9,13},{20,16},{22,1... | collective-permute-start | bytes 2752520 | tf_op jit(solution)/shard_map/ppermute | solution.py:333
  26.1 4.6 %collective-permute-done.2.late_ref = bf16[4,7,128,128]{3,2,1,0:T(8,128)(2,1)S(1)} collective-permute-done((bf16[4,7,128,128]{3,2,1,0:T(8,128)(2,1)S(1)}, bf16[4,7,128,128]{3,2,1,0:T(8,128)(2,1)S(1)}, u32[]{:S(2)}, u32[]{:S(2)}) %collective-permute-start.2) | collective-permute-done | bytes 917536 | tf_op jit(solution)/shard_map/ppermute | solution.py:286
  30.6 20.0 %collective-permute-start.3 = (bf16[4,7,128,128]{3,2,1,0:T(8,128)(2,1)S(1)}, bf16[4,7,128,128]{3,2,1,0:T(8,128)(2,1)S(1)}, u32[]{:S(2)}, u32[]{:S(2)}) collective-permute-start(bf16[4,7,128,128]{3,2,1,0:T(8,128)(2,1)S(1)} %collective-permute-done.2.late_ref), channel_id=1, source_target_pairs={{5,1},{7,3},{2,6},{3,7},{12,8},{14,10},{10,14},{11,15},{21,17},{23... | collective-permute-start | bytes 2752520 | tf_op jit(solution)/shard_map/ppermute | solution.py:334
  50.6 0.2 fetch.1
  50.9 0.0 copy-start
  50.9 0.0 copy-start.3
  50.9 0.0 copy-start.4
  50.9 2.2 %stage1.1 = (bf16[512,512]{1,0:T(8,128)(2,1)S(1)}, bf16[512,512]{1,0:T(8,128)(2,1)S(1)}) custom-call(s32[7,32]{1,0:T(8,128)S(1)} %get-tuple-element.11.cols_ref, bf16[4,7,128,128]{3,2,1,0:T(8,128)(2,1)S(1)} %get-tuple-element.12.f_ref, bf16[256,1024]{1,0:T(8,128)(2,1)S(1)} %get-tuple-element.18.top_hbm, bf16[256,1024]{1,0:T(8,128)(2,1)S(1)} %get-tuple-element.17.bottom_hbm, ...), custom_call_target="tpu_custom_call" | custom-call | tf_op jit(solution)/shard_map/stage1/pallas_call | solution.py:288
  53.2 0.7 collective-permute-start.10
  53.9 0.1 collective-permute-start.9
  53.9 13.5 %collective-permute-done.9.refs_0_ = bf16[512,512]{1,0:T(8,128)(2,1)S(1)} collective-permute-done((bf16[512,512]{1,0:T(8,128)(2,1)S(1)}, bf16[512,512]{1,0:T(8,128)(2,1)S(1)}, u32[]{:S(2)}, u32[]{:S(2)}) %collective-permute-start.9) | collective-permute-done | bytes 524320 | tf_op jit(solution)/shard_map/ppermute | solution.py:302
  67.5 2.3 %stage2.1 = (f32[4,512,128]{2,1,0:T(8,128)S(1)}, bf16[512,2048]{1,0:T(8,128)(2,1)S(1)}) custom-call(s32[7,32]{1,0:T(8,128)S(1)} %get-tuple-element.11.cols_ref, s32[4,8]{1,0:T(4,128)S(1)} %copy-done.3, f32[4,128]{1,0:T(4,128)S(1)} %bitcast.2, bf16[512,1024]{1,0:T(8,128)(2,1)S(1)} %copy-done, bf16[4,7,128,128]{3,2,1,0:T(8,128)(2,1)S(1)} %pick.1.early_ref, ...), custom_call_target="tpu_custom_call" | custom-call | tf_op jit(solution)/shard_map/stage2/pallas_call | solution.py:315
  69.8 2.8 %stage3.1 = f32[512,1024]{1,0:T(8,128)} custom-call(s32[7,32]{1,0:T(8,128)S(1)} %get-tuple-element.11.cols_ref, s32[4,8]{1,0:T(4,128)S(1)} %copy-done.3, f32[4,128]{1,0:T(4,128)S(1)} %bitcast.3, bf16[512,1024]{1,0:T(8,128)(2,1)S(1)} %copy-done, bf16[4,7,128,128]{3,2,1,0:T(8,128)(2,1)S(1)} %collective-permute-done.1.early_ref, ...), custom_call_target="tpu_custom_call" | custom-call | tf_op jit(solution)/shard_map/stage3/pallas_call | solution.py:336
  (18 shorter events, 0.0 us)
Async XLA Ops:
  0.0 0.7 collective-permute-start
  0.7 1.2 %copy-start.1 = (bf16[4,7,128,128]{3,2,1,0:T(8,128)(2,1)S(1)}, bf16[4,7,128,128]{3,2,1,0:T(8,128)(2,1)}, u32[]{:S(2)}) copy-start(bf16[4,7,128,128]{3,2,1,0:T(8,128)(2,1)} %own_hbm.1) | copy-start | bytes 2752516
  1.9 2.5 %copy-start.6 = (bf16[512,1024]{1,0:T(8,128)(2,1)S(1)}, bf16[512,1024]{1,0:T(8,128)(2,1)}, u32[]{:S(2)}) copy-start(bf16[512,1024]{1,0:T(8,128)(2,1)} %param.6) | copy-start | bytes 3145732
  1.9 48.7 %copy-start.2 = (bf16[4,7,128,128]{3,2,1,0:T(8,128)(2,1)S(1)}, bf16[4,7,128,128]{3,2,1,0:T(8,128)(2,1)}, u32[]{:S(2)}) copy-start(bf16[4,7,128,128]{3,2,1,0:T(8,128)(2,1)} %own_hbm.1) | copy-start | bytes 2752516
  1.9 48.7 %copy-start.5 = (s32[32,7]{0,1:T(8,128)S(1)}, s32[32,7]{0,1:T(8,128)}, u32[]{:S(2)}) copy-start(s32[32,7]{0,1:T(8,128)} %param.8) | copy-start | bytes 2692
  3.1 27.5 %collective-permute-start.2 = (bf16[4,7,128,128]{3,2,1,0:T(8,128)(2,1)S(1)}, bf16[4,7,128,128]{3,2,1,0:T(8,128)(2,1)S(1)}, u32[]{:S(2)}, u32[]{:S(2)}) collective-permute-start(bf16[4,7,128,128]{3,2,1,0:T(8,128)(2,1)S(1)} %pick.1.early_ref), channel_id=1, source_target_pairs={{8,24},{20,28},{0,16},{4,12},{1,17},{29,21},{9,25},{13,5},{26,10},... | collective-permute-start | bytes 2752520 | tf_op jit(solution)/shard_map/ppermute | solution.py:286
  4.5 19.5 %collective-permute-start.7 = (bf16[256,1024]{1,0:T(8,128)(2,1)S(1)}, bf16[256,1024]{1,0:T(8,128)(2,1)S(1)}, u32[]{:S(2)}, u32[]{:S(2)}) collective-permute-start(bf16[256,1024]{1,0:T(8,128)(2,1)S(1)} %get-tuple-element.17.bottom_hbm), channel_id=1, source_target_pairs={{12,28},{16,0},{13,29},{17,1},{14,30},{18,2},{15,31},{19,3}} | collective-permute-start | bytes 1572872 | tf_op jit(solution)/shard_map/ppermute | solution.py:269
  5.2 45.7 %collective-permute-start.4 = (bf16[512,1024]{1,0:T(8,128)(2,1)S(1)}, bf16[512,1024]{1,0:T(8,128)(2,1)S(1)}, u32[]{:S(2)}, u32[]{:S(2)}) collective-permute-start(bf16[512,1024]{1,0:T(8,128)(2,1)S(1)} %copy-done.6), channel_id=1, source_target_pairs={{0,4},{8,12},{16,20},{24,28},{4,0},{12,8},{20,16},{28,24},{1,5},{9... | collective-permute-start | bytes 3145736 | tf_op jit(solution)/shard_map/ppermute | solution.py:272
  21.4 29.5 %collective-permute-start.5 = (bf16[512,1024]{1,0:T(8,128)(2,1)S(1)}, bf16[512,1024]{1,0:T(8,128)(2,1)S(1)}, u32[]{:S(2)}, u32[]{:S(2)}) collective-permute-start(bf16[512,1024]{1,0:T(8,128)(2,1)S(1)} %copy-done.6), channel_id=1, source_target_pairs={{4,8},{20,24},{8,4},{24,20},{5,9},{21,25},{9,5},{25,21},{6,10},{22... | collective-permute-start | bytes 3145736 | tf_op jit(solution)/shard_map/ppermute | solution.py:273
  23.3 1.4 %collective-permute-start.6 = (bf16[256,1024]{1,0:T(8,128)(2,1)S(1)}, bf16[256,1024]{1,0:T(8,128)(2,1)S(1)}, u32[]{:S(2)}, u32[]{:S(2)}) collective-permute-start(bf16[256,1024]{1,0:T(8,128)(2,1)S(1)} %get-tuple-element.18.top_hbm), channel_id=1, source_target_pairs={{12,16},{16,12},{13,17},{17,13},{14,18},{18,14},{15,19},{19,15}} | collective-permute-start | bytes 1572872 | tf_op jit(solution)/shard_map/ppermute | solution.py:268
  24.0 26.8 %collective-permute-start.8 = (bf16[256,1024]{1,0:T(8,128)(2,1)S(1)}, bf16[256,1024]{1,0:T(8,128)(2,1)S(1)}, u32[]{:S(2)}, u32[]{:S(2)}) collective-permute-start(bf16[256,1024]{1,0:T(8,128)(2,1)S(1)} %collective-permute-done.7), channel_id=1, source_target_pairs={{28,16},{0,12},{29,17},{1,13},{30,18},{2,14},{31,19},{3,15}} | collective-permute-start | bytes 1572872 | tf_op jit(solution)/shard_map/ppermute | solution.py:270
  24.8 45.1 %collective-permute-start.1 = (bf16[4,7,128,128]{3,2,1,0:T(8,128)(2,1)S(1)}, bf16[4,7,128,128]{3,2,1,0:T(8,128)(2,1)S(1)}, u32[]{:S(2)}, u32[]{:S(2)}) collective-permute-start(bf16[4,7,128,128]{3,2,1,0:T(8,128)(2,1)S(1)} %pick.1.early_ref), channel_id=1, source_target_pairs={{4,0},{6,2},{0,4},{1,5},{13,9},{15,11},{8,12},{9,13},{20,16},{22,1... | collective-permute-start | bytes 2752520 | tf_op jit(solution)/shard_map/ppermute | solution.py:333
  30.6 39.2 %collective-permute-start.3 = (bf16[4,7,128,128]{3,2,1,0:T(8,128)(2,1)S(1)}, bf16[4,7,128,128]{3,2,1,0:T(8,128)(2,1)S(1)}, u32[]{:S(2)}, u32[]{:S(2)}) collective-permute-start(bf16[4,7,128,128]{3,2,1,0:T(8,128)(2,1)S(1)} %collective-permute-done.2.late_ref), channel_id=1, source_target_pairs={{5,1},{7,3},{2,6},{3,7},{12,8},{14,10},{10,14},{11,15},{21,17},{23... | collective-permute-start | bytes 2752520 | tf_op jit(solution)/shard_map/ppermute | solution.py:334
  50.9 16.6 %copy-start = (bf16[512,1024]{1,0:T(8,128)(2,1)S(1)}, bf16[512,1024]{1,0:T(8,128)(2,1)}, u32[]{:S(2)}) copy-start(bf16[512,1024]{1,0:T(8,128)(2,1)} %w_ref.3) | copy-start | bytes 3145732
  50.9 16.5 %copy-start.3 = (s32[4,8]{1,0:T(4,128)S(1)}, s32[4,8]{1,0:T(4,128)}, u32[]{:S(2)}) copy-start(s32[4,8]{1,0:T(4,128)} %mask_ref.3) | copy-start | bytes 388
  50.9 16.5 %copy-start.4 = (f32[512]{0:T(512)S(1)}, f32[512]{0:T(512)}, u32[]{:S(2)}) copy-start(f32[512]{0:T(512)} %param.11) | copy-start | bytes 6148
  53.2 0.8 %collective-permute-start.10 = (bf16[512,512]{1,0:T(8,128)(2,1)S(1)}, bf16[512,512]{1,0:T(8,128)(2,1)S(1)}, u32[]{:S(2)}, u32[]{:S(2)}) collective-permute-start(bf16[512,512]{1,0:T(8,128)(2,1)S(1)} %get-tuple-element.14.refs_2_), channel_id=1, source_target_pairs={{1,2},{2,1},{5,6},{6,5},{9,10},{10,9},{13,14},{14,13},{17,18},{18,... | collective-permute-start | bytes 1572872 | tf_op jit(solution)/shard_map/ppermute | solution.py:303
  53.9 13.6 %collective-permute-start.9 = (bf16[512,512]{1,0:T(8,128)(2,1)S(1)}, bf16[512,512]{1,0:T(8,128)(2,1)S(1)}, u32[]{:S(2)}, u32[]{:S(2)}) collective-permute-start(bf16[512,512]{1,0:T(8,128)(2,1)S(1)} %get-tuple-element.13.refs_1_), channel_id=1, source_target_pairs={{0,1},{2,3},{1,0},{3,2},{4,5},{6,7},{5,4},{7,6},{8,9},{10,11},{9,8... | collective-permute-start | bytes 1572872 | tf_op jit(solution)/shard_map/ppermute | solution.py:302
